TPU v7x, 256 devices: a whole 4x4x8 slice. The times are simulated.
256 devices in a mesh: order: 8 (over y, core), slab: 32 (over x, z).
Axes of the slice: x: 4, y: 4, z: 8, core: 2. Of those that a mesh axis runs over, the one named last changes fastest.
Arguments:
- previous: float32 [64, 384, 256], P('slab'), may hold values from 1 to 3
- fibre_tensor: float32 [6, 64, 384, 256], P(None, 'slab'), may hold values from -4.6 to 9.6, as said below
- tissue: int32 [64, 384, 256], P('slab'), may hold values 0 or 1
- stim_sites: int32 [16], replicated, may hold values from 0 to 6291455, as said below
- stim_times: float32 [16], replicated, may hold values from 0 to 0.5
Outputs:
- merged: float32 [64, 384, 256], P('slab')
- ordering_fields: float32 [8, 64, 384, 256], P('order', 'slab')
Inputs may be any that keep to these rules, and one draw needn't show every extreme that they name: `fibre_tensor`: each voxel's six entries form a symmetric matrix with eigenvalues between 0.4 and 9.6. `stim_sites`: flat indices of voxels of the grid.
All inputs are finite; a program needn't handle non-finite values. No bound on the sum of `tissue` on one device may be relied on, other than what follows from the above.
Results may differ from a plain program's by a relative error of at most 0.00002.
Values sent between devices are 32-bit elements; how exact they have to be, the bound alone decides.
A program may use at most 128 MiB of HBM per device.

v0:
```python
import jax
import jax.numpy as jnp
from jax import lax
from jax.sharding import PartitionSpec as P

LARGE_TIME = 10000.0


def passed_along(block, axis, distance):
    devices = range(lax.axis_size(axis))
    route = [(i - distance, i) for i in devices if i - distance in devices]
    return lax.ppermute(block, axis, route)


def compose(earlier, later):
    earlier_add, earlier_min = earlier
    later_add, later_min = later
    return (earlier_add + later_add, jnp.minimum(earlier_min + later_add, later_min))


def slowness(fibre_tensor, tissue, grid_step):
    tensor_xx, tensor_yy, tensor_zz = (fibre_tensor[0], fibre_tensor[1], fibre_tensor[2])
    tensor_xy, tensor_xz, tensor_yz = (fibre_tensor[3], fibre_tensor[4], fibre_tensor[5])
    cofactor_x = tensor_yy * tensor_zz - tensor_yz * tensor_yz
    cofactor_y = tensor_xx * tensor_zz - tensor_xz * tensor_xz
    cofactor_z = tensor_xx * tensor_yy - tensor_xy * tensor_xy
    determinant = (
        tensor_xx * cofactor_x
        - tensor_xy * (tensor_xy * tensor_zz - tensor_yz * tensor_xz)
        + tensor_xz * (tensor_xy * tensor_yz - tensor_yy * tensor_xz)
    )
    factor = jnp.where(tissue == 1, 1.0, 4.0).astype(jnp.float32) * grid_step
    return (
        jnp.sqrt(cofactor_x / determinant) * factor,
        jnp.sqrt(cofactor_y / determinant) * factor,
        jnp.sqrt(cofactor_z / determinant) * factor,
    )


def local_scan(step_cost, seeded, along_axis, backward):
    return lax.cond(
        backward,
        lambda: lax.associative_scan(compose, (step_cost, seeded), reverse=True, axis=along_axis),
        lambda: lax.associative_scan(compose, (step_cost, seeded), axis=along_axis),
    )


def shards(previous, fibre_tensor, tissue, stim_sites, stim_times):
    planes, cells_y, cells_z = previous.shape
    slabs = lax.axis_size("slab")
    slab_index = lax.axis_index("slab")
    group_index = lax.axis_index("order")
    grid_step = 2.0 / (planes * slabs)
    cost_x, cost_y, cost_z = slowness(fibre_tensor, tissue, grid_step)
    block_cells = planes * cells_y * cells_z
    local_index = stim_sites - slab_index * block_cells
    inside = (local_index >= 0) & (local_index < block_cells)
    clamped = jnp.where(inside, local_index, 0)
    values = jnp.where(inside, stim_times, LARGE_TIME)
    seeded = previous.reshape(-1).at[clamped].min(values).reshape(previous.shape)
    sweep_field = local_scan(cost_z, seeded, 2, group_index // 4 % 2 == 1)[1]
    sweep_field = local_scan(cost_y, sweep_field, 1, group_index // 2 % 2 == 1)[1]
    backward_x = group_index % 2 == 1
    line_add, line_min = local_scan(cost_x, sweep_field, 0, backward_x)
    total = (
        jnp.where(backward_x, line_add[0], line_add[-1]),
        jnp.where(backward_x, line_min[0], line_min[-1]),
    )
    plane_large = jnp.full((cells_y, cells_z), LARGE_TIME, jnp.float32)
    is_first = slab_index == 0
    is_last = slab_index == slabs - 1

    def relay(step_index, incoming):
        leaving = jnp.minimum(incoming + total[0], total[1])
        got_below = passed_along(leaving, "slab", 1)
        got_above = passed_along(leaving, "slab", -1)
        return jnp.where(
            backward_x,
            jnp.where(is_last, LARGE_TIME, got_above),
            jnp.where(is_first, LARGE_TIME, got_below),
        )

    incoming = lax.fori_loop(0, slabs - 1, relay, plane_large)
    sweep_field = jnp.minimum(incoming[None] + line_add, line_min)
    merged = lax.pmin(sweep_field, "order")
    return (merged, sweep_field[None])


def solution(mesh):
    placed = (P("slab", None, None), P(None, "slab", None, None), P("slab", None, None), P(), P())
    return jax.shard_map(
        shards,
        mesh=mesh,
        in_specs=placed,
        out_specs=(P("slab", None, None), P("order", "slab", None, None)),
        check_vma=False,
    )
```

profile of v0, /device:TPU:103, one launch (start us, length us, event | category | flops | bytes accessed | tf_op | source)
XLA Modules:
  0.0 848.0 jit_solution(1174277902713225214)
XLA Ops:
  18.4 118.3 %conditional.3 = (f32[2,384,256]{1,2,0:T(8,128)S(1)}) conditional(s32[]{:T(128)} %convert_element_type.11, (f32[2,384,256]{2,1,0:T(8,128)S(1)}, f32[2,384,256]{2,1,0:T(8,128)S(1)}) %tuple.40, (f32[2,384,256]{2,1,0:T(8,128)S(1)}, f32[2,384,256]{2,1,0:T(8,128)S(1)}) %tuple.40), branch_computations={%region_1.2_spmd, %region_2.3_spmd} | conditional | flops 1741824 | bytes 47650024 | solution.py:41
  136.7 123.6 %conditional.4 = (f32[2,384,256]{2,1,0:T(8,128)S(1)}) conditional(s32[]{:T(128)} %convert_element_type.10, (f32[2,384,256]{1,2,0:T(8,128)S(1)}, f32[2,384,256]{2,1,0:T(8,128)S(1)}) %tuple.41, (f32[2,384,256]{1,2,0:T(8,128)S(1)}, f32[2,384,256]{2,1,0:T(8,128)S(1)}) %tuple.41), branch_computations={%region_3.4_spmd, %region_4.5_spmd} | conditional | flops 1749504 | bytes 46160080 | solution.py:41
  265.5 427.8 %while.11 = (s32[]{:T(128)}, f32[384,256]{1,0:T(8,128)S(1)}, pred[]{:T(512)}, pred[]{:T(512)}, f32[384,256]{1,0:T(8,128)S(1)}, /*index=5*/f32[384,256]{1,0:T(8,128)S(1)}, pred[]{:T(512)}, s32[]{:T(128)}, s32[]{:T(128)}) while((s32[]{:T(128)}, f32[384,256]{1,0:T(8,128)S(1)}, pred[]{:T(512)}, pred[]{:T(512)}, ...), condition=%wide.region_8.9_spmd.clone, body=%wide.region_7.8_spmd.clone.sunk | while | flops 589827 | bytes 5898426 | solution.py:83
  272.3 6.0 collective-permute-done
  278.3 5.0 collective-permute-done.1
  288.7 5.5 collective-permute-done
  388.1 5.4 collective-permute-done
  401.8 6.5 collective-permute-done
  416.5 7.6 collective-permute-done
  432.6 6.9 collective-permute-done
  448.1 6.0 collective-permute-done
  462.6 5.1 collective-permute-done
  477.7 5.6 collective-permute-done
  486.3 5.2 collective-permute-start.1
  498.9 6.2 collective-permute-start.1
  511.9 6.2 collective-permute-start.1
  524.9 6.2 collective-permute-start.1
  537.9 6.2 collective-permute-start.1
  550.9 5.9 collective-permute-start.1
  563.6 5.9 collective-permute-start.1
  576.4 5.9 collective-permute-start.1
  589.9 6.4 collective-permute-start.1
  604.9 6.8 collective-permute-start.1
  611.7 5.8 collective-permute-done
  621.4 6.8 collective-permute-start.1
  628.2 7.0 collective-permute-done
  639.1 6.5 collective-permute-start.1
  645.6 7.0 collective-permute-done
  655.5 5.7 collective-permute-start.1
  661.2 5.8 collective-permute-done
  683.1 5.4 collective-permute-start.1
  695.5 143.6 %all-reduce.74.cloned.1.call-done = f32[2,384,256]{2,1,0:T(8,128)} async-done(((f32[2,384,256]{2,1,0:T(8,128)}), f32[2,384,256]{2,1,0:T(8,128)}) %all-reduce.74.cloned.1.call-update) | async-done | bytes 786448 | tf_op jit(solution)/shard_map/pmin | solution.py:85
  (390 shorter events, 521.8 us)
Async XLA Ops:
  7.2 831.9 %all-reduce.74.cloned.1.call-start = ((), (), s32[]{:S(2)}) async-start(), calls=%async_computation | async-start | bytes 1572864 | tf_op jit(solution)/shard_map/pmin | solution.py:85
  265.6 12.7 %collective-permute-start = (f32[384,256]{1,0:T(8,128)S(1)}, f32[384,256]{1,0:T(8,128)S(1)}, u32[]{:S(2)}, u32[]{:S(2)}) collective-permute-start(f32[384,256]{1,0:T(8,128)S(1)} %fusion.101), channel_id=1, source_target_pairs={{0,1},{1,2},{2,3},{3,4},{4,5},{5,6},{6,7},{7,8},{8,9},{9,10},{10,1... | collective-permute-start | bytes 1179656 | tf_op jit(solution)/shard_map/while/body/eval_jaxpr/ppermute | solution.py:12
  270.4 12.9 %collective-permute-start.1 = (f32[384,256]{1,0:T(8,128)S(1)}, f32[384,256]{1,0:T(8,128)S(1)}, u32[]{:S(2)}, u32[]{:S(2)}) collective-permute-start(f32[384,256]{1,0:T(8,128)S(1)} %fusion.101), channel_id=1, source_target_pairs={{1,0},{2,1},{3,2},{4,3},{5,4},{6,5},{7,6},{8,7},{9,8},{10,9},{11,1... | collective-permute-start | bytes 1179656 | tf_op jit(solution)/shard_map/while/body/eval_jaxpr/ppermute | solution.py:12
  285.4 12.0 %collective-permute-start.1 = (f32[384,256]{1,0:T(8,128)S(1)}, f32[384,256]{1,0:T(8,128)S(1)}, u32[]{:S(2)}, u32[]{:S(2)}) collective-permute-start(f32[384,256]{1,0:T(8,128)S(1)} %fusion.101), channel_id=1, source_target_pairs={{1,0},{2,1},{3,2},{4,3},{5,4},{6,5},{7,6},{8,7},{9,8},{10,9},{11,1... | collective-permute-start | bytes 1179656 | tf_op jit(solution)/shard_map/while/body/eval_jaxpr/ppermute | solution.py:12
  384.7 11.6 %collective-permute-start.1 = (f32[384,256]{1,0:T(8,128)S(1)}, f32[384,256]{1,0:T(8,128)S(1)}, u32[]{:S(2)}, u32[]{:S(2)}) collective-permute-start(f32[384,256]{1,0:T(8,128)S(1)} %fusion.101), channel_id=1, source_target_pairs={{1,0},{2,1},{3,2},{4,3},{5,4},{6,5},{7,6},{8,7},{9,8},{10,9},{11,1... | collective-permute-start | bytes 1179656 | tf_op jit(solution)/shard_map/while/body/eval_jaxpr/ppermute | solution.py:12
  396.5 11.8 %collective-permute-start = (f32[384,256]{1,0:T(8,128)S(1)}, f32[384,256]{1,0:T(8,128)S(1)}, u32[]{:S(2)}, u32[]{:S(2)}) collective-permute-start(f32[384,256]{1,0:T(8,128)S(1)} %fusion.101), channel_id=1, source_target_pairs={{0,1},{1,2},{2,3},{3,4},{4,5},{5,6},{6,7},{7,8},{8,9},{9,10},{10,1... | collective-permute-start | bytes 1179656 | tf_op jit(solution)/shard_map/while/body/eval_jaxpr/ppermute | solution.py:12
  398.4 12.7 %collective-permute-start.1 = (f32[384,256]{1,0:T(8,128)S(1)}, f32[384,256]{1,0:T(8,128)S(1)}, u32[]{:S(2)}, u32[]{:S(2)}) collective-permute-start(f32[384,256]{1,0:T(8,128)S(1)} %fusion.101), channel_id=1, source_target_pairs={{1,0},{2,1},{3,2},{4,3},{5,4},{6,5},{7,6},{8,7},{9,8},{10,9},{11,1... | collective-permute-start | bytes 1179656 | tf_op jit(solution)/shard_map/while/body/eval_jaxpr/ppermute | solution.py:12
  411.2 12.9 %collective-permute-start = (f32[384,256]{1,0:T(8,128)S(1)}, f32[384,256]{1,0:T(8,128)S(1)}, u32[]{:S(2)}, u32[]{:S(2)}) collective-permute-start(f32[384,256]{1,0:T(8,128)S(1)} %fusion.101), channel_id=1, source_target_pairs={{0,1},{1,2},{2,3},{3,4},{4,5},{5,6},{6,7},{7,8},{8,9},{9,10},{10,1... | collective-permute-start | bytes 1179656 | tf_op jit(solution)/shard_map/while/body/eval_jaxpr/ppermute | solution.py:12
  413.2 13.9 %collective-permute-start.1 = (f32[384,256]{1,0:T(8,128)S(1)}, f32[384,256]{1,0:T(8,128)S(1)}, u32[]{:S(2)}, u32[]{:S(2)}) collective-permute-start(f32[384,256]{1,0:T(8,128)S(1)} %fusion.101), channel_id=1, source_target_pairs={{1,0},{2,1},{3,2},{4,3},{5,4},{6,5},{7,6},{8,7},{9,8},{10,9},{11,1... | collective-permute-start | bytes 1179656 | tf_op jit(solution)/shard_map/while/body/eval_jaxpr/ppermute | solution.py:12
  427.3 12.2 %collective-permute-start = (f32[384,256]{1,0:T(8,128)S(1)}, f32[384,256]{1,0:T(8,128)S(1)}, u32[]{:S(2)}, u32[]{:S(2)}) collective-permute-start(f32[384,256]{1,0:T(8,128)S(1)} %fusion.101), channel_id=1, source_target_pairs={{0,1},{1,2},{2,3},{3,4},{4,5},{5,6},{6,7},{7,8},{8,9},{9,10},{10,1... | collective-permute-start | bytes 1179656 | tf_op jit(solution)/shard_map/while/body/eval_jaxpr/ppermute | solution.py:12
  429.2 13.4 %collective-permute-start.1 = (f32[384,256]{1,0:T(8,128)S(1)}, f32[384,256]{1,0:T(8,128)S(1)}, u32[]{:S(2)}, u32[]{:S(2)}) collective-permute-start(f32[384,256]{1,0:T(8,128)S(1)} %fusion.101), channel_id=1, source_target_pairs={{1,0},{2,1},{3,2},{4,3},{5,4},{6,5},{7,6},{8,7},{9,8},{10,9},{11,1... | collective-permute-start | bytes 1179656 | tf_op jit(solution)/shard_map/while/body/eval_jaxpr/ppermute | solution.py:12
  442.8 11.3 %collective-permute-start = (f32[384,256]{1,0:T(8,128)S(1)}, f32[384,256]{1,0:T(8,128)S(1)}, u32[]{:S(2)}, u32[]{:S(2)}) collective-permute-start(f32[384,256]{1,0:T(8,128)S(1)} %fusion.101), channel_id=1, source_target_pairs={{0,1},{1,2},{2,3},{3,4},{4,5},{5,6},{6,7},{7,8},{8,9},{9,10},{10,1... | collective-permute-start | bytes 1179656 | tf_op jit(solution)/shard_map/while/body/eval_jaxpr/ppermute | solution.py:12
  444.7 12.5 %collective-permute-start.1 = (f32[384,256]{1,0:T(8,128)S(1)}, f32[384,256]{1,0:T(8,128)S(1)}, u32[]{:S(2)}, u32[]{:S(2)}) collective-permute-start(f32[384,256]{1,0:T(8,128)S(1)} %fusion.101), channel_id=1, source_target_pairs={{1,0},{2,1},{3,2},{4,3},{5,4},{6,5},{7,6},{8,7},{9,8},{10,9},{11,1... | collective-permute-start | bytes 1179656 | tf_op jit(solution)/shard_map/while/body/eval_jaxpr/ppermute | solution.py:12
  459.3 11.6 %collective-permute-start.1 = (f32[384,256]{1,0:T(8,128)S(1)}, f32[384,256]{1,0:T(8,128)S(1)}, u32[]{:S(2)}, u32[]{:S(2)}) collective-permute-start(f32[384,256]{1,0:T(8,128)S(1)} %fusion.101), channel_id=1, source_target_pairs={{1,0},{2,1},{3,2},{4,3},{5,4},{6,5},{7,6},{8,7},{9,8},{10,9},{11,1... | collective-permute-start | bytes 1179656 | tf_op jit(solution)/shard_map/while/body/eval_jaxpr/ppermute | solution.py:12
  471.0 12.3 %collective-permute-start = (f32[384,256]{1,0:T(8,128)S(1)}, f32[384,256]{1,0:T(8,128)S(1)}, u32[]{:S(2)}, u32[]{:S(2)}) collective-permute-start(f32[384,256]{1,0:T(8,128)S(1)} %fusion.101), channel_id=1, source_target_pairs={{0,1},{1,2},{2,3},{3,4},{4,5},{5,6},{6,7},{7,8},{8,9},{9,10},{10,1... | collective-permute-start | bytes 1179656 | tf_op jit(solution)/shard_map/while/body/eval_jaxpr/ppermute | solution.py:12
  484.3 11.6 %collective-permute-start = (f32[384,256]{1,0:T(8,128)S(1)}, f32[384,256]{1,0:T(8,128)S(1)}, u32[]{:S(2)}, u32[]{:S(2)}) collective-permute-start(f32[384,256]{1,0:T(8,128)S(1)} %fusion.101), channel_id=1, source_target_pairs={{0,1},{1,2},{2,3},{3,4},{4,5},{5,6},{6,7},{7,8},{8,9},{9,10},{10,1... | collective-permute-start | bytes 1179656 | tf_op jit(solution)/shard_map/while/body/eval_jaxpr/ppermute | solution.py:12
  497.0 11.4 %collective-permute-start = (f32[384,256]{1,0:T(8,128)S(1)}, f32[384,256]{1,0:T(8,128)S(1)}, u32[]{:S(2)}, u32[]{:S(2)}) collective-permute-start(f32[384,256]{1,0:T(8,128)S(1)} %fusion.101), channel_id=1, source_target_pairs={{0,1},{1,2},{2,3},{3,4},{4,5},{5,6},{6,7},{7,8},{8,9},{9,10},{10,1... | collective-permute-start | bytes 1179656 | tf_op jit(solution)/shard_map/while/body/eval_jaxpr/ppermute | solution.py:12
  510.0 11.4 %collective-permute-start = (f32[384,256]{1,0:T(8,128)S(1)}, f32[384,256]{1,0:T(8,128)S(1)}, u32[]{:S(2)}, u32[]{:S(2)}) collective-permute-start(f32[384,256]{1,0:T(8,128)S(1)} %fusion.101), channel_id=1, source_target_pairs={{0,1},{1,2},{2,3},{3,4},{4,5},{5,6},{6,7},{7,8},{8,9},{9,10},{10,1... | collective-permute-start | bytes 1179656 | tf_op jit(solution)/shard_map/while/body/eval_jaxpr/ppermute | solution.py:12
  523.0 11.4 %collective-permute-start = (f32[384,256]{1,0:T(8,128)S(1)}, f32[384,256]{1,0:T(8,128)S(1)}, u32[]{:S(2)}, u32[]{:S(2)}) collective-permute-start(f32[384,256]{1,0:T(8,128)S(1)} %fusion.101), channel_id=1, source_target_pairs={{0,1},{1,2},{2,3},{3,4},{4,5},{5,6},{6,7},{7,8},{8,9},{9,10},{10,1... | collective-permute-start | bytes 1179656 | tf_op jit(solution)/shard_map/while/body/eval_jaxpr/ppermute | solution.py:12
  536.0 11.4 %collective-permute-start = (f32[384,256]{1,0:T(8,128)S(1)}, f32[384,256]{1,0:T(8,128)S(1)}, u32[]{:S(2)}, u32[]{:S(2)}) collective-permute-start(f32[384,256]{1,0:T(8,128)S(1)} %fusion.101), channel_id=1, source_target_pairs={{0,1},{1,2},{2,3},{3,4},{4,5},{5,6},{6,7},{7,8},{8,9},{9,10},{10,1... | collective-permute-start | bytes 1179656 | tf_op jit(solution)/shard_map/while/body/eval_jaxpr/ppermute | solution.py:12
  574.4 11.6 %collective-permute-start = (f32[384,256]{1,0:T(8,128)S(1)}, f32[384,256]{1,0:T(8,128)S(1)}, u32[]{:S(2)}, u32[]{:S(2)}) collective-permute-start(f32[384,256]{1,0:T(8,128)S(1)} %fusion.101), channel_id=1, source_target_pairs={{0,1},{1,2},{2,3},{3,4},{4,5},{5,6},{6,7},{7,8},{8,9},{9,10},{10,1... | collective-permute-start | bytes 1179656 | tf_op jit(solution)/shard_map/while/body/eval_jaxpr/ppermute | solution.py:12
  576.4 11.4 %collective-permute-start.1 = (f32[384,256]{1,0:T(8,128)S(1)}, f32[384,256]{1,0:T(8,128)S(1)}, u32[]{:S(2)}, u32[]{:S(2)}) collective-permute-start(f32[384,256]{1,0:T(8,128)S(1)} %fusion.101), channel_id=1, source_target_pairs={{1,0},{2,1},{3,2},{4,3},{5,4},{6,5},{7,6},{8,7},{9,8},{10,9},{11,1... | collective-permute-start | bytes 1179656 | tf_op jit(solution)/shard_map/while/body/eval_jaxpr/ppermute | solution.py:12
  588.0 13.1 %collective-permute-start = (f32[384,256]{1,0:T(8,128)S(1)}, f32[384,256]{1,0:T(8,128)S(1)}, u32[]{:S(2)}, u32[]{:S(2)}) collective-permute-start(f32[384,256]{1,0:T(8,128)S(1)} %fusion.101), channel_id=1, source_target_pairs={{0,1},{1,2},{2,3},{3,4},{4,5},{5,6},{6,7},{7,8},{8,9},{9,10},{10,1... | collective-permute-start | bytes 1179656 | tf_op jit(solution)/shard_map/while/body/eval_jaxpr/ppermute | solution.py:12
  589.9 12.9 %collective-permute-start.1 = (f32[384,256]{1,0:T(8,128)S(1)}, f32[384,256]{1,0:T(8,128)S(1)}, u32[]{:S(2)}, u32[]{:S(2)}) collective-permute-start(f32[384,256]{1,0:T(8,128)S(1)} %fusion.101), channel_id=1, source_target_pairs={{1,0},{2,1},{3,2},{4,3},{5,4},{6,5},{7,6},{8,7},{9,8},{10,9},{11,1... | collective-permute-start | bytes 1179656 | tf_op jit(solution)/shard_map/while/body/eval_jaxpr/ppermute | solution.py:12
  603.0 14.6 %collective-permute-start = (f32[384,256]{1,0:T(8,128)S(1)}, f32[384,256]{1,0:T(8,128)S(1)}, u32[]{:S(2)}, u32[]{:S(2)}) collective-permute-start(f32[384,256]{1,0:T(8,128)S(1)} %fusion.101), channel_id=1, source_target_pairs={{0,1},{1,2},{2,3},{3,4},{4,5},{5,6},{6,7},{7,8},{8,9},{9,10},{10,1... | collective-permute-start | bytes 1179656 | tf_op jit(solution)/shard_map/while/body/eval_jaxpr/ppermute | solution.py:12
  604.9 14.4 %collective-permute-start.1 = (f32[384,256]{1,0:T(8,128)S(1)}, f32[384,256]{1,0:T(8,128)S(1)}, u32[]{:S(2)}, u32[]{:S(2)}) collective-permute-start(f32[384,256]{1,0:T(8,128)S(1)} %fusion.101), channel_id=1, source_target_pairs={{1,0},{2,1},{3,2},{4,3},{5,4},{6,5},{7,6},{8,7},{9,8},{10,9},{11,1... | collective-permute-start | bytes 1179656 | tf_op jit(solution)/shard_map/while/body/eval_jaxpr/ppermute | solution.py:12
  619.5 15.7 %collective-permute-start = (f32[384,256]{1,0:T(8,128)S(1)}, f32[384,256]{1,0:T(8,128)S(1)}, u32[]{:S(2)}, u32[]{:S(2)}) collective-permute-start(f32[384,256]{1,0:T(8,128)S(1)} %fusion.101), channel_id=1, source_target_pairs={{0,1},{1,2},{2,3},{3,4},{4,5},{5,6},{6,7},{7,8},{8,9},{9,10},{10,1... | collective-permute-start | bytes 1179656 | tf_op jit(solution)/shard_map/while/body/eval_jaxpr/ppermute | solution.py:12
  621.4 15.6 %collective-permute-start.1 = (f32[384,256]{1,0:T(8,128)S(1)}, f32[384,256]{1,0:T(8,128)S(1)}, u32[]{:S(2)}, u32[]{:S(2)}) collective-permute-start(f32[384,256]{1,0:T(8,128)S(1)} %fusion.101), channel_id=1, source_target_pairs={{1,0},{2,1},{3,2},{4,3},{5,4},{6,5},{7,6},{8,7},{9,8},{10,9},{11,1... | collective-permute-start | bytes 1179656 | tf_op jit(solution)/shard_map/while/body/eval_jaxpr/ppermute | solution.py:12
  637.1 15.5 %collective-permute-start = (f32[384,256]{1,0:T(8,128)S(1)}, f32[384,256]{1,0:T(8,128)S(1)}, u32[]{:S(2)}, u32[]{:S(2)}) collective-permute-start(f32[384,256]{1,0:T(8,128)S(1)} %fusion.101), channel_id=1, source_target_pairs={{0,1},{1,2},{2,3},{3,4},{4,5},{5,6},{6,7},{7,8},{8,9},{9,10},{10,1... | collective-permute-start | bytes 1179656 | tf_op jit(solution)/shard_map/while/body/eval_jaxpr/ppermute | solution.py:12
  639.1 14.4 %collective-permute-start.1 = (f32[384,256]{1,0:T(8,128)S(1)}, f32[384,256]{1,0:T(8,128)S(1)}, u32[]{:S(2)}, u32[]{:S(2)}) collective-permute-start(f32[384,256]{1,0:T(8,128)S(1)} %fusion.101), channel_id=1, source_target_pairs={{1,0},{2,1},{3,2},{4,3},{5,4},{6,5},{7,6},{8,7},{9,8},{10,9},{11,1... | collective-permute-start | bytes 1179656 | tf_op jit(solution)/shard_map/while/body/eval_jaxpr/ppermute | solution.py:12
  653.6 13.3 %collective-permute-start = (f32[384,256]{1,0:T(8,128)S(1)}, f32[384,256]{1,0:T(8,128)S(1)}, u32[]{:S(2)}, u32[]{:S(2)}) collective-permute-start(f32[384,256]{1,0:T(8,128)S(1)} %fusion.101), channel_id=1, source_target_pairs={{0,1},{1,2},{2,3},{3,4},{4,5},{5,6},{6,7},{7,8},{8,9},{9,10},{10,1... | collective-permute-start | bytes 1179656 | tf_op jit(solution)/shard_map/while/body/eval_jaxpr/ppermute | solution.py:12
  655.5 12.3 %collective-permute-start.1 = (f32[384,256]{1,0:T(8,128)S(1)}, f32[384,256]{1,0:T(8,128)S(1)}, u32[]{:S(2)}, u32[]{:S(2)}) collective-permute-start(f32[384,256]{1,0:T(8,128)S(1)} %fusion.101), channel_id=1, source_target_pairs={{1,0},{2,1},{3,2},{4,3},{5,4},{6,5},{7,6},{8,7},{9,8},{10,9},{11,1... | collective-permute-start | bytes 1179656 | tf_op jit(solution)/shard_map/while/body/eval_jaxpr/ppermute | solution.py:12
  (43 other events, 805.9 us)
Sparse Core Ops, SparseCore 0:
  695.6 143.4 all-reduce.73
where the time goes:
time: 861 us; the launch traced here: 848 us
  waiting for transfers between devices  360 us (42%)
  starting transfers between devices  206 us (24%)
  local copies, waits for them, and re-layouts  179 us (21%)
  other arithmetic  87.2 us (10%)
  between operations  14.2 us (2%)
    ppermute x62, waiting for transfers between devices, passed_along(): return lax.ppermute(block, axis, route)  216 us
    ppermute x62, starting transfers between devices, passed_along(): return lax.ppermute(block, axis, route)  206 us
    pmin x1, waiting for transfers between devices, shards(): merged = lax.pmin(sweep_field, 'order')  144 us
    slice x95, local copies, waits for them, and re-layouts, local_scan(): lax.associative_scan(compose, (step_cost, seeded), axis=along_axis)  116 us
    pad x29, local copies, waits for them, and re-layouts, local_scan(): lax.associative_scan(compose, (step_cost, seeded), axis=along_axis)  54.8 us
    add x16, other arithmetic, local_scan(): lax.associative_scan(compose, (step_cost, seeded), axis=along_axis)  23 us
    add x13, other arithmetic, compose(): earlier_add + later_add  19.7 us
  transfers between devices with their start and end apart: 63, of which 63 were waited for; matrix products, arithmetic and copies ran while one was open for 0% of the time, Pallas kernels for 0%

commit v1 on v0

v1 whole, which is shorter than its diff:
```python
import functools

import jax
import jax.numpy as jnp
from jax import lax
from jax.experimental import pallas as pl
from jax.experimental.pallas import tpu as pltpu
from jax.sharding import PartitionSpec as P

ROWS = 8


def scan_step(a, m, k, axis, reverse, last):
    n = a.shape[axis]
    index = lax.broadcasted_iota(jnp.int32, a.shape, axis)
    shift = n - k if reverse else k
    source = pltpu.roll(index, shift, axis)
    valid = source == (index + k if reverse else index - k)
    a_src = pltpu.roll(a, shift, axis)
    m_src = pltpu.roll(m, shift, axis)
    m = jnp.where(valid, jnp.minimum(m_src + a, m), m)
    if not last:
        a = jnp.where(valid, a_src + a, a)
    return a, m


def block_scan(a, m, axis, reverse, need_sum):
    n = a.shape[axis]
    k = 1
    while k < n:
        a, m = scan_step(a, m, k, axis, reverse, last=(2 * k >= n) and not need_sum)
        k *= 2
    return a, m


def local_kernel(flags, fibre, tissue, seeded, line_add, line_min, cost_x, cost_y, field,
                 *, grid_step):
    planes, cells_y, cells_z = seeded.shape
    blocks = cells_y // ROWS
    inf = jnp.float32(jnp.inf)

    def costs_and_z(reverse):
        def body(i, carry):
            p = i // blocks
            rows = pl.ds(pl.multiple_of((i % blocks) * ROWS, ROWS), ROWS)
            xx = fibre[0, p, rows, :]
            yy = fibre[1, p, rows, :]
            zz = fibre[2, p, rows, :]
            xy = fibre[3, p, rows, :]
            xz = fibre[4, p, rows, :]
            yz = fibre[5, p, rows, :]
            cx = yy * zz - yz * yz
            cy = xx * zz - xz * xz
            cz = xx * yy - xy * xy
            det = xx * cx - xy * (xy * zz - yz * xz) + xz * (xy * yz - yy * xz)
            factor = jnp.where(tissue[p, rows, :] == 1, 1.0, 4.0).astype(jnp.float32) * grid_step
            cost_x[p, rows, :] = jnp.sqrt(cx / det) * factor
            cost_y[p, rows, :] = jnp.sqrt(cy / det) * factor
            step_z = jnp.sqrt(cz / det) * factor
            _, u = block_scan(step_z, seeded[p, rows, :], 1, reverse, False)
            field[p, rows, :] = u
            return carry

        lax.fori_loop(0, planes * blocks, body, 0)

    def sweep_y(reverse):
        def body(j, carry):
            i = blocks - 1 - j if reverse else j
            rows = pl.ds(pl.multiple_of(i * ROWS, ROWS), ROWS)
            out = []
            for p in range(planes):
                a, m = block_scan(cost_y[p, rows, :], field[p, rows, :], 0, reverse, True)
                u = jnp.minimum(carry[p] + a, m)
                field[p, rows, :] = u
                edge = u[0:1, :] if reverse else u[ROWS - 1:ROWS, :]
                out.append(jnp.broadcast_to(edge, u.shape))
            return tuple(out)

        start = tuple(jnp.full((ROWS, cells_z), inf, jnp.float32) for _ in range(planes))
        lax.fori_loop(0, blocks, body, start)

    def sweep_x(reverse):
        def body(i, carry):
            rows = pl.ds(pl.multiple_of(i * ROWS, ROWS), ROWS)
            order = range(planes - 1, -1, -1) if reverse else range(planes)
            a = None
            m = None
            for p in order:
                c = cost_x[p, rows, :]
                u = field[p, rows, :]
                if a is None:
                    a, m = c, u
                else:
                    a, m = a + c, jnp.minimum(m + c, u)
                line_add[p, rows, :] = a
                line_min[p, rows, :] = m
            return carry

        lax.fori_loop(0, blocks, body, 0)

    for flag, fn in ((flags[2], costs_and_z), (flags[1], sweep_y), (flags[0], sweep_x)):
        pl.when(flag == 1)(functools.partial(fn, True))
        pl.when(flag != 1)(functools.partial(fn, False))


def local_sweeps(flags, fibre, tissue, seeded, grid_step):
    planes, cells_y, cells_z = seeded.shape
    plane = jax.ShapeDtypeStruct(seeded.shape, jnp.float32)
    vmem = pl.BlockSpec(memory_space=pltpu.VMEM)
    elements = planes * cells_y * cells_z
    return pl.pallas_call(
        functools.partial(local_kernel, grid_step=grid_step),
        out_shape=(plane, plane),
        in_specs=[pl.BlockSpec(memory_space=pltpu.SMEM), vmem, vmem, vmem],
        out_specs=(vmem, vmem),
        scratch_shapes=[pltpu.VMEM(seeded.shape, jnp.float32) for _ in range(3)],
        compiler_params=pltpu.CompilerParams(vmem_limit_bytes=48 * 1024 * 1024),
        cost_estimate=pl.CostEstimate(
            flops=300 * elements, transcendentals=6 * elements, bytes_accessed=44 * elements
        ),
    )(flags, fibre, tissue, seeded)


def shifted(value, distance, orders, slabs):
    route = []
    for g in range(orders):
        for s in range(slabs):
            t = s + distance if g % 2 == 0 else s - distance
            if 0 <= t < slabs:
                route.append((g * slabs + s, g * slabs + t))
    return lax.ppermute(value, ("order", "slab"), route)


def shards(previous, fibre_tensor, tissue, stim_sites, stim_times):
    planes, cells_y, cells_z = previous.shape
    slabs = lax.axis_size("slab")
    orders = lax.axis_size("order")
    slab_index = lax.axis_index("slab")
    group_index = lax.axis_index("order")
    grid_step = 2.0 / (planes * slabs)

    plane_index = stim_sites // (cells_y * cells_z) - slab_index * planes
    inside = (plane_index >= 0) & (plane_index < planes)
    plane_index = jnp.where(inside, plane_index, planes)
    row_index = stim_sites // cells_z % cells_y
    column_index = stim_sites % cells_z
    seeded = previous.at[plane_index, row_index, column_index].min(stim_times, mode="drop")

    bits = jnp.stack([group_index % 2, group_index // 2 % 2, group_index // 4 % 2]).astype(jnp.int32)
    line_add, line_min = local_sweeps(bits, fibre_tensor, tissue, seeded, grid_step)

    backward_x = group_index % 2 == 1
    rank = jnp.where(backward_x, slabs - 1 - slab_index, slab_index)
    edge = jnp.where(backward_x, 0, planes - 1)
    total_add = lax.dynamic_index_in_dim(line_add, edge, 0, keepdims=False)
    total_min = lax.dynamic_index_in_dim(line_min, edge, 0, keepdims=False)

    distance = 1
    while distance < slabs:
        if 2 * distance < slabs:
            got = shifted(jnp.stack([total_add, total_min]), distance, orders, slabs)
            take = rank >= distance
            total_min = jnp.where(take, jnp.minimum(got[1] + total_add, total_min), total_min)
            total_add = jnp.where(take, got[0] + total_add, total_add)
        else:
            got = shifted(total_min, distance, orders, slabs)
            total_min = jnp.where(rank >= distance, jnp.minimum(got + total_add, total_min), total_min)
        distance *= 2
    got = shifted(total_min, 1, orders, slabs)
    incoming = jnp.where(rank >= 1, got, jnp.inf)

    sweep_field = jnp.minimum(incoming[None] + line_add, line_min)
    merged = sweep_field
    mask = 1
    while mask < orders:
        got = lax.ppermute(merged, "order", [(g, g ^ mask) for g in range(orders)])
        merged = jnp.minimum(merged, got)
        mask *= 2
    return (merged, sweep_field[None])


def solution(mesh):
    placed = (P("slab", None, None), P(None, "slab", None, None), P("slab", None, None), P(), P())
    return jax.shard_map(
        shards,
        mesh=mesh,
        in_specs=placed,
        out_specs=(P("slab", None, None), P("order", "slab", None, None)),
        check_vma=False,
    )
```

time: 861 us -> 231 us (0.27); the launches traced: 848 us -> 228 us
  waiting for transfers between devices: 360 us -> 115 us
  local copies, waits for them, and re-layouts: 179 us -> 3.81 us
  starting transfers between devices: 206 us -> 41.1 us
  other arithmetic: 87.2 us -> 13.9 us
  Pallas kernels: 0 us -> 53.6 us
  between operations: 14.2 us -> 0.81 us
    ppermute x62 -> x9, starting transfers between devices: 206 us -> 41.1 us  [the longest x6 30.5 us: shifted(): return lax.ppermute(value, ('order', 'slab'), route)]
    pmin x1 -> x0, waiting for transfers between devices: 144 us -> none  [shards(): merged = lax.pmin(sweep_field, 'order')]
    slice x95 -> x0, local copies, waits for them, and re-layouts: 116 us -> none  [local_scan(): lax.associative_scan(compose, (step_cost, seeded), axis=along_axis)]
    ppermute x62 -> x9, waiting for transfers between devices: 216 us -> 115 us  [the longest x6 79.4 us: shifted(): return lax.ppermute(value, ('order', 'slab'), route)]
    pad x29 -> x0, local copies, waits for them, and re-layouts: 54.8 us -> none  [local_scan(): lax.associative_scan(compose, (step_cost, seeded), axis=along_axis)]
    pallas_call x0 -> x1, Pallas kernels: none -> 53.6 us  [local_sweeps(): pl.pallas_call(functools.partial(local_kernel, grid_step=grid_step), out_...]
    add x30 -> x0, other arithmetic: 42.8 us -> none  [the longest x16 23 us: local_scan(): lax.associative_scan(compose, (step_cost, seeded), axis=along_axis)]
    min x46 -> x3, other arithmetic: 17.5 us -> 1.18 us  [shards(): merged = jnp.minimum(merged, got)]
  transfers between devices with their start and end apart: 63 -> 9, of which waited for: 63 -> 9; matrix products, arithmetic and copies ran while one was open for 0% -> 0% of each run, Pallas kernels for 0% -> 0%
where the time goes in v1:
time: 231 us; the launch traced here: 228 us
  waiting for transfers between devices  115 us (50%)
  Pallas kernels  53.6 us (23%)
  starting transfers between devices  41.1 us (18%)
  other arithmetic  13.9 us (6%)
  local copies, waits for them, and re-layouts  3.81 us (2%)
    ppermute x6, waiting for transfers between devices, shifted(): return lax.ppermute(value, ('order', 'slab'), route)  79.4 us
    pallas_call x1, Pallas kernels, local_sweeps(): pl.pallas_call(functools.partial(local_kernel, grid_step=grid_step), out_...  53.6 us
    ppermute x3, waiting for transfers between devices, shards(): got = lax.ppermute(merged, 'order', [(g, g ^ mask) for g in range(orders)])  35.8 us
    ppermute x6, starting transfers between devices, shifted(): return lax.ppermute(value, ('order', 'slab'), route)  30.5 us
    ppermute x3, starting transfers between devices, shards(): got = lax.ppermute(merged, 'order', [(g, g ^ mask) for g in range(orders)])  10.6 us
  transfers between devices with their start and end apart: 9, of which 9 were waited for; matrix products, arithmetic and copies ran while one was open for 0% of the time, Pallas kernels for 0%

profile of v1, /device:TPU:103, one launch (start us, length us, event | category | flops | bytes accessed | tf_op | source)
XLA Modules:
  0.0 228.5 jit_solution(18139607847155034960)
XLA Ops:
  0.6 1.1 copy.9
  2.5 2.0 scatter_fusion
  4.6 1.1 copy-done
  5.7 53.6 %shard_map.68 = (f32[2,384,256]{2,1,0:T(8,128)S(1)}, f32[2,384,256]{2,1,0:T(8,128)S(1)}) custom-call(s32[3]{0:T(128)S(1)} %pad_add_fusion.flags, f32[6,2,384,256]{3,2,1,0:T(8,128)} %fibre.1, s32[2,384,256]{2,1,0:T(8,128)S(1)} %copy-done, f32[2,384,256]{2,1,0:T(8,128)S(1)} %scatter_fusion), custom_call_target="tpu_custom_call" | custom-call | flops 58982400 | bytes 8650752 | tf_op jit(solution)/shard_map/pallas_call | solution.py:111
  59.4 0.9 pad_maximum_fusion
  60.3 1.9 collective-permute-start
  62.3 12.4 %collective-permute-done = f32[2,384,256]{2,1,0:T(8,128)S(1)} collective-permute-done((f32[2,384,256]{2,1,0:T(8,128)}, f32[2,384,256]{2,1,0:T(8,128)S(1)}, u32[]{:S(2)}, u32[]{:S(2)}) %collective-permute-start) | collective-permute-done | bytes 786464 | tf_op jit(solution)/shard_map/ppermute | solution.py:131
  75.5 0.9 pad_maximum_fusion.1
  76.5 1.9 collective-permute-start.1
  78.4 21.7 %collective-permute-done.1 = f32[2,384,256]{2,1,0:T(8,128)} collective-permute-done((f32[2,384,256]{2,1,0:T(8,128)}, f32[2,384,256]{2,1,0:T(8,128)}, u32[]{:S(2)}, u32[]{:S(2)}) %collective-permute-start.1) | collective-permute-done | bytes 786464 | tf_op jit(solution)/shard_map/ppermute | solution.py:131
  100.0 1.5 add_select_fusion.5
  101.5 0.7 copy-done.1
  102.2 0.9 pad_maximum_fusion.2
  103.2 6.2 %collective-permute-start.2 = (f32[2,384,256]{2,1,0:T(8,128)}, f32[2,384,256]{2,1,0:T(8,128)}, u32[]{:S(2)}, u32[]{:S(2)}) collective-permute-start(f32[2,384,256]{2,1,0:T(8,128)} %pad_maximum_fusion.2), channel_id=1, source_target_pairs={{0,4},{1,5},{2,6},{3,7},{4,8},{5,9},{6,10},{7,11},{8,12},{9,13},{1... | collective-permute-start | bytes 2359304 | tf_op jit(solution)/shard_map/ppermute | solution.py:131
  109.3 24.5 %collective-permute-done.2 = f32[2,384,256]{2,1,0:T(8,128)} collective-permute-done((f32[2,384,256]{2,1,0:T(8,128)}, f32[2,384,256]{2,1,0:T(8,128)}, u32[]{:S(2)}, u32[]{:S(2)}) %collective-permute-start.2) | collective-permute-done | bytes 786464 | tf_op jit(solution)/shard_map/ppermute | solution.py:131
  133.9 1.3 add_select_fusion.4
  135.2 0.9 pad_maximum_fusion.3
  136.1 14.4 %collective-permute-start.3 = (f32[2,384,256]{2,1,0:T(8,128)}, f32[2,384,256]{2,1,0:T(8,128)}, u32[]{:S(2)}, u32[]{:S(2)}) collective-permute-start(f32[2,384,256]{2,1,0:T(8,128)} %pad_maximum_fusion.3), channel_id=1, source_target_pairs={{0,8},{1,9},{2,10},{3,11},{4,12},{5,13},{6,14},{7,15},{8,16},{9,17... | collective-permute-start | bytes 2359304 | tf_op jit(solution)/shard_map/ppermute | solution.py:131
  150.6 8.3 %collective-permute-done.3 = f32[2,384,256]{2,1,0:T(8,128)} collective-permute-done((f32[2,384,256]{2,1,0:T(8,128)}, f32[2,384,256]{2,1,0:T(8,128)}, u32[]{:S(2)}, u32[]{:S(2)}) %collective-permute-start.3) | collective-permute-done | bytes 786464 | tf_op jit(solution)/shard_map/ppermute | solution.py:131
  158.9 1.7 minimum_select_fusion.1
  160.6 4.2 %collective-permute-start.4 = (f32[384,256]{1,0:T(8,128)S(1)}, f32[384,256]{1,0:T(8,128)S(1)}, u32[]{:S(2)}, u32[]{:S(2)}) collective-permute-start(f32[384,256]{1,0:T(8,128)S(1)} %minimum_select_fusion.1), channel_id=1, source_target_pairs={{0,16},{1,17},{2,18},{3,19},{4,20},{5,21},{6,22},{7,23},{8,24},{9,... | collective-permute-start | bytes 1179656 | tf_op jit(solution)/shard_map/ppermute | solution.py:131
  164.8 4.7 %collective-permute-done.4 = f32[384,256]{1,0:T(8,128)S(1)} collective-permute-done((f32[384,256]{1,0:T(8,128)S(1)}, f32[384,256]{1,0:T(8,128)S(1)}, u32[]{:S(2)}, u32[]{:S(2)}) %collective-permute-start.4) | collective-permute-done | bytes 393248 | tf_op jit(solution)/shard_map/ppermute | solution.py:131
  169.5 1.4 minimum_select_fusion
  170.9 1.9 collective-permute-start.5
  172.8 7.8 %collective-permute-done.5 = f32[384,256]{1,0:T(8,128)S(1)} collective-permute-done((f32[384,256]{1,0:T(8,128)S(1)}, f32[384,256]{1,0:T(8,128)S(1)}, u32[]{:S(2)}, u32[]{:S(2)}) %collective-permute-start.5) | collective-permute-done | bytes 393248 | tf_op jit(solution)/shard_map/ppermute | solution.py:131
  180.8 6.3 %collective-permute-start.6 = (f32[2,384,256]{2,1,0:T(8,128)S(1)}, f32[2,384,256]{2,1,0:T(8,128)S(1)}, u32[]{:S(2)}, u32[]{:S(2)}) collective-permute-start(f32[2,384,256]{2,1,0:T(8,128)S(1)} %add_minimum_fusion), channel_id=1, source_target_pairs={{0,32},{32,0},{64,96},{96,64},{128,160},{160,128},{192,224},{224,1... | collective-permute-start | bytes 2359304 | tf_op jit(solution)/shard_map/ppermute | solution.py:176
  187.1 1.9 collective-permute-done.6
  189.1 1.4 collective-permute-start.7
  190.5 17.5 %collective-permute-done.7 = f32[2,384,256]{2,1,0:T(8,128)S(1)} collective-permute-done((f32[2,384,256]{2,1,0:T(8,128)S(1)}, f32[2,384,256]{2,1,0:T(8,128)S(1)}, u32[]{:S(2)}, u32[]{:S(2)}) %collective-permute-start.7) | collective-permute-done | bytes 786464 | tf_op jit(solution)/shard_map/ppermute | solution.py:176
  208.0 3.0 %collective-permute-start.8 = (f32[2,384,256]{2,1,0:T(8,128)S(1)}, f32[2,384,256]{2,1,0:T(8,128)S(1)}, u32[]{:S(2)}, u32[]{:S(2)}) collective-permute-start(f32[2,384,256]{2,1,0:T(8,128)S(1)} %min.51), channel_id=1, source_target_pairs={{0,128},{32,160},{64,192},{96,224},{128,0},{160,32},{192,64},{224,... | collective-permute-start | bytes 2359304 | tf_op jit(solution)/shard_map/ppermute | solution.py:176
  211.0 16.4 %collective-permute-done.8 = f32[2,384,256]{2,1,0:T(8,128)S(1)} collective-permute-done((f32[2,384,256]{2,1,0:T(8,128)S(1)}, f32[2,384,256]{2,1,0:T(8,128)S(1)}, u32[]{:S(2)}, u32[]{:S(2)}) %collective-permute-start.8) | collective-permute-done | bytes 786464 | tf_op jit(solution)/shard_map/ppermute | solution.py:176
  227.5 1.0 min.52
  (16 shorter events, 2.0 us)
Async XLA Ops:
  4.6 1.1 copy-start
  60.3 14.3 %collective-permute-start = (f32[2,384,256]{2,1,0:T(8,128)}, f32[2,384,256]{2,1,0:T(8,128)S(1)}, u32[]{:S(2)}, u32[]{:S(2)}) collective-permute-start(f32[2,384,256]{2,1,0:T(8,128)} %pad_maximum_fusion), channel_id=1, source_target_pairs={{0,1},{1,2},{2,3},{3,4},{4,5},{5,6},{6,7},{7,8},{8,9},{9,10},{10,1... | collective-permute-start | bytes 2359304 | tf_op jit(solution)/shard_map/ppermute | solution.py:131
  74.8 0.7 copy-start.2
  74.8 1.7 copy-start.3
  76.5 23.6 %collective-permute-start.1 = (f32[2,384,256]{2,1,0:T(8,128)}, f32[2,384,256]{2,1,0:T(8,128)}, u32[]{:S(2)}, u32[]{:S(2)}) collective-permute-start(f32[2,384,256]{2,1,0:T(8,128)} %pad_maximum_fusion.1), channel_id=1, source_target_pairs={{0,2},{1,3},{2,4},{3,5},{4,6},{5,7},{6,8},{7,9},{8,10},{9,11},{10,... | collective-permute-start | bytes 2359304 | tf_op jit(solution)/shard_map/ppermute | solution.py:131
  101.5 0.7 copy-start.1
  103.2 30.7 %collective-permute-start.2 = (f32[2,384,256]{2,1,0:T(8,128)}, f32[2,384,256]{2,1,0:T(8,128)}, u32[]{:S(2)}, u32[]{:S(2)}) collective-permute-start(f32[2,384,256]{2,1,0:T(8,128)} %pad_maximum_fusion.2), channel_id=1, source_target_pairs={{0,4},{1,5},{2,6},{3,7},{4,8},{5,9},{6,10},{7,11},{8,12},{9,13},{1... | collective-permute-start | bytes 2359304 | tf_op jit(solution)/shard_map/ppermute | solution.py:131
  136.1 22.8 %collective-permute-start.3 = (f32[2,384,256]{2,1,0:T(8,128)}, f32[2,384,256]{2,1,0:T(8,128)}, u32[]{:S(2)}, u32[]{:S(2)}) collective-permute-start(f32[2,384,256]{2,1,0:T(8,128)} %pad_maximum_fusion.3), channel_id=1, source_target_pairs={{0,8},{1,9},{2,10},{3,11},{4,12},{5,13},{6,14},{7,15},{8,16},{9,17... | collective-permute-start | bytes 2359304 | tf_op jit(solution)/shard_map/ppermute | solution.py:131
  160.6 8.9 %collective-permute-start.4 = (f32[384,256]{1,0:T(8,128)S(1)}, f32[384,256]{1,0:T(8,128)S(1)}, u32[]{:S(2)}, u32[]{:S(2)}) collective-permute-start(f32[384,256]{1,0:T(8,128)S(1)} %minimum_select_fusion.1), channel_id=1, source_target_pairs={{0,16},{1,17},{2,18},{3,19},{4,20},{5,21},{6,22},{7,23},{8,24},{9,... | collective-permute-start | bytes 1179656 | tf_op jit(solution)/shard_map/ppermute | solution.py:131
  170.9 9.7 %collective-permute-start.5 = (f32[384,256]{1,0:T(8,128)S(1)}, f32[384,256]{1,0:T(8,128)S(1)}, u32[]{:S(2)}, u32[]{:S(2)}) collective-permute-start(f32[384,256]{1,0:T(8,128)S(1)} %minimum_select_fusion), channel_id=1, source_target_pairs={{0,1},{1,2},{2,3},{3,4},{4,5},{5,6},{6,7},{7,8},{8,9},{9,10},{10,1... | collective-permute-start | bytes 1179656 | tf_op jit(solution)/shard_map/ppermute | solution.py:131
  180.8 47.7 %copy-start.4 = (f32[2,384,256]{2,1,0:T(8,128)}, f32[2,384,256]{2,1,0:T(8,128)S(1)}, u32[]{:S(2)}) copy-start(f32[2,384,256]{2,1,0:T(8,128)S(1)} %add_minimum_fusion) | copy-start | bytes 2359300
  180.8 8.2 %collective-permute-start.6 = (f32[2,384,256]{2,1,0:T(8,128)S(1)}, f32[2,384,256]{2,1,0:T(8,128)S(1)}, u32[]{:S(2)}, u32[]{:S(2)}) collective-permute-start(f32[2,384,256]{2,1,0:T(8,128)S(1)} %add_minimum_fusion), channel_id=1, source_target_pairs={{0,32},{32,0},{64,96},{96,64},{128,160},{160,128},{192,224},{224,1... | collective-permute-start | bytes 2359304 | tf_op jit(solution)/shard_map/ppermute | solution.py:176
  189.1 18.8 %collective-permute-start.7 = (f32[2,384,256]{2,1,0:T(8,128)S(1)}, f32[2,384,256]{2,1,0:T(8,128)S(1)}, u32[]{:S(2)}, u32[]{:S(2)}) collective-permute-start(f32[2,384,256]{2,1,0:T(8,128)S(1)} %min.50), channel_id=1, source_target_pairs={{0,64},{32,96},{64,0},{96,32},{128,192},{160,224},{192,128},{224,1... | collective-permute-start | bytes 2359304 | tf_op jit(solution)/shard_map/ppermute | solution.py:176
  208.0 19.4 %collective-permute-start.8 = (f32[2,384,256]{2,1,0:T(8,128)S(1)}, f32[2,384,256]{2,1,0:T(8,128)S(1)}, u32[]{:S(2)}, u32[]{:S(2)}) collective-permute-start(f32[2,384,256]{2,1,0:T(8,128)S(1)} %min.51), channel_id=1, source_target_pairs={{0,128},{32,160},{64,192},{96,224},{128,0},{160,32},{192,64},{224,... | collective-permute-start | bytes 2359304 | tf_op jit(solution)/shard_map/ppermute | solution.py:176

commit v2 on v1

--- a/solution.py
+++ b/solution.py
@@ -8,14 +8,14 @@
 from jax.sharding import PartitionSpec as P
 
 ROWS = 8
+CHUNK = 32
 
 
 def scan_step(a, m, k, axis, reverse, last):
     n = a.shape[axis]
     index = lax.broadcasted_iota(jnp.int32, a.shape, axis)
     shift = n - k if reverse else k
-    source = pltpu.roll(index, shift, axis)
-    valid = source == (index + k if reverse else index - k)
+    valid = index < n - k if reverse else index >= k
     a_src = pltpu.roll(a, shift, axis)
     m_src = pltpu.roll(m, shift, axis)
     m = jnp.where(valid, jnp.minimum(m_src + a, m), m)
@@ -33,16 +33,15 @@
     return a, m
 
 
-def local_kernel(flags, fibre, tissue, seeded, line_add, line_min, cost_x, cost_y, field,
-                 *, grid_step):
+def local_kernel(flags, fibre, tissue, seeded, cost_x, field, cost_y, *, grid_step):
     planes, cells_y, cells_z = seeded.shape
-    blocks = cells_y // ROWS
+    chunks = cells_y // CHUNK
     inf = jnp.float32(jnp.inf)
 
     def costs_and_z(reverse):
         def body(i, carry):
-            p = i // blocks
-            rows = pl.ds(pl.multiple_of((i % blocks) * ROWS, ROWS), ROWS)
+            p = i // chunks
+            rows = pl.ds(pl.multiple_of((i % chunks) * CHUNK, CHUNK), CHUNK)
             xx = fibre[0, p, rows, :]
             yy = fibre[1, p, rows, :]
             zz = fibre[2, p, rows, :]
@@ -61,44 +60,25 @@
             field[p, rows, :] = u
             return carry
 
-        lax.fori_loop(0, planes * blocks, body, 0)
+        lax.fori_loop(0, planes * chunks, body, 0)
 
     def sweep_y(reverse):
         def body(j, carry):
-            i = blocks - 1 - j if reverse else j
-            rows = pl.ds(pl.multiple_of(i * ROWS, ROWS), ROWS)
+            i = chunks - 1 - j if reverse else j
+            rows = pl.ds(pl.multiple_of(i * CHUNK, CHUNK), CHUNK)
             out = []
             for p in range(planes):
                 a, m = block_scan(cost_y[p, rows, :], field[p, rows, :], 0, reverse, True)
                 u = jnp.minimum(carry[p] + a, m)
                 field[p, rows, :] = u
-                edge = u[0:1, :] if reverse else u[ROWS - 1:ROWS, :]
+                edge = u[0:1, :] if reverse else u[CHUNK - 1:CHUNK, :]
                 out.append(jnp.broadcast_to(edge, u.shape))
             return tuple(out)
 
-        start = tuple(jnp.full((ROWS, cells_z), inf, jnp.float32) for _ in range(planes))
-        lax.fori_loop(0, blocks, body, start)
+        start = tuple(jnp.full((CHUNK, cells_z), inf, jnp.float32) for _ in range(planes))
+        lax.fori_loop(0, chunks, body, start)
 
-    def sweep_x(reverse):
-        def body(i, carry):
-            rows = pl.ds(pl.multiple_of(i * ROWS, ROWS), ROWS)
-            order = range(planes - 1, -1, -1) if reverse else range(planes)
-            a = None
-            m = None
-            for p in order:
-                c = cost_x[p, rows, :]
-                u = field[p, rows, :]
-                if a is None:
-                    a, m = c, u
-                else:
-                    a, m = a + c, jnp.minimum(m + c, u)
-                line_add[p, rows, :] = a
-                line_min[p, rows, :] = m
-            return carry
-
-        lax.fori_loop(0, blocks, body, 0)
-
-    for flag, fn in ((flags[2], costs_and_z), (flags[1], sweep_y), (flags[0], sweep_x)):
+    for flag, fn in ((flags[2], costs_and_z), (flags[1], sweep_y)):
         pl.when(flag == 1)(functools.partial(fn, True))
         pl.when(flag != 1)(functools.partial(fn, False))
 
@@ -113,10 +93,10 @@
         out_shape=(plane, plane),
         in_specs=[pl.BlockSpec(memory_space=pltpu.SMEM), vmem, vmem, vmem],
         out_specs=(vmem, vmem),
-        scratch_shapes=[pltpu.VMEM(seeded.shape, jnp.float32) for _ in range(3)],
+        scratch_shapes=[pltpu.VMEM(seeded.shape, jnp.float32)],
         compiler_params=pltpu.CompilerParams(vmem_limit_bytes=48 * 1024 * 1024),
         cost_estimate=pl.CostEstimate(
-            flops=300 * elements, transcendentals=6 * elements, bytes_accessed=44 * elements
+            flops=300 * elements, transcendentals=6 * elements, bytes_accessed=40 * elements
         ),
     )(flags, fibre, tissue, seeded)
 
@@ -147,13 +127,33 @@
     seeded = previous.at[plane_index, row_index, column_index].min(stim_times, mode="drop")
 
     bits = jnp.stack([group_index % 2, group_index // 2 % 2, group_index // 4 % 2]).astype(jnp.int32)
-    line_add, line_min = local_sweeps(bits, fibre_tensor, tissue, seeded, grid_step)
+    cost_x, field = local_sweeps(bits, fibre_tensor, tissue, seeded, grid_step)
+
+    up_add = jnp.stack([cost_x[0], cost_x[0] + cost_x[1]])
+    up_min = jnp.stack([field[0], jnp.minimum(field[0] + cost_x[1], field[1])])
+    down_add = jnp.stack([cost_x[1] + cost_x[0], cost_x[1]])
+    down_min = jnp.stack([jnp.minimum(field[1] + cost_x[0], field[0]), field[1]])
 
     backward_x = group_index % 2 == 1
+    line_add = jnp.where(backward_x, down_add, up_add)
+    line_min = jnp.where(backward_x, down_min, up_min)
+
+    core = group_index % 2
+    own_plane = lax.dynamic_index_in_dim(field, core, 0, keepdims=False)
+    for mask in [m for m in (2, 4, 8, 16) if m < orders]:
+        got = lax.ppermute(own_plane, "order", [(g, g ^ mask) for g in range(orders)])
+        own_plane = jnp.minimum(own_plane, got)
+    other_plane = lax.ppermute(own_plane, "order", [(g, g ^ 1) for g in range(orders)])
+    least0 = jnp.where(core == 0, own_plane, other_plane)
+    least1 = jnp.where(core == 0, other_plane, own_plane)
+    least_local = jnp.stack([
+        jnp.minimum(least0, least1 + cost_x[0]),
+        jnp.minimum(least1, least0 + cost_x[1]),
+    ])
+
     rank = jnp.where(backward_x, slabs - 1 - slab_index, slab_index)
-    edge = jnp.where(backward_x, 0, planes - 1)
-    total_add = lax.dynamic_index_in_dim(line_add, edge, 0, keepdims=False)
-    total_min = lax.dynamic_index_in_dim(line_min, edge, 0, keepdims=False)
+    total_add = jnp.where(backward_x, line_add[0], line_add[planes - 1])
+    total_min = jnp.where(backward_x, line_min[0], line_min[planes - 1])
 
     distance = 1
     while distance < slabs:
@@ -170,12 +170,18 @@
     incoming = jnp.where(rank >= 1, got, jnp.inf)
 
     sweep_field = jnp.minimum(incoming[None] + line_add, line_min)
-    merged = sweep_field
-    mask = 1
-    while mask < orders:
-        got = lax.ppermute(merged, "order", [(g, g ^ mask) for g in range(orders)])
-        merged = jnp.minimum(merged, got)
-        mask *= 2
+
+    least_in = incoming
+    for mask in [m for m in (2, 4, 8, 16) if m < orders]:
+        got = lax.ppermute(least_in, "order", [(g, g ^ mask) for g in range(orders)])
+        least_in = jnp.minimum(least_in, got)
+    other_in = lax.ppermute(least_in, "order", [(g, g ^ 1) for g in range(orders)])
+    up_in = jnp.where(core == 0, least_in, other_in)
+    down_in = jnp.where(core == 0, other_in, least_in)
+    merged = jnp.minimum(
+        least_local,
+        jnp.minimum(up_in[None] + up_add, down_in[None] + down_add),
+    )
     return (merged, sweep_field[None])
 
 

time: 231 us -> 192 us (0.83)
  Pallas kernels: 53.6 us -> 16.8 us
  waiting for transfers between devices: 115 us -> 92.3 us
  other arithmetic: 13.9 us -> 24.8 us
  starting transfers between devices: 41.1 us -> 50.6 us
    pallas_call x1, Pallas kernels: 53.6 us -> 16.8 us  [local_sweeps(): pl.pallas_call(functools.partial(local_kernel, grid_step=grid_step), out_...]
    ppermute x3 -> x6, waiting for transfers between devices: 35.8 us -> 14 us  [the longest x2 7.17 us: shards(): lax.ppermute(own_plane, 'order', [(g, g ^ mask) for g in range(orders)])]
    ppermute x3 -> x6, starting transfers between devices: 10.6 us -> 20 us  [the longest x1 7.31 us: shards(): lax.ppermute(own_plane, 'order', [(g, g ^ 1) for g in range(orders)])]
    min x3 -> x5, other arithmetic: 1.18 us -> 4.12 us  [the longest x2 1.96 us: shards(): least_in = jnp.minimum(least_in, got)]
    another operation x0 -> x2, other arithmetic: none -> 2.43 us  [the longest x1 1.34 us: shards(): up_min = jnp.stack([field[0], jnp.minimum(field[0] + cost_x[1], field[1])])]
    min x1, other arithmetic: 0.13 us -> 2.44 us  [shards(): sweep_field = jnp.minimum(incoming[None] + line_add, line_min)]
  transfers between devices with their start and end apart: 9 -> 12, of which waited for: 9 -> 9; matrix products, arithmetic and copies ran while one was open for 0% -> 4% of each run, Pallas kernels for 0% -> 0%
where the time goes in v2:
time: 192 us; the launch traced here: 189 us
  waiting for transfers between devices  92.3 us (48%)
  starting transfers between devices  50.6 us (26%)
  other arithmetic  24.8 us (13%)
  Pallas kernels  16.8 us (9%)
  local copies, waits for them, and re-layouts  3.43 us (2%)
    ppermute x6, waiting for transfers between devices, shifted(): return lax.ppermute(value, ('order', 'slab'), route)  78.3 us
    ppermute x6, starting transfers between devices, shifted(): return lax.ppermute(value, ('order', 'slab'), route)  30.6 us
    pallas_call x1, Pallas kernels, local_sweeps(): pl.pallas_call(functools.partial(local_kernel, grid_step=grid_step), out_...  16.8 us
    ppermute x1, starting transfers between devices, shards(): lax.ppermute(own_plane, 'order', [(g, g ^ 1) for g in range(orders)])  7.31 us
    ppermute x2, waiting for transfers between devices, shards(): lax.ppermute(own_plane, 'order', [(g, g ^ mask) for g in range(orders)])  7.17 us
    ppermute x2, waiting for transfers between devices, shards(): lax.ppermute(least_in, 'order', [(g, g ^ mask) for g in range(orders)])  6.8 us
    another operation x4, other arithmetic, shards(): got = shifted(jnp.stack([total_add, total_min]), distance, orders, slabs)  4.84 us
    ppermute x2, starting transfers between devices, shards(): lax.ppermute(least_in, 'order', [(g, g ^ mask) for g in range(orders)])  4.49 us
  transfers between devices with their start and end apart: 12, of which 9 were waited for; matrix products, arithmetic and copies ran while one was open for 4% of the time, Pallas kernels for 0%

profile of v2, /device:TPU:103, one launch (start us, length us, event | category | flops | bytes accessed | tf_op | source)
XLA Modules:
  0.0 188.7 jit_solution(7006036261692802629)
XLA Ops:
  0.6 1.1 copy.9
  2.5 2.0 %scatter_fusion = f32[2,384,256]{2,1,0:T(8,128)S(1)} fusion(f32[2,384,256]{2,1,0:T(8,128)S(1)} %copy.9, s32[16]{0:T(128)S(1)} %fusion.14, f32[16]{0:T(128)} %param.9), kind=kCustom, calls=%fused_computation | custom fusion | flops 16 | bytes 384 | tf_op jit(solution)/shard_map/scatter-min | solution.py:127
  5.7 16.8 %shard_map.68 = (f32[2,384,256]{2,1,0:T(8,128)S(1)}, f32[2,384,256]{2,1,0:T(8,128)S(1)}) custom-call(s32[3]{0:T(128)S(1)} %pad_add_fusion.flags, f32[6,2,384,256]{3,2,1,0:T(8,128)} %fibre.1, s32[2,384,256]{2,1,0:T(8,128)S(1)} %copy-done, f32[2,384,256]{2,1,0:T(8,128)S(1)} %scatter_fusion), custom_call_target="tpu_custom_call" | custom-call | flops 58982400 | bytes 7864320 | tf_op jit(solution)/shard_map/pallas_call | solution.py:91
  22.5 1.3 slice_bitcast_fusion.2
  25.5 1.9 %collective-permute-start.3 = (f32[2,384,256]{2,1,0:T(8,128)}, f32[2,384,256]{2,1,0:T(8,128)S(1)}, u32[]{:S(2)}, u32[]{:S(2)}) collective-permute-start(f32[2,384,256]{2,1,0:T(8,128)} %pad_maximum_fusion.2), channel_id=1, source_target_pairs={{0,1},{1,2},{2,3},{3,4},{4,5},{5,6},{6,7},{7,8},{8,9},{9,10},{10,1... | collective-permute-start | bytes 2359304 | tf_op jit(solution)/shard_map/ppermute | solution.py:111
  27.4 12.4 %collective-permute-done.3 = f32[2,384,256]{2,1,0:T(8,128)S(1)} collective-permute-done((f32[2,384,256]{2,1,0:T(8,128)}, f32[2,384,256]{2,1,0:T(8,128)S(1)}, u32[]{:S(2)}, u32[]{:S(2)}) %collective-permute-start.3) | collective-permute-done | bytes 786464 | tf_op jit(solution)/shard_map/ppermute | solution.py:111
  41.6 1.9 %collective-permute-start.4 = (f32[2,384,256]{2,1,0:T(8,128)}, f32[2,384,256]{2,1,0:T(8,128)S(1)}, u32[]{:S(2)}, u32[]{:S(2)}) collective-permute-start(f32[2,384,256]{2,1,0:T(8,128)} %pad_maximum_fusion.3), channel_id=1, source_target_pairs={{0,2},{1,3},{2,4},{3,5},{4,6},{5,7},{6,8},{7,9},{8,10},{9,11},{10,... | collective-permute-start | bytes 2359304 | tf_op jit(solution)/shard_map/ppermute | solution.py:111
  43.5 21.5 %collective-permute-done.4 = f32[2,384,256]{2,1,0:T(8,128)S(1)} collective-permute-done((f32[2,384,256]{2,1,0:T(8,128)}, f32[2,384,256]{2,1,0:T(8,128)S(1)}, u32[]{:S(2)}, u32[]{:S(2)}) %collective-permute-start.4) | collective-permute-done | bytes 786464 | tf_op jit(solution)/shard_map/ppermute | solution.py:111
  65.1 2.2 %add_select_fusion.5 = (f32[1,384,256]{2,1,0:T(8,128)}, f32[1,384,256]{2,1,0:T(8,128)}) fusion(f32[1,384,256]{2,1,0:T(8,128)} %copy-done.2, f32[2,384,256]{2,1,0:T(8,128)S(1)} %collective-permute-done.4, pred[]{:T(512)S(6)} %ge.24, f32[1,384,256]{2,1,0:T(8,128)} %copy-done.3), kind=kLoop, calls=%fused_computation.26 | loop fusion | flops 491520 | bytes 2359297 | tf_op jit(solution)/shard_map/jit(_where)/select_n | solution.py:164
  67.3 2.0 %pad_maximum_fusion.4 = f32[2,384,256]{2,1,0:T(8,128)} fusion(f32[1,384,256]{2,1,0:T(8,128)} %get-tuple-element.13, f32[1,384,256]{2,1,0:T(8,128)} %get-tuple-element.12), kind=kLoop, calls=%fused_computation.7 | loop fusion | flops 196608 | bytes 1572864 | tf_op jit(solution)/shard_map/stack | solution.py:161
  69.3 6.2 %collective-permute-start.5 = (f32[2,384,256]{2,1,0:T(8,128)}, f32[2,384,256]{2,1,0:T(8,128)}, u32[]{:S(2)}, u32[]{:S(2)}) collective-permute-start(f32[2,384,256]{2,1,0:T(8,128)} %pad_maximum_fusion.4), channel_id=1, source_target_pairs={{0,4},{1,5},{2,6},{3,7},{4,8},{5,9},{6,10},{7,11},{8,12},{9,13},{1... | collective-permute-start | bytes 2359304 | tf_op jit(solution)/shard_map/ppermute | solution.py:111
  75.5 24.6 %collective-permute-done.5 = f32[2,384,256]{2,1,0:T(8,128)} collective-permute-done((f32[2,384,256]{2,1,0:T(8,128)}, f32[2,384,256]{2,1,0:T(8,128)}, u32[]{:S(2)}, u32[]{:S(2)}) %collective-permute-start.5) | collective-permute-done | bytes 786464 | tf_op jit(solution)/shard_map/ppermute | solution.py:111
  100.1 1.5 add_select_fusion.4
  102.5 14.4 %collective-permute-start.6 = (f32[2,384,256]{2,1,0:T(8,128)}, f32[2,384,256]{2,1,0:T(8,128)}, u32[]{:S(2)}, u32[]{:S(2)}) collective-permute-start(f32[2,384,256]{2,1,0:T(8,128)} %pad_maximum_fusion.5), channel_id=1, source_target_pairs={{0,8},{1,9},{2,10},{3,11},{4,12},{5,13},{6,14},{7,15},{8,16},{9,17... | collective-permute-start | bytes 2359304 | tf_op jit(solution)/shard_map/ppermute | solution.py:111
  116.9 8.3 %collective-permute-done.6 = f32[2,384,256]{2,1,0:T(8,128)} collective-permute-done((f32[2,384,256]{2,1,0:T(8,128)}, f32[2,384,256]{2,1,0:T(8,128)}, u32[]{:S(2)}, u32[]{:S(2)}) %collective-permute-start.6) | collective-permute-done | bytes 786464 | tf_op jit(solution)/shard_map/ppermute | solution.py:111
  125.2 2.5 %minimum_select_fusion.1 = f32[384,256]{1,0:T(8,128)} fusion(f32[2,384,256]{2,1,0:T(8,128)} %collective-permute-done.6, f32[2,384,256]{2,1,0:T(8,128)} %collective-permute-done.5, f32[2,384,256]{2,1,0:T(8,128)S(1)} %collective-permute-done.4, f32[2,384,256]{2,1,0:T(8,128)} %copy-done.1, pred[]{:T(512)S(6)} %ge.24, pred[]{:T(512)S(6)} %ge.23, pred[]{:T(512)S(6)} %ge.22, ...), kind=kLoop, calls=%fused_computation.16 | loop fusion | flops 1966080 | bytes 4718597 | tf_op jit(solution)/shard_map/jit(_where)/select_n | solution.py:163
  127.7 4.2 %collective-permute-start.7 = (f32[384,256]{1,0:T(8,128)}, f32[384,256]{1,0:T(8,128)S(1)}, u32[]{:S(2)}, u32[]{:S(2)}) collective-permute-start(f32[384,256]{1,0:T(8,128)} %minimum_select_fusion.1), channel_id=1, source_target_pairs={{0,16},{1,17},{2,18},{3,19},{4,20},{5,21},{6,22},{7,23},{8,24},{9,... | collective-permute-start | bytes 1179656 | tf_op jit(solution)/shard_map/ppermute | solution.py:111
  131.9 5.0 %collective-permute-done.7 = f32[384,256]{1,0:T(8,128)S(1)} collective-permute-done((f32[384,256]{1,0:T(8,128)}, f32[384,256]{1,0:T(8,128)S(1)}, u32[]{:S(2)}, u32[]{:S(2)}) %collective-permute-start.7) | collective-permute-done | bytes 393248 | tf_op jit(solution)/shard_map/ppermute | solution.py:111
  136.9 1.6 minimum_select_fusion
  138.4 2.1 %collective-permute-start.8 = (f32[384,256]{1,0:T(8,128)S(1)}, f32[384,256]{1,0:T(8,128)S(1)}, u32[]{:S(2)}, u32[]{:S(2)}) collective-permute-start(f32[384,256]{1,0:T(8,128)S(1)} %minimum_select_fusion), channel_id=1, source_target_pairs={{0,1},{1,2},{2,3},{3,4},{4,5},{5,6},{6,7},{7,8},{8,9},{9,10},{10,1... | collective-permute-start | bytes 1179656 | tf_op jit(solution)/shard_map/ppermute | solution.py:111
  140.5 1.4 collective-permute-start
  141.9 6.4 %collective-permute-done.8 = f32[384,256]{1,0:T(8,128)S(1)} collective-permute-done((f32[384,256]{1,0:T(8,128)S(1)}, f32[384,256]{1,0:T(8,128)S(1)}, u32[]{:S(2)}, u32[]{:S(2)}) %collective-permute-start.8) | collective-permute-done | bytes 393248 | tf_op jit(solution)/shard_map/ppermute | solution.py:111
  148.3 1.4 collective-permute-start.9
  150.8 2.9 %collective-permute-start.1 = (f32[384,256]{1,0:T(8,128)S(1)}, f32[384,256]{1,0:T(8,128)S(1)}, u32[]{:S(2)}, u32[]{:S(2)}) collective-permute-start(f32[384,256]{1,0:T(8,128)S(1)} %min.71), channel_id=1, source_target_pairs={{0,128},{32,160},{64,192},{96,224},{128,0},{160,32},{192,64},{224,... | collective-permute-start | bytes 1179656 | tf_op jit(solution)/shard_map/ppermute | solution.py:144
  153.7 5.7 %collective-permute-done.9 = f32[384,256]{1,0:T(8,128)S(1)} collective-permute-done((f32[384,256]{1,0:T(8,128)S(1)}, f32[384,256]{1,0:T(8,128)S(1)}, u32[]{:S(2)}, u32[]{:S(2)}) %collective-permute-start.9) | collective-permute-done | bytes 393248 | tf_op jit(solution)/shard_map/ppermute | solution.py:176
  160.1 3.1 %collective-permute-start.10 = (f32[384,256]{1,0:T(8,128)}, f32[384,256]{1,0:T(8,128)}, u32[]{:S(2)}, u32[]{:S(2)}) collective-permute-start(f32[384,256]{1,0:T(8,128)} %fusion.15), channel_id=1, source_target_pairs={{0,128},{32,160},{64,192},{96,224},{128,0},{160,32},{192,64},{224,... | collective-permute-start | bytes 1179656 | tf_op jit(solution)/shard_map/ppermute | solution.py:176
  163.2 7.2 %collective-permute-done.1 = f32[384,256]{1,0:T(8,128)S(1)} collective-permute-done((f32[384,256]{1,0:T(8,128)S(1)}, f32[384,256]{1,0:T(8,128)S(1)}, u32[]{:S(2)}, u32[]{:S(2)}) %collective-permute-start.1) | collective-permute-done | bytes 393248 | tf_op jit(solution)/shard_map/ppermute | solution.py:144
  170.5 7.3 %collective-permute-start.2 = (f32[384,256]{1,0:T(8,128)S(1)}, f32[384,256]{1,0:T(8,128)}, u32[]{:S(2)}, u32[]{:S(2)}) collective-permute-start(f32[384,256]{1,0:T(8,128)S(1)} %min.72), channel_id=1, source_target_pairs={{0,32},{32,0},{64,96},{96,64},{128,160},{160,128},{192,224},{224,1... | collective-permute-start | bytes 1179656 | tf_op jit(solution)/shard_map/ppermute | solution.py:146
  177.8 1.1 collective-permute-done.10
  178.9 1.2 min.86
  180.1 3.9 %collective-permute-start.11 = (f32[384,256]{1,0:T(8,128)S(1)}, f32[384,256]{1,0:T(8,128)S(1)}, u32[]{:S(2)}, u32[]{:S(2)}) collective-permute-start(f32[384,256]{1,0:T(8,128)S(1)} %min.86), channel_id=1, source_target_pairs={{0,32},{32,0},{64,96},{96,64},{128,160},{160,128},{192,224},{224,1... | collective-permute-start | bytes 1179656 | tf_op jit(solution)/shard_map/ppermute | solution.py:178
  185.1 2.4 %fusion.1 = f32[1,2,384,256]{3,2,1,0:T(8,128)} fusion(f32[1,1,384,256]{3,2,1,0:T(8,128)} %get-tuple-element.21, f32[1,1,384,256]{3,2,1,0:T(8,128)S(1)} %bitcast.109, f32[1,1,384,256]{3,2,1,0:T(8,128)} %get-tuple-element.20, f32[1,1,384,256]{3,2,1,0:T(8,128)} %get-tuple-element.17, f32[1,1,384,256]{3,2,1,0:T(8,128)S(1)} %bitcast.110, ...), kind=kLoop, calls=%fused_computation.11 | loop fusion | flops 1572864 | bytes 3932161 | tf_op jit(solution)/shard_map/min | solution.py:172
  (43 shorter events, 10.4 us)
Async XLA Ops:
  4.6 1.1 copy-start
  23.8 0.7 copy-start.4
  23.8 1.7 copy-start.6
  23.8 1.7 copy-start.8
  23.8 1.7 copy-start.10
  25.5 14.3 %collective-permute-start.3 = (f32[2,384,256]{2,1,0:T(8,128)}, f32[2,384,256]{2,1,0:T(8,128)S(1)}, u32[]{:S(2)}, u32[]{:S(2)}) collective-permute-start(f32[2,384,256]{2,1,0:T(8,128)} %pad_maximum_fusion.2), channel_id=1, source_target_pairs={{0,1},{1,2},{2,3},{3,4},{4,5},{5,6},{6,7},{7,8},{8,9},{9,10},{10,1... | collective-permute-start | bytes 2359304 | tf_op jit(solution)/shard_map/ppermute | solution.py:111
  39.8 0.9 copy-start.1
  40.0 1.7 copy-start.2
  40.0 1.6 copy-start.3
  41.6 23.5 %collective-permute-start.4 = (f32[2,384,256]{2,1,0:T(8,128)}, f32[2,384,256]{2,1,0:T(8,128)S(1)}, u32[]{:S(2)}, u32[]{:S(2)}) collective-permute-start(f32[2,384,256]{2,1,0:T(8,128)} %pad_maximum_fusion.3), channel_id=1, source_target_pairs={{0,2},{1,3},{2,4},{3,5},{4,6},{5,7},{6,8},{7,9},{8,10},{9,11},{10,... | collective-permute-start | bytes 2359304 | tf_op jit(solution)/shard_map/ppermute | solution.py:111
  69.3 30.8 %collective-permute-start.5 = (f32[2,384,256]{2,1,0:T(8,128)}, f32[2,384,256]{2,1,0:T(8,128)}, u32[]{:S(2)}, u32[]{:S(2)}) collective-permute-start(f32[2,384,256]{2,1,0:T(8,128)} %pad_maximum_fusion.4), channel_id=1, source_target_pairs={{0,4},{1,5},{2,6},{3,7},{4,8},{5,9},{6,10},{7,11},{8,12},{9,13},{1... | collective-permute-start | bytes 2359304 | tf_op jit(solution)/shard_map/ppermute | solution.py:111
  102.5 22.7 %collective-permute-start.6 = (f32[2,384,256]{2,1,0:T(8,128)}, f32[2,384,256]{2,1,0:T(8,128)}, u32[]{:S(2)}, u32[]{:S(2)}) collective-permute-start(f32[2,384,256]{2,1,0:T(8,128)} %pad_maximum_fusion.5), channel_id=1, source_target_pairs={{0,8},{1,9},{2,10},{3,11},{4,12},{5,13},{6,14},{7,15},{8,16},{9,17... | collective-permute-start | bytes 2359304 | tf_op jit(solution)/shard_map/ppermute | solution.py:111
  127.7 9.2 %collective-permute-start.7 = (f32[384,256]{1,0:T(8,128)}, f32[384,256]{1,0:T(8,128)S(1)}, u32[]{:S(2)}, u32[]{:S(2)}) collective-permute-start(f32[384,256]{1,0:T(8,128)} %minimum_select_fusion.1), channel_id=1, source_target_pairs={{0,16},{1,17},{2,18},{3,19},{4,20},{5,21},{6,22},{7,23},{8,24},{9,... | collective-permute-start | bytes 1179656 | tf_op jit(solution)/shard_map/ppermute | solution.py:111
  138.4 46.7 %copy-start.9 = (f32[1,384,256]{2,1,0:T(8,128)S(1)}, f32[1,384,256]{2,1,0:T(8,128)}, u32[]{:S(2)}) copy-start(f32[1,384,256]{2,1,0:T(8,128)} %copy-done.8) | copy-start | bytes 1179652
  138.4 46.7 %copy-start.11 = (f32[1,384,256]{2,1,0:T(8,128)S(1)}, f32[1,384,256]{2,1,0:T(8,128)}, u32[]{:S(2)}) copy-start(f32[1,384,256]{2,1,0:T(8,128)} %copy-done.10) | copy-start | bytes 1179652
  138.4 9.9 %collective-permute-start.8 = (f32[384,256]{1,0:T(8,128)S(1)}, f32[384,256]{1,0:T(8,128)S(1)}, u32[]{:S(2)}, u32[]{:S(2)}) collective-permute-start(f32[384,256]{1,0:T(8,128)S(1)} %minimum_select_fusion), channel_id=1, source_target_pairs={{0,1},{1,2},{2,3},{3,4},{4,5},{5,6},{6,7},{7,8},{8,9},{9,10},{10,1... | collective-permute-start | bytes 1179656 | tf_op jit(solution)/shard_map/ppermute | solution.py:111
  140.5 9.2 %collective-permute-start = (f32[384,256]{1,0:T(8,128)}, f32[384,256]{1,0:T(8,128)S(1)}, u32[]{:S(2)}, u32[]{:S(2)}) collective-permute-start(f32[384,256]{1,0:T(8,128)} %get-tuple-element.27), channel_id=1, source_target_pairs={{0,64},{32,96},{64,0},{96,32},{128,192},{160,224},{192,128},{224,1... | collective-permute-start | bytes 1179656 | tf_op jit(solution)/shard_map/ppermute | solution.py:144
  148.3 11.0 %collective-permute-start.9 = (f32[384,256]{1,0:T(8,128)S(1)}, f32[384,256]{1,0:T(8,128)S(1)}, u32[]{:S(2)}, u32[]{:S(2)}) collective-permute-start(f32[384,256]{1,0:T(8,128)S(1)} %broadcast_select_fusion), channel_id=1, source_target_pairs={{0,64},{32,96},{64,0},{96,32},{128,192},{160,224},{192,128},{224,1... | collective-permute-start | bytes 1179656 | tf_op jit(solution)/shard_map/ppermute | solution.py:176
  150.8 19.6 %collective-permute-start.1 = (f32[384,256]{1,0:T(8,128)S(1)}, f32[384,256]{1,0:T(8,128)S(1)}, u32[]{:S(2)}, u32[]{:S(2)}) collective-permute-start(f32[384,256]{1,0:T(8,128)S(1)} %min.71), channel_id=1, source_target_pairs={{0,128},{32,160},{64,192},{96,224},{128,0},{160,32},{192,64},{224,... | collective-permute-start | bytes 1179656 | tf_op jit(solution)/shard_map/ppermute | solution.py:144
  160.1 18.8 %collective-permute-start.10 = (f32[384,256]{1,0:T(8,128)}, f32[384,256]{1,0:T(8,128)}, u32[]{:S(2)}, u32[]{:S(2)}) collective-permute-start(f32[384,256]{1,0:T(8,128)} %fusion.15), channel_id=1, source_target_pairs={{0,128},{32,160},{64,192},{96,224},{128,0},{160,32},{192,64},{224,... | collective-permute-start | bytes 1179656 | tf_op jit(solution)/shard_map/ppermute | solution.py:176
  170.5 17.2 %copy-start.5 = (f32[1,384,256]{2,1,0:T(8,128)S(1)}, f32[1,384,256]{2,1,0:T(8,128)}, u32[]{:S(2)}) copy-start(f32[1,384,256]{2,1,0:T(8,128)} %copy-done.4) | copy-start | bytes 1179652
  170.5 17.2 %copy-start.7 = (f32[1,384,256]{2,1,0:T(8,128)S(1)}, f32[1,384,256]{2,1,0:T(8,128)}, u32[]{:S(2)}) copy-start(f32[1,384,256]{2,1,0:T(8,128)} %copy-done.6) | copy-start | bytes 1179652
  170.5 13.5 %collective-permute-start.2 = (f32[384,256]{1,0:T(8,128)S(1)}, f32[384,256]{1,0:T(8,128)}, u32[]{:S(2)}, u32[]{:S(2)}) collective-permute-start(f32[384,256]{1,0:T(8,128)S(1)} %min.72), channel_id=1, source_target_pairs={{0,32},{32,0},{64,96},{96,64},{128,160},{160,128},{192,224},{224,1... | collective-permute-start | bytes 1179656 | tf_op jit(solution)/shard_map/ppermute | solution.py:146
  180.1 7.5 %collective-permute-start.11 = (f32[384,256]{1,0:T(8,128)S(1)}, f32[384,256]{1,0:T(8,128)S(1)}, u32[]{:S(2)}, u32[]{:S(2)}) collective-permute-start(f32[384,256]{1,0:T(8,128)S(1)} %min.86), channel_id=1, source_target_pairs={{0,32},{32,0},{64,96},{96,64},{128,160},{160,128},{192,224},{224,1... | collective-permute-start | bytes 1179656 | tf_op jit(solution)/shard_map/ppermute | solution.py:178

commit v3 on v2

--- a/solution.py
+++ b/solution.py
@@ -101,14 +101,98 @@
     )(flags, fibre, tissue, seeded)
 
 
-def shifted(value, distance, orders, slabs):
-    route = []
-    for g in range(orders):
-        for s in range(slabs):
-            t = s + distance if g % 2 == 0 else s - distance
-            if 0 <= t < slabs:
-                route.append((g * slabs + s, g * slabs + t))
-    return lax.ppermute(value, ("order", "slab"), route)
+RELAY_ROWS = 16
+
+
+def relay_kernel(total_add, total_min, incoming, inbox, outbox, send_sems, recv_sems):
+    cells_y, cells_z = incoming.shape
+    chunks = cells_y // RELAY_ROWS
+    slabs = lax.axis_size("slab")
+    slab = lax.axis_index("slab")
+    group = lax.axis_index("order")
+    step = 1 - 2 * (group % 2)
+    rank = jnp.where(group % 2 == 1, slabs - 1 - slab, slab)
+    has_prev = rank > 0
+    has_next = rank < slabs - 1
+    prev_slab = slab - step
+    next_slab = slab + step
+
+    barrier = pltpu.get_barrier_semaphore()
+
+    @pl.when(has_prev)
+    def _():
+        pl.semaphore_signal(barrier, 1, device_id=(group, prev_slab), device_id_type=pl.DeviceIdType.MESH)
+
+    @pl.when(has_next)
+    def _():
+        pl.semaphore_signal(barrier, 1, device_id=(group, next_slab), device_id_type=pl.DeviceIdType.MESH)
+
+    @pl.when(has_prev & has_next)
+    def _():
+        pl.semaphore_wait(barrier, 2)
+
+    @pl.when(has_prev != has_next)
+    def _():
+        pl.semaphore_wait(barrier, 1)
+
+    def send(c):
+        return pltpu.make_async_remote_copy(
+            src_ref=outbox.at[c],
+            dst_ref=inbox.at[c],
+            send_sem=send_sems.at[c],
+            recv_sem=recv_sems.at[c],
+            device_id=(group, next_slab),
+            device_id_type=pl.DeviceIdType.MESH,
+        )
+
+    def body(c, carry):
+        rows = pl.ds(pl.multiple_of(c * RELAY_ROWS, RELAY_ROWS), RELAY_ROWS)
+
+        @pl.when(has_prev)
+        def _():
+            send(c).wait_recv()
+            incoming[rows, :] = inbox[c]
+
+        @pl.when(jnp.logical_not(has_prev))
+        def _():
+            incoming[rows, :] = jnp.full((RELAY_ROWS, cells_z), jnp.inf, jnp.float32)
+
+        @pl.when(has_next)
+        def _():
+            outbox[c] = jnp.minimum(incoming[rows, :] + total_add[rows, :], total_min[rows, :])
+            send(c).start()
+
+        return carry
+
+    lax.fori_loop(0, chunks, body, 0)
+
+    def drain(c, carry):
+        @pl.when(has_next)
+        def _():
+            send(c).wait_send()
+
+        return carry
+
+    lax.fori_loop(0, chunks, drain, 0)
+
+
+def relay(total_add, total_min):
+    cells_y, cells_z = total_add.shape
+    chunks = cells_y // RELAY_ROWS
+    vmem = pl.BlockSpec(memory_space=pltpu.VMEM)
+    return pl.pallas_call(
+        relay_kernel,
+        out_shape=jax.ShapeDtypeStruct(total_add.shape, jnp.float32),
+        in_specs=[vmem, vmem],
+        out_specs=vmem,
+        scratch_shapes=[
+            pltpu.VMEM((chunks, RELAY_ROWS, cells_z), jnp.float32),
+            pltpu.VMEM((chunks, RELAY_ROWS, cells_z), jnp.float32),
+            pltpu.SemaphoreType.DMA((chunks,)),
+            pltpu.SemaphoreType.DMA((chunks,)),
+        ],
+        compiler_params=pltpu.CompilerParams(collective_id=0, has_side_effects=True),
+    )(total_add, total_min)
 
 
 def shards(previous, fibre_tensor, tissue, stim_sites, stim_times):
@@ -151,23 +235,10 @@
         jnp.minimum(least1, least0 + cost_x[1]),
     ])
 
-    rank = jnp.where(backward_x, slabs - 1 - slab_index, slab_index)
     total_add = jnp.where(backward_x, line_add[0], line_add[planes - 1])
     total_min = jnp.where(backward_x, line_min[0], line_min[planes - 1])
 
-    distance = 1
-    while distance < slabs:
-        if 2 * distance < slabs:
-            got = shifted(jnp.stack([total_add, total_min]), distance, orders, slabs)
-            take = rank >= distance
-            total_min = jnp.where(take, jnp.minimum(got[1] + total_add, total_min), total_min)
-            total_add = jnp.where(take, got[0] + total_add, total_add)
-        else:
-            got = shifted(total_min, distance, orders, slabs)
-            total_min = jnp.where(rank >= distance, jnp.minimum(got + total_add, total_min), total_min)
-        distance *= 2
-    got = shifted(total_min, 1, orders, slabs)
-    incoming = jnp.where(rank >= 1, got, jnp.inf)
+    incoming = relay(total_add, total_min)
 
     sweep_field = jnp.minimum(incoming[None] + line_add, line_min)
 

time: 192 us -> 148 us (0.77)
  the two profiles are of different devices: /device:TPU:103 before, /device:TPU:231 now
where the time goes in v3:
time: 148 us; the launch traced here: 147 us
  starting transfers between devices  99.6 us (67%)
  Pallas kernels  24.5 us (17%)
  other arithmetic  15.6 us (11%)
  waiting for transfers between devices  4.38 us (3%)
  local copies, waits for them, and re-layouts  2.27 us (2%)
    ppermute x1, starting transfers between devices, shards(): lax.ppermute(own_plane, 'order', [(g, g ^ 1) for g in range(orders)])  87.7 us
    pallas_call x1, Pallas kernels, local_sweeps(): pl.pallas_call(functools.partial(local_kernel, grid_step=grid_step), out_...  16.7 us
    pallas_call x1, Pallas kernels, relay(): pl.pallas_call(relay_kernel, out_shape=jax.ShapeDtypeStruct(total_add.sha...  7.79 us
    ppermute x2, starting transfers between devices, shards(): lax.ppermute(own_plane, 'order', [(g, g ^ mask) for g in range(orders)])  4.51 us
    ppermute x1, starting transfers between devices, shards(): lax.ppermute(least_in, 'order', [(g, g ^ 1) for g in range(orders)])  4.26 us
    ppermute x2, starting transfers between devices, shards(): lax.ppermute(least_in, 'order', [(g, g ^ mask) for g in range(orders)])  3.15 us
  transfers between devices with their start and end apart: 6, of which 2 were waited for; matrix products, arithmetic and copies ran while one was open for 6% of the time, Pallas kernels for 5%

profile of v3, /device:TPU:231, one launch (start us, length us, event | category | flops | bytes accessed | tf_op | source)
XLA Modules:
  0.0 147.1 jit_solution(10151902325857557621)
XLA Ops:
  0.6 1.1 copy.9
  1.8 0.7 fusion.14
  2.4 0.1 pad_add_fusion.flags
  2.5 2.0 %scatter_fusion = f32[2,384,256]{2,1,0:T(8,128)S(1)} fusion(f32[2,384,256]{2,1,0:T(8,128)S(1)} %copy.9, s32[16]{0:T(128)S(1)} %fusion.14, f32[16]{0:T(128)} %param.9), kind=kCustom, calls=%fused_computation | custom fusion | flops 16 | bytes 384 | tf_op jit(solution)/shard_map/scatter-min | solution.py:211
  4.5 0.0 copy-start
  4.6 1.1 copy-done
  5.7 16.7 %shard_map.68 = (f32[2,384,256]{2,1,0:T(8,128)S(1)}, f32[2,384,256]{2,1,0:T(8,128)S(1)}) custom-call(s32[3]{0:T(128)S(1)} %pad_add_fusion.flags, f32[6,2,384,256]{3,2,1,0:T(8,128)} %fibre.1, s32[2,384,256]{2,1,0:T(8,128)S(1)} %copy-done, f32[2,384,256]{2,1,0:T(8,128)S(1)} %scatter_fusion), custom_call_target="tpu_custom_call" | custom-call | flops 58982400 | bytes 7864320 | tf_op jit(solution)/shard_map/pallas_call | solution.py:91
  22.4 1.3 slice_bitcast_fusion
  23.8 1.3 collective-permute-start
  25.1 1.2 maximum_select_fusion
  26.3 0.8 fusion.3.total_min
  27.1 0.8 fusion.4.total_add
  27.9 7.8 %shard_map.69 = f32[384,256]{1,0:T(8,128)} custom-call(f32[384,256]{1,0:T(8,128)} %fusion.4.total_add, f32[384,256]{1,0:T(8,128)} %fusion.3.total_min), custom_call_target="tpu_custom_call" | custom-call | tf_op jit(solution)/shard_map/pallas_call | solution.py:183
  35.7 0.2 collective-permute-start.3
  35.9 0.0 collective-permute-done
  35.9 1.2 min.44
  37.1 3.2 %collective-permute-start.1 = (f32[384,256]{1,0:T(8,128)S(1)}, f32[384,256]{1,0:T(8,128)S(1)}, u32[]{:S(2)}, u32[]{:S(2)}) collective-permute-start(f32[384,256]{1,0:T(8,128)S(1)} %min.44), channel_id=1, source_target_pairs={{0,128},{32,160},{64,192},{96,224},{128,0},{160,32},{192,64},{224,... | collective-permute-start | bytes 1179656 | tf_op jit(solution)/shard_map/ppermute | solution.py:228
  40.3 2.3 %collective-permute-done.3 = f32[384,256]{1,0:T(8,128)S(1)} collective-permute-done((f32[384,256]{1,0:T(8,128)}, f32[384,256]{1,0:T(8,128)S(1)}, u32[]{:S(2)}, u32[]{:S(2)}) %collective-permute-start.3) | collective-permute-done | bytes 393248 | tf_op jit(solution)/shard_map/ppermute | solution.py:247
  42.6 1.0 min.50
  43.6 2.9 %collective-permute-start.4 = (f32[384,256]{1,0:T(8,128)S(1)}, f32[384,256]{1,0:T(8,128)S(1)}, u32[]{:S(2)}, u32[]{:S(2)}) collective-permute-start(f32[384,256]{1,0:T(8,128)S(1)} %min.50), channel_id=1, source_target_pairs={{0,128},{32,160},{64,192},{96,224},{128,0},{160,32},{192,64},{224,... | collective-permute-start | bytes 1179656 | tf_op jit(solution)/shard_map/ppermute | solution.py:247
  46.6 2.1 %collective-permute-done.1 = f32[384,256]{1,0:T(8,128)S(1)} collective-permute-done((f32[384,256]{1,0:T(8,128)S(1)}, f32[384,256]{1,0:T(8,128)S(1)}, u32[]{:S(2)}, u32[]{:S(2)}) %collective-permute-start.1) | collective-permute-done | bytes 393248 | tf_op jit(solution)/shard_map/ppermute | solution.py:228
  48.6 0.1 min.45
  48.7 87.7 %collective-permute-start.2 = (f32[384,256]{1,0:T(8,128)S(1)}, f32[384,256]{1,0:T(8,128)}, u32[]{:S(2)}, u32[]{:S(2)}) collective-permute-start(f32[384,256]{1,0:T(8,128)S(1)} %min.45), channel_id=1, source_target_pairs={{0,32},{32,0},{64,96},{96,64},{128,160},{160,128},{192,224},{224,1... | collective-permute-start | bytes 1179656 | tf_op jit(solution)/shard_map/ppermute | solution.py:230
  136.4 0.0 collective-permute-done.4
  136.4 0.8 min.51
  137.2 4.3 %collective-permute-start.5 = (f32[384,256]{1,0:T(8,128)}, f32[384,256]{1,0:T(8,128)}, u32[]{:S(2)}, u32[]{:S(2)}) collective-permute-start(f32[384,256]{1,0:T(8,128)} %min.51), channel_id=1, source_target_pairs={{0,32},{32,0},{64,96},{96,64},{128,160},{160,128},{192,224},{224,1... | collective-permute-start | bytes 1179656 | tf_op jit(solution)/shard_map/ppermute | solution.py:249
  141.5 2.3 %fusion.1 = f32[1,2,384,256]{3,2,1,0:T(8,128)} fusion(f32[1,1,384,256]{3,2,1,0:T(8,128)} %get-tuple-element.15, f32[1,1,384,256]{3,2,1,0:T(8,128)S(1)} %bitcast.56, f32[1,1,384,256]{3,2,1,0:T(8,128)} %get-tuple-element.14, f32[1,1,384,256]{3,2,1,0:T(8,128)} %get-tuple-element.11, f32[1,1,384,256]{3,2,1,0:T(8,128)S(1)} %bitcast.57, ...), kind=kLoop, calls=%fused_computation.7 | loop fusion | flops 1572864 | bytes 3932161 | tf_op jit(solution)/shard_map/min | solution.py:243
  143.8 0.0 collective-permute-done.2
  143.8 1.1 fusion.8
  144.9 0.0 collective-permute-done.5
  144.9 1.2 broadcast_select_fusion.1
  146.1 1.1 maximum_minimum_fusion
  (2 shorter events, 0.0 us)
Async XLA Ops:
  4.5 1.1 copy-start
  23.8 12.1 %collective-permute-start = (f32[384,256]{1,0:T(8,128)}, f32[384,256]{1,0:T(8,128)}, u32[]{:S(2)}, u32[]{:S(2)}) collective-permute-start(f32[384,256]{1,0:T(8,128)} %get-tuple-element.21), channel_id=1, source_target_pairs={{0,64},{32,96},{64,0},{96,32},{128,192},{160,224},{192,128},{224,1... | collective-permute-start | bytes 1179656 | tf_op jit(solution)/shard_map/ppermute | solution.py:228
  35.7 105.8 %copy-start.1 = (f32[384,256]{1,0:T(8,128)S(1)}, f32[384,256]{1,0:T(8,128)}, u32[]{:S(2)}) copy-start(f32[384,256]{1,0:T(8,128)} %shard_map.69) | copy-start | bytes 1179652
  35.7 6.9 %collective-permute-start.3 = (f32[384,256]{1,0:T(8,128)}, f32[384,256]{1,0:T(8,128)S(1)}, u32[]{:S(2)}, u32[]{:S(2)}) collective-permute-start(f32[384,256]{1,0:T(8,128)} %shard_map.69), channel_id=1, source_target_pairs={{0,64},{32,96},{64,0},{96,32},{128,192},{160,224},{192,128},{224,1... | collective-permute-start | bytes 1179656 | tf_op jit(solution)/shard_map/ppermute | solution.py:247
  37.1 11.5 %collective-permute-start.1 = (f32[384,256]{1,0:T(8,128)S(1)}, f32[384,256]{1,0:T(8,128)S(1)}, u32[]{:S(2)}, u32[]{:S(2)}) collective-permute-start(f32[384,256]{1,0:T(8,128)S(1)} %min.44), channel_id=1, source_target_pairs={{0,128},{32,160},{64,192},{96,224},{128,0},{160,32},{192,64},{224,... | collective-permute-start | bytes 1179656 | tf_op jit(solution)/shard_map/ppermute | solution.py:228
  43.6 92.8 %collective-permute-start.4 = (f32[384,256]{1,0:T(8,128)S(1)}, f32[384,256]{1,0:T(8,128)S(1)}, u32[]{:S(2)}, u32[]{:S(2)}) collective-permute-start(f32[384,256]{1,0:T(8,128)S(1)} %min.50), channel_id=1, source_target_pairs={{0,128},{32,160},{64,192},{96,224},{128,0},{160,32},{192,64},{224,... | collective-permute-start | bytes 1179656 | tf_op jit(solution)/shard_map/ppermute | solution.py:247
  48.7 95.1 %collective-permute-start.2 = (f32[384,256]{1,0:T(8,128)S(1)}, f32[384,256]{1,0:T(8,128)}, u32[]{:S(2)}, u32[]{:S(2)}) collective-permute-start(f32[384,256]{1,0:T(8,128)S(1)} %min.45), channel_id=1, source_target_pairs={{0,32},{32,0},{64,96},{96,64},{128,160},{160,128},{192,224},{224,1... | collective-permute-start | bytes 1179656 | tf_op jit(solution)/shard_map/ppermute | solution.py:230
  137.2 7.7 %collective-permute-start.5 = (f32[384,256]{1,0:T(8,128)}, f32[384,256]{1,0:T(8,128)}, u32[]{:S(2)}, u32[]{:S(2)}) collective-permute-start(f32[384,256]{1,0:T(8,128)} %min.51), channel_id=1, source_target_pairs={{0,32},{32,0},{64,96},{96,64},{128,160},{160,128},{192,224},{224,1... | collective-permute-start | bytes 1179656 | tf_op jit(solution)/shard_map/ppermute | solution.py:249

commit v4 on v3

--- a/solution.py
+++ b/solution.py
@@ -102,93 +102,226 @@
 
 
 RELAY_ROWS = 16
-
-
-def relay_kernel(total_add, total_min, incoming, inbox, outbox, send_sems, recv_sems):
+LINE = 8
+
+
+def relay_kernel(total_add, total_min, incoming, before, line_total, box1_in, box1_out, box2_in,
+                 box2_out, box3_in, send1, recv1, send2, recv2, send3, recv3, *, line):
     cells_y, cells_z = incoming.shape
     chunks = cells_y // RELAY_ROWS
     slabs = lax.axis_size("slab")
+    lines = slabs // line
+    half = line // 2
     slab = lax.axis_index("slab")
     group = lax.axis_index("order")
-    step = 1 - 2 * (group % 2)
-    rank = jnp.where(group % 2 == 1, slabs - 1 - slab, slab)
-    has_prev = rank > 0
-    has_next = rank < slabs - 1
-    prev_slab = slab - step
-    next_slab = slab + step
+    odd = group % 2
+    rank = slab + odd * (slabs - 1 - 2 * slab)
+    col = rank // line
+    pos = rank % line
+    last = line - 1
+    mesh_id = pl.DeviceIdType.MESH
+
+    def device(r):
+        return (group, r + odd * (slabs - 1 - 2 * r))
+
+    def at(c, p):
+        return device(c * line + p)
+
+    first_col = col == 0
+    is_end = pos == last
+    in_up = pos < half
+    in_down = (pos >= half) & (pos < last)
+    up_next = pos + 1 < half
+    down_next = pos > half
 
     barrier = pltpu.get_barrier_semaphore()
-
-    @pl.when(has_prev)
-    def _():
-        pl.semaphore_signal(barrier, 1, device_id=(group, prev_slab), device_id_type=pl.DeviceIdType.MESH)
-
-    @pl.when(has_next)
-    def _():
-        pl.semaphore_signal(barrier, 1, device_id=(group, next_slab), device_id_type=pl.DeviceIdType.MESH)
-
-    @pl.when(has_prev & has_next)
-    def _():
-        pl.semaphore_wait(barrier, 2)
-
-    @pl.when(has_prev != has_next)
-    def _():
-        pl.semaphore_wait(barrier, 1)
-
-    def send(c):
-        return pltpu.make_async_remote_copy(
-            src_ref=outbox.at[c],
-            dst_ref=inbox.at[c],
-            send_sem=send_sems.at[c],
-            recv_sem=recv_sems.at[c],
-            device_id=(group, next_slab),
-            device_id_type=pl.DeviceIdType.MESH,
-        )
-
-    def body(c, carry):
-        rows = pl.ds(pl.multiple_of(c * RELAY_ROWS, RELAY_ROWS), RELAY_ROWS)
-
-        @pl.when(has_prev)
-        def _():
-            send(c).wait_recv()
-            incoming[rows, :] = inbox[c]
-
-        @pl.when(jnp.logical_not(has_prev))
-        def _():
-            incoming[rows, :] = jnp.full((RELAY_ROWS, cells_z), jnp.inf, jnp.float32)
-
-        @pl.when(has_next)
-        def _():
-            outbox[c] = jnp.minimum(incoming[rows, :] + total_add[rows, :], total_min[rows, :])
-            send(c).start()
+    neighbours = []
+    neighbours.append((pos > 0, at(col, pos - 1)))
+    neighbours.append((pos < last, at(col, pos + 1)))
+    neighbours.append(((pos == 0) & (col > 0) & (last > 0), at(col, last)))
+    neighbours.append((is_end & (col > 0) & (last > 0), at(col, 0)))
+    neighbours.append((is_end & (col > 0), at(col - 1, last)))
+    neighbours.append((is_end & (col < lines - 1), at(col + 1, last)))
+    count = jnp.int32(0)
+    for cond, dev in neighbours:
+        @pl.when(cond)
+        def _():
+            pl.semaphore_signal(barrier, 1, device_id=dev, device_id_type=mesh_id)
+
+        count = count + cond.astype(jnp.int32)
+    pl.semaphore_wait(barrier, count)
+
+    def copy1(c):
+        return pltpu.make_async_remote_copy(box1_out.at[c], box1_in.at[c], send1.at[c], recv1.at[c],
+                                            device_id=at(col, pos + 1), device_id_type=mesh_id)
+
+    def copy2(c):
+        return pltpu.make_async_remote_copy(box2_out.at[c], box2_in.at[c], send2.at[c], recv2.at[c],
+                                            device_id=at(col + 1, last), device_id_type=mesh_id)
+
+    def copy3_from_end(c, k, target):
+        return pltpu.make_async_remote_copy(box2_in.at[c], box3_in.at[c], send3.at[c, k], recv3.at[c],
+                                            device_id=target, device_id_type=mesh_id)
+
+    def copy3_relay(c, target):
+        return pltpu.make_async_remote_copy(box3_in.at[c], box3_in.at[c], send3.at[c, 0], recv3.at[c],
+                                            device_id=target, device_id_type=mesh_id)
+
+    def rows_of(c):
+        return pl.ds(pl.multiple_of(c * RELAY_ROWS, RELAY_ROWS), RELAY_ROWS)
+
+    def stage1(c, carry):
+        rows = rows_of(c)
+        own_add = total_add[rows, :]
+        own_min = total_min[rows, :]
+
+        @pl.when(pos == 0)
+        def _():
+            box1_out[c, 0] = own_add
+            box1_out[c, 1] = own_min
+
+        @pl.when(pos > 0)
+        def _():
+            copy1(c).wait_recv()
+            got_add = box1_in[c, 0]
+            got_min = box1_in[c, 1]
+            before[0, rows, :] = got_add
+            before[1, rows, :] = got_min
+            new_add = got_add + own_add
+            new_min = jnp.minimum(got_min + own_add, own_min)
+
+            @pl.when(pos < last)
+            def _():
+                box1_out[c, 0] = new_add
+                box1_out[c, 1] = new_min
+
+            @pl.when(is_end)
+            def _():
+                line_total[0, rows, :] = new_add
+                line_total[1, rows, :] = new_min
+
+        @pl.when((pos == 0) & is_end)
+        def _():
+            line_total[0, rows, :] = own_add
+            line_total[1, rows, :] = own_min
+
+        @pl.when(pos < last)
+        def _():
+            copy1(c).start()
 
         return carry
 
-    lax.fori_loop(0, chunks, body, 0)
+    lax.fori_loop(0, chunks, stage1, 0)
+
+    def stage2(c, carry):
+        rows = rows_of(c)
+
+        @pl.when(is_end & first_col)
+        def _():
+            incoming[rows, :] = jnp.where(pos > 0, before[1, rows, :], jnp.inf)
+            box2_out[c] = line_total[1, rows, :]
+
+        @pl.when(is_end & jnp.logical_not(first_col))
+        def _():
+            copy2(c).wait_recv()
+            value = box2_in[c]
+            incoming[rows, :] = jnp.where(
+                pos > 0, jnp.minimum(value + before[0, rows, :], before[1, rows, :]), value)
+            box2_out[c] = jnp.minimum(value + line_total[0, rows, :], line_total[1, rows, :])
+
+            @pl.when(pos > 0)
+            def _():
+                copy3_from_end(c, 0, at(col, 0)).start()
+
+            @pl.when(half < last)
+            def _():
+                copy3_from_end(c, 1, at(col, last - 1)).start()
+
+        @pl.when(is_end & (col < lines - 1))
+        def _():
+            copy2(c).start()
+
+        return carry
+
+    lax.fori_loop(0, chunks, stage2, 0)
+
+    def stage3(c, carry):
+        rows = rows_of(c)
+
+        @pl.when(first_col & jnp.logical_not(is_end))
+        def _():
+            incoming[rows, :] = jnp.where(pos > 0, before[1, rows, :], jnp.inf)
+
+        @pl.when(jnp.logical_not(first_col) & (in_up | in_down))
+        def _():
+            copy3_relay(c, at(col, 0)).wait_recv()
+            value = box3_in[c]
+            incoming[rows, :] = jnp.where(
+                pos > 0, jnp.minimum(value + before[0, rows, :], before[1, rows, :]), value)
+
+            @pl.when(in_up & up_next)
+            def _():
+                copy3_relay(c, at(col, pos + 1)).start()
+
+            @pl.when(in_down & down_next)
+            def _():
+                copy3_relay(c, at(col, pos - 1)).start()
+
+        return carry
+
+    lax.fori_loop(0, chunks, stage3, 0)
 
     def drain(c, carry):
-        @pl.when(has_next)
-        def _():
-            send(c).wait_send()
+        @pl.when(pos < last)
+        def _():
+            copy1(c).wait_send()
+
+        @pl.when(is_end & (col < lines - 1))
+        def _():
+            copy2(c).wait_send()
+
+        @pl.when(is_end & jnp.logical_not(first_col) & (pos > 0))
+        def _():
+            copy3_from_end(c, 0, at(col, 0)).wait_send()
+
+        @pl.when(is_end & jnp.logical_not(first_col) & (half < last))
+        def _():
+            copy3_from_end(c, 1, at(col, last - 1)).wait_send()
+
+        @pl.when(jnp.logical_not(first_col) & ((in_up & up_next) | (in_down & down_next)))
+        def _():
+            copy3_relay(c, at(col, 0)).wait_send()
 
         return carry
 
     lax.fori_loop(0, chunks, drain, 0)
 
 
-def relay(total_add, total_min):
+def relay(total_add, total_min, slabs):
     cells_y, cells_z = total_add.shape
     chunks = cells_y // RELAY_ROWS
+    line = LINE if slabs % LINE == 0 else slabs
     vmem = pl.BlockSpec(memory_space=pltpu.VMEM)
+    box = pltpu.VMEM((chunks, RELAY_ROWS, cells_z), jnp.float32)
+    pair_box = pltpu.VMEM((chunks, 2, RELAY_ROWS, cells_z), jnp.float32)
     return pl.pallas_call(
-        relay_kernel,
+        functools.partial(relay_kernel, line=line),
         out_shape=jax.ShapeDtypeStruct(total_add.shape, jnp.float32),
         in_specs=[vmem, vmem],
         out_specs=vmem,
         scratch_shapes=[
-            pltpu.VMEM((chunks, RELAY_ROWS, cells_z), jnp.float32),
-            pltpu.VMEM((chunks, RELAY_ROWS, cells_z), jnp.float32),
+            pltpu.VMEM((2, cells_y, cells_z), jnp.float32),
+            pltpu.VMEM((2, cells_y, cells_z), jnp.float32),
+            pair_box,
+            pair_box,
+            box,
+            box,
+            box,
             pltpu.SemaphoreType.DMA((chunks,)),
+            pltpu.SemaphoreType.DMA((chunks,)),
+            pltpu.SemaphoreType.DMA((chunks,)),
+            pltpu.SemaphoreType.DMA((chunks,)),
+            pltpu.SemaphoreType.DMA((chunks, 2)),
             pltpu.SemaphoreType.DMA((chunks,)),
         ],
         compiler_params=pltpu.CompilerParams(collective_id=0, has_side_effects=True),
@@ -238,7 +371,7 @@
     total_add = jnp.where(backward_x, line_add[0], line_add[planes - 1])
     total_min = jnp.where(backward_x, line_min[0], line_min[planes - 1])
 
-    incoming = relay(total_add, total_min)
+    incoming = relay(total_add, total_min, slabs)
 
     sweep_field = jnp.minimum(incoming[None] + line_add, line_min)
 

time: 148 us -> 115 us (0.78)
  the two profiles are of different devices: /device:TPU:231 before, /device:TPU:131 now
where the time goes in v4:
time: 115 us; the launch traced here: 114 us
  Pallas kernels  66.4 us (58%)
  starting transfers between devices  16 us (14%)
  other arithmetic  15.6 us (14%)
  waiting for transfers between devices  13.6 us (12%)
  local copies, waits for them, and re-layouts  2.27 us (2%)
    pallas_call x1, Pallas kernels, relay(): pl.pallas_call(functools.partial(relay_kernel, line=line), out_shape=jax....  49.7 us
    pallas_call x1, Pallas kernels, local_sweeps(): pl.pallas_call(functools.partial(local_kernel, grid_step=grid_step), out_...  16.7 us
    ppermute x2, waiting for transfers between devices, shards(): lax.ppermute(least_in, 'order', [(g, g ^ mask) for g in range(orders)])  7.29 us
    ppermute x2, waiting for transfers between devices, shards(): lax.ppermute(own_plane, 'order', [(g, g ^ mask) for g in range(orders)])  6.28 us
    ppermute x1, starting transfers between devices, shards(): lax.ppermute(own_plane, 'order', [(g, g ^ 1) for g in range(orders)])  5.43 us
    ppermute x2, starting transfers between devices, shards(): lax.ppermute(own_plane, 'order', [(g, g ^ mask) for g in range(orders)])  4.51 us
    ppermute x2, starting transfers between devices, shards(): lax.ppermute(least_in, 'order', [(g, g ^ mask) for g in range(orders)])  3.15 us
    ppermute x1, starting transfers between devices, shards(): lax.ppermute(least_in, 'order', [(g, g ^ 1) for g in range(orders)])  2.87 us
  transfers between devices with their start and end apart: 6, of which 3 were waited for; matrix products, arithmetic and copies ran while one was open for 8% of the time, Pallas kernels for 43%

profile of v4, /device:TPU:131, one launch (start us, length us, event | category | flops | bytes accessed | tf_op | source)
XLA Modules:
  0.0 114.5 jit_solution(11140076947512053081)
XLA Ops:
  0.6 1.1 copy.9
  1.8 0.7 fusion.14
  2.4 0.1 pad_add_fusion.flags
  2.5 2.0 %scatter_fusion = f32[2,384,256]{2,1,0:T(8,128)S(1)} fusion(f32[2,384,256]{2,1,0:T(8,128)S(1)} %copy.9, s32[16]{0:T(128)S(1)} %fusion.14, f32[16]{0:T(128)} %param.9), kind=kCustom, calls=%fused_computation | custom fusion | flops 16 | bytes 384 | tf_op jit(solution)/shard_map/scatter-min | solution.py:344
  4.6 0.0 copy-start
  4.6 1.1 copy-done
  5.7 16.7 %shard_map.68 = (f32[2,384,256]{2,1,0:T(8,128)S(1)}, f32[2,384,256]{2,1,0:T(8,128)S(1)}) custom-call(s32[3]{0:T(128)S(1)} %pad_add_fusion.flags, f32[6,2,384,256]{3,2,1,0:T(8,128)} %fibre.1, s32[2,384,256]{2,1,0:T(8,128)S(1)} %copy-done, f32[2,384,256]{2,1,0:T(8,128)S(1)} %scatter_fusion), custom_call_target="tpu_custom_call" | custom-call | flops 58982400 | bytes 7864320 | tf_op jit(solution)/shard_map/pallas_call | solution.py:91
  22.4 1.3 %slice_bitcast_fusion = (f32[1,1,384,256]{3,2,1,0:T(8,128)S(1)}, f32[1,1,384,256]{3,2,1,0:T(8,128)}, f32[1,384,256]{2,1,0:T(8,128)S(1)}, f32[1,384,256]{2,1,0:T(...) fusion(f32[2,384,256]{2,1,0:T(8,128)S(1)} %get-tuple-element.4,, ...), kind=kLoop, calls=%fused_computation.49 | loop fusion | flops 491520 | bytes 6684676 | tf_op jit(solution)/shard_map/stack | solution.py:350
  23.8 1.3 %collective-permute-start = (f32[384,256]{1,0:T(8,128)}, f32[384,256]{1,0:T(8,128)}, u32[]{:S(2)}, u32[]{:S(2)}) collective-permute-start(f32[384,256]{1,0:T(8,128)} %get-tuple-element.21), channel_id=1, source_target_pairs={{0,64},{32,96},{64,0},{96,32},{128,192},{160,224},{192,128},{224,1... | collective-permute-start | bytes 1179656 | tf_op jit(solution)/shard_map/ppermute | solution.py:361
  25.1 1.2 %maximum_select_fusion = (f32[2,384,256]{2,1,0:T(8,128)S(1)}, f32[2,384,256]{2,1,0:T(8,128)S(1)}) fusion(f32[1,384,256]{2,1,0:T(8,128)} %get-tuple-element.20, f32[1,384,256]{2,1,0:T(8,128)S(1)} %get-tuple-element.12, f32[1,384,256]{2,1,0:T(8,128)S(1)} %get-tuple-element.13, f32[1,384,256]{2,1,0:T(8,128)S(1)} %get-tuple-element.19, pred[]{:T(512)S(6)} %eq.19, ...), kind=kLoop, calls=%fused_computation.4 | loop fusion | flops 1179648 | bytes 4325377 | tf_op jit(solution)/shard_map/jit(_where)/select_n | solution.py:356
  26.3 0.8 fusion.3.total_min
  27.1 0.8 fusion.4.total_add
  27.9 49.7 %shard_map.69 = f32[384,256]{1,0:T(8,128)} custom-call(f32[384,256]{1,0:T(8,128)} %fusion.4.total_add, f32[384,256]{1,0:T(8,128)} %fusion.3.total_min), custom_call_target="tpu_custom_call" | custom-call | tf_op jit(solution)/shard_map/pallas_call | solution.py:307
  77.5 0.2 collective-permute-start.3
  77.8 0.0 collective-permute-done
  77.8 1.2 %min.44 = f32[384,256]{1,0:T(8,128)S(1)} minimum(f32[384,256]{1,0:T(8,128)} %get-tuple-element.21, f32[384,256]{1,0:T(8,128)} %collective-permute-done) | non-fusion elementwise | flops 98304 | bytes 1179648 | tf_op jit(solution)/shard_map/min | solution.py:362
  79.0 3.2 %collective-permute-start.1 = (f32[384,256]{1,0:T(8,128)S(1)}, f32[384,256]{1,0:T(8,128)S(1)}, u32[]{:S(2)}, u32[]{:S(2)}) collective-permute-start(f32[384,256]{1,0:T(8,128)S(1)} %min.44), channel_id=1, source_target_pairs={{0,128},{32,160},{64,192},{96,224},{128,0},{160,32},{192,64},{224,... | collective-permute-start | bytes 1179656 | tf_op jit(solution)/shard_map/ppermute | solution.py:361
  82.2 4.3 %collective-permute-done.3 = f32[384,256]{1,0:T(8,128)S(1)} collective-permute-done((f32[384,256]{1,0:T(8,128)}, f32[384,256]{1,0:T(8,128)S(1)}, u32[]{:S(2)}, u32[]{:S(2)}) %collective-permute-start.3) | collective-permute-done | bytes 393248 | tf_op jit(solution)/shard_map/ppermute | solution.py:380
  86.5 1.0 min.50
  87.6 2.9 %collective-permute-start.4 = (f32[384,256]{1,0:T(8,128)S(1)}, f32[384,256]{1,0:T(8,128)S(1)}, u32[]{:S(2)}, u32[]{:S(2)}) collective-permute-start(f32[384,256]{1,0:T(8,128)S(1)} %min.50), channel_id=1, source_target_pairs={{0,128},{32,160},{64,192},{96,224},{128,0},{160,32},{192,64},{224,... | collective-permute-start | bytes 1179656 | tf_op jit(solution)/shard_map/ppermute | solution.py:380
  90.5 6.3 %collective-permute-done.1 = f32[384,256]{1,0:T(8,128)S(1)} collective-permute-done((f32[384,256]{1,0:T(8,128)S(1)}, f32[384,256]{1,0:T(8,128)S(1)}, u32[]{:S(2)}, u32[]{:S(2)}) %collective-permute-start.1) | collective-permute-done | bytes 393248 | tf_op jit(solution)/shard_map/ppermute | solution.py:361
  96.7 0.1 min.45
  96.8 5.4 %collective-permute-start.2 = (f32[384,256]{1,0:T(8,128)S(1)}, f32[384,256]{1,0:T(8,128)}, u32[]{:S(2)}, u32[]{:S(2)}) collective-permute-start(f32[384,256]{1,0:T(8,128)S(1)} %min.45), channel_id=1, source_target_pairs={{0,32},{32,0},{64,96},{96,64},{128,160},{160,128},{192,224},{224,1... | collective-permute-start | bytes 1179656 | tf_op jit(solution)/shard_map/ppermute | solution.py:363
  102.2 2.9 %collective-permute-done.4 = f32[384,256]{1,0:T(8,128)S(1)} collective-permute-done((f32[384,256]{1,0:T(8,128)S(1)}, f32[384,256]{1,0:T(8,128)S(1)}, u32[]{:S(2)}, u32[]{:S(2)}) %collective-permute-start.4) | collective-permute-done | bytes 393248 | tf_op jit(solution)/shard_map/ppermute | solution.py:380
  105.2 0.8 min.51
  106.0 2.9 %collective-permute-start.5 = (f32[384,256]{1,0:T(8,128)}, f32[384,256]{1,0:T(8,128)}, u32[]{:S(2)}, u32[]{:S(2)}) collective-permute-start(f32[384,256]{1,0:T(8,128)} %min.51), channel_id=1, source_target_pairs={{0,32},{32,0},{64,96},{96,64},{128,160},{160,128},{192,224},{224,1... | collective-permute-start | bytes 1179656 | tf_op jit(solution)/shard_map/ppermute | solution.py:382
  108.8 2.3 %fusion.1 = f32[1,2,384,256]{3,2,1,0:T(8,128)} fusion(f32[1,1,384,256]{3,2,1,0:T(8,128)} %get-tuple-element.15, f32[1,1,384,256]{3,2,1,0:T(8,128)S(1)} %bitcast.56, f32[1,1,384,256]{3,2,1,0:T(8,128)} %get-tuple-element.14, f32[1,1,384,256]{3,2,1,0:T(8,128)} %get-tuple-element.11, f32[1,1,384,256]{3,2,1,0:T(8,128)S(1)} %bitcast.57, ...), kind=kLoop, calls=%fused_computation.7 | loop fusion | flops 1572864 | bytes 3932161 | tf_op jit(solution)/shard_map/min | solution.py:376
  111.1 0.0 collective-permute-done.2
  111.2 1.1 fusion.8
  112.3 0.0 collective-permute-done.5
  112.3 1.2 %broadcast_select_fusion.1 = (f32[384,256]{1,0:T(8,128)S(1)}, f32[384,256]{1,0:T(8,128)S(1)}) fusion(f32[384,256]{1,0:T(8,128)} %min.51, f32[384,256]{1,0:T(8,128)} %collective-permute-done.5, pred[]{:T(512)S(6)} %eq.18), kind=kLoop, calls=%fused_computation.24 | loop fusion | flops 196608 | bytes 1572865 | tf_op jit(solution)/shard_map/jit(_where)/select_n | solution.py:383
  113.4 1.1 maximum_minimum_fusion
  (2 shorter events, 0.0 us)
Async XLA Ops:
  4.6 1.1 copy-start
  23.8 54.0 %collective-permute-start = (f32[384,256]{1,0:T(8,128)}, f32[384,256]{1,0:T(8,128)}, u32[]{:S(2)}, u32[]{:S(2)}) collective-permute-start(f32[384,256]{1,0:T(8,128)} %get-tuple-element.21), channel_id=1, source_target_pairs={{0,64},{32,96},{64,0},{96,32},{128,192},{160,224},{192,128},{224,1... | collective-permute-start | bytes 1179656 | tf_op jit(solution)/shard_map/ppermute | solution.py:361
  77.5 31.3 %copy-start.1 = (f32[384,256]{1,0:T(8,128)S(1)}, f32[384,256]{1,0:T(8,128)}, u32[]{:S(2)}) copy-start(f32[384,256]{1,0:T(8,128)} %shard_map.69) | copy-start | bytes 1179652
  77.5 9.0 %collective-permute-start.3 = (f32[384,256]{1,0:T(8,128)}, f32[384,256]{1,0:T(8,128)S(1)}, u32[]{:S(2)}, u32[]{:S(2)}) collective-permute-start(f32[384,256]{1,0:T(8,128)} %shard_map.69), channel_id=1, source_target_pairs={{0,64},{32,96},{64,0},{96,32},{128,192},{160,224},{192,128},{224,1... | collective-permute-start | bytes 1179656 | tf_op jit(solution)/shard_map/ppermute | solution.py:380
  79.0 17.8 %collective-permute-start.1 = (f32[384,256]{1,0:T(8,128)S(1)}, f32[384,256]{1,0:T(8,128)S(1)}, u32[]{:S(2)}, u32[]{:S(2)}) collective-permute-start(f32[384,256]{1,0:T(8,128)S(1)} %min.44), channel_id=1, source_target_pairs={{0,128},{32,160},{64,192},{96,224},{128,0},{160,32},{192,64},{224,... | collective-permute-start | bytes 1179656 | tf_op jit(solution)/shard_map/ppermute | solution.py:361
  87.6 17.6 %collective-permute-start.4 = (f32[384,256]{1,0:T(8,128)S(1)}, f32[384,256]{1,0:T(8,128)S(1)}, u32[]{:S(2)}, u32[]{:S(2)}) collective-permute-start(f32[384,256]{1,0:T(8,128)S(1)} %min.50), channel_id=1, source_target_pairs={{0,128},{32,160},{64,192},{96,224},{128,0},{160,32},{192,64},{224,... | collective-permute-start | bytes 1179656 | tf_op jit(solution)/shard_map/ppermute | solution.py:380
  96.8 14.4 %collective-permute-start.2 = (f32[384,256]{1,0:T(8,128)S(1)}, f32[384,256]{1,0:T(8,128)}, u32[]{:S(2)}, u32[]{:S(2)}) collective-permute-start(f32[384,256]{1,0:T(8,128)S(1)} %min.45), channel_id=1, source_target_pairs={{0,32},{32,0},{64,96},{96,64},{128,160},{160,128},{192,224},{224,1... | collective-permute-start | bytes 1179656 | tf_op jit(solution)/shard_map/ppermute | solution.py:363
  106.0 6.3 %collective-permute-start.5 = (f32[384,256]{1,0:T(8,128)}, f32[384,256]{1,0:T(8,128)}, u32[]{:S(2)}, u32[]{:S(2)}) collective-permute-start(f32[384,256]{1,0:T(8,128)} %min.51), channel_id=1, source_target_pairs={{0,32},{32,0},{64,96},{96,64},{128,160},{160,128},{192,224},{224,1... | collective-permute-start | bytes 1179656 | tf_op jit(solution)/shard_map/ppermute | solution.py:382

commit v5 on v4

--- a/solution.py
+++ b/solution.py
@@ -33,10 +33,31 @@
     return a, m
 
 
-def local_kernel(flags, fibre, tissue, seeded, cost_x, field, cost_y, *, grid_step):
-    planes, cells_y, cells_z = seeded.shape
+def local_kernel(flags, stims, stim_times, fibre, tissue, previous, cost_x, field, totals, own,
+                 cost_y, *, grid_step):
+    planes, cells_y, cells_z = previous.shape
     chunks = cells_y // CHUNK
     inf = jnp.float32(jnp.inf)
+
+    field[...] = previous[...]
+
+    def seed(k, carry):
+        p = stims[0, k]
+        r = stims[1, k]
+        c = stims[2, k]
+
+        @pl.when((p >= 0) & (p < planes))
+        def _():
+            base = pl.multiple_of(r // ROWS * ROWS, ROWS)
+            block = field[p, pl.ds(base, ROWS), :]
+            row = lax.broadcasted_iota(jnp.int32, block.shape, 0)
+            lane = lax.broadcasted_iota(jnp.int32, block.shape, 1)
+            hit = (row == r - base) & (lane == c)
+            field[p, pl.ds(base, ROWS), :] = jnp.where(hit, jnp.minimum(block, stim_times[k]), block)
+
+        return carry
+
+    lax.fori_loop(0, stims.shape[1], seed, 0)
 
     def costs_and_z(reverse):
         def body(i, carry):
@@ -56,7 +77,7 @@
             cost_x[p, rows, :] = jnp.sqrt(cx / det) * factor
             cost_y[p, rows, :] = jnp.sqrt(cy / det) * factor
             step_z = jnp.sqrt(cz / det) * factor
-            _, u = block_scan(step_z, seeded[p, rows, :], 1, reverse, False)
+            _, u = block_scan(step_z, field[p, rows, :], 1, reverse, False)
             field[p, rows, :] = u
             return carry
 
@@ -82,23 +103,40 @@
         pl.when(flag == 1)(functools.partial(fn, True))
         pl.when(flag != 1)(functools.partial(fn, False))
 
-
-def local_sweeps(flags, fibre, tissue, seeded, grid_step):
-    planes, cells_y, cells_z = seeded.shape
-    plane = jax.ShapeDtypeStruct(seeded.shape, jnp.float32)
+    def edge(i, carry):
+        rows = pl.ds(pl.multiple_of(i * CHUNK, CHUNK), CHUNK)
+        c0 = cost_x[0, rows, :]
+        c1 = cost_x[1, rows, :]
+        u0 = field[0, rows, :]
+        u1 = field[1, rows, :]
+        down = flags[0] == 1
+        totals[0, rows, :] = jnp.where(down, c1 + c0, c0 + c1)
+        totals[1, rows, :] = jnp.where(down, jnp.minimum(u1 + c0, u0), jnp.minimum(u0 + c1, u1))
+        own[rows, :] = jnp.where(down, u1, u0)
+        return carry
+
+    lax.fori_loop(0, chunks, edge, 0)
+
+
+def local_sweeps(flags, stims, stim_times, fibre, tissue, previous, grid_step):
+    planes, cells_y, cells_z = previous.shape
+    field = jax.ShapeDtypeStruct(previous.shape, jnp.float32)
+    totals = jax.ShapeDtypeStruct((2, cells_y, cells_z), jnp.float32)
+    own = jax.ShapeDtypeStruct((cells_y, cells_z), jnp.float32)
     vmem = pl.BlockSpec(memory_space=pltpu.VMEM)
+    smem = pl.BlockSpec(memory_space=pltpu.SMEM)
     elements = planes * cells_y * cells_z
     return pl.pallas_call(
         functools.partial(local_kernel, grid_step=grid_step),
-        out_shape=(plane, plane),
-        in_specs=[pl.BlockSpec(memory_space=pltpu.SMEM), vmem, vmem, vmem],
-        out_specs=(vmem, vmem),
-        scratch_shapes=[pltpu.VMEM(seeded.shape, jnp.float32)],
+        out_shape=(field, field, totals, own),
+        in_specs=[smem, smem, smem, vmem, vmem, vmem],
+        out_specs=(vmem, vmem, vmem, vmem),
+        scratch_shapes=[pltpu.VMEM(previous.shape, jnp.float32)],
         compiler_params=pltpu.CompilerParams(vmem_limit_bytes=48 * 1024 * 1024),
         cost_estimate=pl.CostEstimate(
             flops=300 * elements, transcendentals=6 * elements, bytes_accessed=40 * elements
         ),
-    )(flags, fibre, tissue, seeded)
+    )(flags, stims, stim_times, fibre, tissue, previous)
 
 
 RELAY_ROWS = 16
@@ -337,51 +375,46 @@
     grid_step = 2.0 / (planes * slabs)
 
     plane_index = stim_sites // (cells_y * cells_z) - slab_index * planes
-    inside = (plane_index >= 0) & (plane_index < planes)
-    plane_index = jnp.where(inside, plane_index, planes)
     row_index = stim_sites // cells_z % cells_y
     column_index = stim_sites % cells_z
-    seeded = previous.at[plane_index, row_index, column_index].min(stim_times, mode="drop")
+    stims = jnp.stack([plane_index, row_index, column_index]).astype(jnp.int32)
 
     bits = jnp.stack([group_index % 2, group_index // 2 % 2, group_index // 4 % 2]).astype(jnp.int32)
-    cost_x, field = local_sweeps(bits, fibre_tensor, tissue, seeded, grid_step)
+    cost_x, field, totals, own_plane = local_sweeps(
+        bits, stims, stim_times, fibre_tensor, tissue, previous, grid_step)
+
+    partners = [m for m in range(2, orders, 2)]
+    core = group_index % 2
+    gathered = [lax.ppermute(own_plane, "order", [(g, g ^ m) for g in range(orders)]) for m in partners]
+
+    incoming = relay(totals[0], totals[1], slabs)
+
+    least_plane = own_plane
+    for got in gathered:
+        least_plane = jnp.minimum(least_plane, got)
+    least_in = incoming
+    for m in partners:
+        least_in = jnp.minimum(least_in, lax.ppermute(incoming, "order", [(g, g ^ m) for g in range(orders)]))
+    other = lax.ppermute(jnp.stack([least_plane, least_in]), "order", [(g, g ^ 1) for g in range(orders)])
+
+    least0 = jnp.where(core == 0, least_plane, other[0])
+    least1 = jnp.where(core == 0, other[0], least_plane)
+    up_in = jnp.where(core == 0, least_in, other[1])
+    down_in = jnp.where(core == 0, other[1], least_in)
 
     up_add = jnp.stack([cost_x[0], cost_x[0] + cost_x[1]])
     up_min = jnp.stack([field[0], jnp.minimum(field[0] + cost_x[1], field[1])])
     down_add = jnp.stack([cost_x[1] + cost_x[0], cost_x[1]])
     down_min = jnp.stack([jnp.minimum(field[1] + cost_x[0], field[0]), field[1]])
-
-    backward_x = group_index % 2 == 1
+    backward_x = core == 1
     line_add = jnp.where(backward_x, down_add, up_add)
     line_min = jnp.where(backward_x, down_min, up_min)
-
-    core = group_index % 2
-    own_plane = lax.dynamic_index_in_dim(field, core, 0, keepdims=False)
-    for mask in [m for m in (2, 4, 8, 16) if m < orders]:
-        got = lax.ppermute(own_plane, "order", [(g, g ^ mask) for g in range(orders)])
-        own_plane = jnp.minimum(own_plane, got)
-    other_plane = lax.ppermute(own_plane, "order", [(g, g ^ 1) for g in range(orders)])
-    least0 = jnp.where(core == 0, own_plane, other_plane)
-    least1 = jnp.where(core == 0, other_plane, own_plane)
+    sweep_field = jnp.minimum(incoming[None] + line_add, line_min)
+
     least_local = jnp.stack([
         jnp.minimum(least0, least1 + cost_x[0]),
         jnp.minimum(least1, least0 + cost_x[1]),
     ])
-
-    total_add = jnp.where(backward_x, line_add[0], line_add[planes - 1])
-    total_min = jnp.where(backward_x, line_min[0], line_min[planes - 1])
-
-    incoming = relay(total_add, total_min, slabs)
-
-    sweep_field = jnp.minimum(incoming[None] + line_add, line_min)
-
-    least_in = incoming
-    for mask in [m for m in (2, 4, 8, 16) if m < orders]:
-        got = lax.ppermute(least_in, "order", [(g, g ^ mask) for g in range(orders)])
-        least_in = jnp.minimum(least_in, got)
-    other_in = lax.ppermute(least_in, "order", [(g, g ^ 1) for g in range(orders)])
-    up_in = jnp.where(core == 0, least_in, other_in)
-    down_in = jnp.where(core == 0, other_in, least_in)
     merged = jnp.minimum(
         least_local,
         jnp.minimum(up_in[None] + up_add, down_in[None] + down_add),

time: 115 us -> 108 us (0.939)
  the two profiles are of different devices: /device:TPU:131 before, /device:TPU:103 now
where the time goes in v5:
time: 108 us
  starting transfers between devices  43.2 us (40%)
  Pallas kernels  41.7 us (39%)
  waiting for transfers between devices  12.7 us (12%)
  other arithmetic  5.84 us (5%)
  local copies, waits for them, and re-layouts  3.85 us (4%)
    ppermute x1, starting transfers between devices, shards(): lax.ppermute(jnp.stack([least_plane, least_in]), 'order', [(g, g ^ 1) for...  35 us
    pallas_call x1, Pallas kernels, relay(): pl.pallas_call(functools.partial(relay_kernel, line=line), out_shape=jax....  24.5 us
    pallas_call x1, Pallas kernels, local_sweeps(): pl.pallas_call(functools.partial(local_kernel, grid_step=grid_step), out_...  17.2 us
    ppermute x3, waiting for transfers between devices, shards(): lax.ppermute(incoming, 'order', [(g, g ^ m) for g in range(orders)])  12.1 us
    ppermute x3, starting transfers between devices, shards(): lax.ppermute(own_plane, 'order', [(g, g ^ m) for g in range(orders)])  4.22 us
    ppermute x3, starting transfers between devices, shards(): lax.ppermute(incoming, 'order', [(g, g ^ m) for g in range(orders)])  3.94 us
    unnamed x8, local copies, waits for them, and re-layouts  2.92 us
  transfers between devices with their start and end apart: 7, of which 4 were waited for; matrix products, arithmetic and copies ran while one was open for 2% of the time, Pallas kernels for 23%

profile of v5, /device:TPU:103, one launch (start us, length us, event | category | flops | bytes accessed | tf_op | source)
XLA Modules:
  0.0 108.1 jit_solution(10096039800125547696)
XLA Ops:
  0.7 0.7 subtract_bitcast_fusion
  1.4 0.1 pad_add_fusion.1.flags
  1.5 0.0 copy-start
  1.5 1.1 %copy-done = s32[2,384,256]{2,1,0:T(8,128)S(1)} copy-done((s32[2,384,256]{2,1,0:T(8,128)S(1)}, s32[2,384,256]{2,1,0:T(8,128)}, u32[]{:S(2)}) %copy-start) | copy-done | bytes 786456
  2.6 1.1 %copy-done.1 = f32[2,384,256]{2,1,0:T(8,128)S(1)} copy-done((f32[2,384,256]{2,1,0:T(8,128)S(1)}, f32[2,384,256]{2,1,0:T(8,128)}, u32[]{:S(2)}) %copy-start.1) | copy-done | bytes 786456
  3.7 0.7 copy-done.2
  4.4 17.2 %shard_map.68 = (f32[2,384,256]{2,1,0:T(8,128)S(1)}, f32[2,384,256]{2,1,0:T(8,128)S(1)}, f32[2,384,256]{2,1,0:T(8,128)S(1)}, f32[384,256]{1,0:T(8,128)S(1)}) custom-call(s32[3]{0:T(128)S(1)} %pad_add_fusion.1.flags, s32[3,16]{1,0:T(4,128)S(1)} %pad_add_fusion.stims, f32[16]{0:T(128)S(1)} %copy-done.2, f32[6,2,384,256]{3,2,1,0:T(8,128)} %fibre.1, ...), custom_call_target="tpu_custom_call" | custom-call | flops 58982400 | bytes 7864320 | tf_op jit(solution)/shard_map/pallas_call | solution.py:129
  21.6 1.4 %collective-permute-start = (f32[384,256]{1,0:T(8,128)S(1)}, f32[384,256]{1,0:T(8,128)S(1)}, u32[]{:S(2)}, u32[]{:S(2)}) collective-permute-start(f32[384,256]{1,0:T(8,128)S(1)} %get-tuple-element.6), channel_id=1, source_target_pairs={{0,64},{32,96},{64,0},{96,32},{128,192},{160,224},{192,128},{224,1... | collective-permute-start | bytes 1179656 | tf_op jit(solution)/shard_map/ppermute | solution.py:388
  23.0 2.8 %collective-permute-start.1 = (f32[384,256]{1,0:T(8,128)S(1)}, f32[384,256]{1,0:T(8,128)S(1)}, u32[]{:S(2)}, u32[]{:S(2)}) collective-permute-start(f32[384,256]{1,0:T(8,128)S(1)} %get-tuple-element.6), channel_id=1, source_target_pairs={{0,128},{32,160},{64,192},{96,224},{128,0},{160,32},{192,64},{224,... | collective-permute-start | bytes 1179656 | tf_op jit(solution)/shard_map/ppermute | solution.py:388
  25.8 0.0 collective-permute-start.2
  25.8 0.9 slice_bitcast_fusion.2
  26.8 24.5 %shard_map.69 = f32[384,256]{1,0:T(8,128)} custom-call(f32[384,256]{1,0:T(8,128)} %get-tuple-element.26.total_add, f32[384,256]{1,0:T(8,128)} %get-tuple-element.25.total_min), custom_call_target="tpu_custom_call" | custom-call | tf_op jit(solution)/shard_map/pallas_call | solution.py:345
  51.3 0.1 collective-permute-start.3
  51.4 3.8 %collective-permute-start.4 = (f32[384,256]{1,0:T(8,128)}, f32[384,256]{1,0:T(8,128)S(1)}, u32[]{:S(2)}, u32[]{:S(2)}) collective-permute-start(f32[384,256]{1,0:T(8,128)} %shard_map.69), channel_id=1, source_target_pairs={{0,128},{32,160},{64,192},{96,224},{128,0},{160,32},{192,64},{224,... | collective-permute-start | bytes 1179656 | tf_op jit(solution)/shard_map/ppermute | solution.py:397
  55.2 0.0 collective-permute-done
  55.2 0.0 collective-permute-start.5
  55.2 0.0 collective-permute-done.1
  55.2 0.0 collective-permute-done.2
  55.2 0.1 minimum_minimum_fusion.1
  55.3 0.0 copy-start.3
  55.3 2.8 %collective-permute-done.3 = f32[384,256]{1,0:T(8,128)S(1)} collective-permute-done((f32[384,256]{1,0:T(8,128)}, f32[384,256]{1,0:T(8,128)S(1)}, u32[]{:S(2)}, u32[]{:S(2)}) %collective-permute-start.3) | collective-permute-done | bytes 393248 | tf_op jit(solution)/shard_map/ppermute | solution.py:397
  58.2 6.7 %collective-permute-done.4 = f32[384,256]{1,0:T(8,128)S(1)} collective-permute-done((f32[384,256]{1,0:T(8,128)}, f32[384,256]{1,0:T(8,128)S(1)}, u32[]{:S(2)}, u32[]{:S(2)}) %collective-permute-start.4) | collective-permute-done | bytes 393248 | tf_op jit(solution)/shard_map/ppermute | solution.py:397
  64.9 2.6 %collective-permute-done.5 = f32[384,256]{1,0:T(8,128)S(1)} collective-permute-done((f32[384,256]{1,0:T(8,128)}, f32[384,256]{1,0:T(8,128)S(1)}, u32[]{:S(2)}, u32[]{:S(2)}) %collective-permute-start.5) | collective-permute-done | bytes 393248 | tf_op jit(solution)/shard_map/ppermute | solution.py:397
  67.5 1.1 %minimum_minimum_fusion = f32[384,256]{1,0:T(8,128)S(1)} fusion(f32[384,256]{1,0:T(8,128)S(1)} %collective-permute-done.5, f32[384,256]{1,0:T(8,128)S(1)} %collective-permute-done.4, f32[384,256]{1,0:T(8,128)} %shard_map.69, f32[384,256]{1,0:T(8,128)S(1)} %collective-permute-done.3), kind=kLoop, calls=%fused_computation.19 | loop fusion | flops 294912 | bytes 1966080 | tf_op jit(solution)/shard_map/min | solution.py:397
  68.6 0.1 pad_maximum_fusion
  68.6 35.0 %collective-permute-start.6 = (f32[2,384,256]{2,1,0:T(8,128)S(1)}, f32[2,384,256]{2,1,0:T(8,128)}, u32[]{:S(2)}, u32[]{:S(2)}) collective-permute-start(f32[2,384,256]{2,1,0:T(8,128)S(1)} %pad_maximum_fusion), channel_id=1, source_target_pairs={{0,32},{32,0},{64,96},{96,64},{128,160},{160,128},{192,224},{224,1... | collective-permute-start | bytes 2359304 | tf_op jit(solution)/shard_map/ppermute | solution.py:398
  103.7 0.3 minimum_bitcast_fusion
  104.0 0.0 copy-done.3
  104.0 1.1 %fusion.2 = f32[1,2,384,256]{3,2,1,0:T(8,128)} fusion(f32[1,1,384,256]{3,2,1,0:T(8,128)S(1)} %get-tuple-element.19, f32[1,1,384,256]{3,2,1,0:T(8,128)S(1)} %bitcast.64, f32[1,1,384,256]{3,2,1,0:T(8,128)S(1)} %get-tuple-element.17, f32[1,1,384,256]{3,2,1,0:T(8,128)S(1)} %get-tuple-element.22, f32[1,1,384,256]{3,2,1,0:T(8,128)S(1)} %get-tuple-element.13, ...), kind=kLoop, calls=%fused_computation.7 | loop fusion | flops 1572864 | bytes 3932161 | tf_op jit(solution)/shard_map/min | solution.py:412
  105.1 0.6 collective-permute-done.6
  105.7 1.3 %fusion.10 = (f32[384,256]{1,0:T(8,128)S(1)}, f32[384,256]{1,0:T(8,128)S(1)}, f32[1,384,256]{2,1,0:T(8,128)S(1)}, f32[1,384,256]{2,1,0:T(8,128)S(1)}) fusion(f32[384,256]{1,0:T(8,128)S(1)} %minimum_minimum_fusion, f32[2,384,256]{2,1,0:T(8,128)} %collective-permute-done.6, pred[]{:T(512)S(6)} %eq.17, f32[2,384,256]{2,1,0:T(8,128)S(1)} %get-tuple-element.8, ...), kind=kLoop, calls=%fused_computation.26 | loop fusion | flops 786432 | bytes 3932161 | tf_op jit(solution)/shard_map/jit(_where)/select_n | solution.py:402
  107.0 1.1 %maximum_minimum_fusion = f32[2,384,256]{2,1,0:T(8,128)} fusion(f32[1,384,256]{2,1,0:T(8,128)S(1)} %get-tuple-element.23, f32[1,384,256]{2,1,0:T(8,128)S(1)} %get-tuple-element.24, f32[1,384,256]{2,1,0:T(8,128)S(1)} %get-tuple-element.18, f32[1,384,256]{2,1,0:T(8,128)S(1)} %get-tuple-element.21, f32[1,384,256]{2,1,0:T(8,128)S(1)} %get-tuple-element.20, ...), kind=kLoop, calls=%fused_computation.1 | loop fusion | flops 1376256 | bytes 3538944 | tf_op jit(solution)/shard_map/min | solution.py:418
  (3 shorter events, 0.0 us)
Async XLA Ops:
  1.5 1.1 %copy-start = (s32[2,384,256]{2,1,0:T(8,128)S(1)}, s32[2,384,256]{2,1,0:T(8,128)}, u32[]{:S(2)}) copy-start(s32[2,384,256]{2,1,0:T(8,128)} %tissue.1) | copy-start | bytes 2359300
  2.6 1.1 %copy-start.1 = (f32[2,384,256]{2,1,0:T(8,128)S(1)}, f32[2,384,256]{2,1,0:T(8,128)}, u32[]{:S(2)}) copy-start(f32[2,384,256]{2,1,0:T(8,128)} %previous.1) | copy-start | bytes 2359300
  3.7 0.7 copy-start.2
  21.6 33.6 %collective-permute-start = (f32[384,256]{1,0:T(8,128)S(1)}, f32[384,256]{1,0:T(8,128)S(1)}, u32[]{:S(2)}, u32[]{:S(2)}) collective-permute-start(f32[384,256]{1,0:T(8,128)S(1)} %get-tuple-element.6), channel_id=1, source_target_pairs={{0,64},{32,96},{64,0},{96,32},{128,192},{160,224},{192,128},{224,1... | collective-permute-start | bytes 1179656 | tf_op jit(solution)/shard_map/ppermute | solution.py:388
  23.0 32.2 %collective-permute-start.1 = (f32[384,256]{1,0:T(8,128)S(1)}, f32[384,256]{1,0:T(8,128)S(1)}, u32[]{:S(2)}, u32[]{:S(2)}) collective-permute-start(f32[384,256]{1,0:T(8,128)S(1)} %get-tuple-element.6), channel_id=1, source_target_pairs={{0,128},{32,160},{64,192},{96,224},{128,0},{160,32},{192,64},{224,... | collective-permute-start | bytes 1179656 | tf_op jit(solution)/shard_map/ppermute | solution.py:388
  25.8 29.4 %collective-permute-start.2 = (f32[384,256]{1,0:T(8,128)S(1)}, f32[384,256]{1,0:T(8,128)S(1)}, u32[]{:S(2)}, u32[]{:S(2)}) collective-permute-start(f32[384,256]{1,0:T(8,128)S(1)} %get-tuple-element.6), channel_id=1, source_target_pairs={{0,192},{32,224},{64,128},{96,160},{128,64},{160,96},{192,0},{224,... | collective-permute-start | bytes 1179656 | tf_op jit(solution)/shard_map/ppermute | solution.py:388
  51.3 6.9 %collective-permute-start.3 = (f32[384,256]{1,0:T(8,128)}, f32[384,256]{1,0:T(8,128)S(1)}, u32[]{:S(2)}, u32[]{:S(2)}) collective-permute-start(f32[384,256]{1,0:T(8,128)} %shard_map.69), channel_id=1, source_target_pairs={{0,64},{32,96},{64,0},{96,32},{128,192},{160,224},{192,128},{224,1... | collective-permute-start | bytes 1179656 | tf_op jit(solution)/shard_map/ppermute | solution.py:397
  51.4 13.5 %collective-permute-start.4 = (f32[384,256]{1,0:T(8,128)}, f32[384,256]{1,0:T(8,128)S(1)}, u32[]{:S(2)}, u32[]{:S(2)}) collective-permute-start(f32[384,256]{1,0:T(8,128)} %shard_map.69), channel_id=1, source_target_pairs={{0,128},{32,160},{64,192},{96,224},{128,0},{160,32},{192,64},{224,... | collective-permute-start | bytes 1179656 | tf_op jit(solution)/shard_map/ppermute | solution.py:397
  55.2 12.3 %collective-permute-start.5 = (f32[384,256]{1,0:T(8,128)}, f32[384,256]{1,0:T(8,128)S(1)}, u32[]{:S(2)}, u32[]{:S(2)}) collective-permute-start(f32[384,256]{1,0:T(8,128)} %shard_map.69), channel_id=1, source_target_pairs={{0,192},{32,224},{64,128},{96,160},{128,64},{160,96},{192,0},{224,... | collective-permute-start | bytes 1179656 | tf_op jit(solution)/shard_map/ppermute | solution.py:397
  55.3 48.7 %copy-start.3 = (f32[384,256]{1,0:T(8,128)S(1)}, f32[384,256]{1,0:T(8,128)}, u32[]{:S(2)}) copy-start(f32[384,256]{1,0:T(8,128)} %shard_map.69) | copy-start | bytes 1179652
  68.6 37.1 %collective-permute-start.6 = (f32[2,384,256]{2,1,0:T(8,128)S(1)}, f32[2,384,256]{2,1,0:T(8,128)}, u32[]{:S(2)}, u32[]{:S(2)}) collective-permute-start(f32[2,384,256]{2,1,0:T(8,128)S(1)} %pad_maximum_fusion), channel_id=1, source_target_pairs={{0,32},{32,0},{64,96},{96,64},{128,160},{160,128},{192,224},{224,1... | collective-permute-start | bytes 2359304 | tf_op jit(solution)/shard_map/ppermute | solution.py:398

commit v6 on v5

--- a/solution.py
+++ b/solution.py
@@ -249,8 +249,6 @@
 
         return carry
 
-    lax.fori_loop(0, chunks, stage1, 0)
-
     def stage2(c, carry):
         rows = rows_of(c)
 
@@ -281,7 +279,11 @@
 
         return carry
 
-    lax.fori_loop(0, chunks, stage2, 0)
+    def stages12(c, carry):
+        stage1(c, carry)
+        return stage2(c, carry)
+
+    lax.fori_loop(0, chunks, stages12, 0)
 
     def stage3(c, carry):
         rows = rows_of(c)

time: 108 us -> 104 us (0.963)
  starting transfers between devices: 43.2 us -> 39.2 us
    ppermute x1, starting transfers between devices: 35 us -> 31.1 us  [shards(): lax.ppermute(jnp.stack([least_plane, least_in]), 'order', [(g, g ^ 1) for...]
  transfers between devices with their start and end apart: 7 -> 7, of which waited for: 4 -> 4; matrix products, arithmetic and copies ran while one was open for 2% -> 2% of each run, Pallas kernels for 23% -> 24%
where the time goes in v6:
time: 104 us
  Pallas kernels  41.7 us (40%)
  starting transfers between devices  39.2 us (38%)
  waiting for transfers between devices  12.7 us (12%)
  other arithmetic  5.84 us (6%)
  local copies, waits for them, and re-layouts  3.85 us (4%)
    ppermute x1, starting transfers between devices, shards(): lax.ppermute(jnp.stack([least_plane, least_in]), 'order', [(g, g ^ 1) for...  31.1 us
    pallas_call x1, Pallas kernels, relay(): pl.pallas_call(functools.partial(relay_kernel, line=line), out_shape=jax....  24.5 us
    pallas_call x1, Pallas kernels, local_sweeps(): pl.pallas_call(functools.partial(local_kernel, grid_step=grid_step), out_...  17.2 us
    ppermute x3, waiting for transfers between devices, shards(): lax.ppermute(incoming, 'order', [(g, g ^ m) for g in range(orders)])  12.1 us
    ppermute x3, starting transfers between devices, shards(): lax.ppermute(own_plane, 'order', [(g, g ^ m) for g in range(orders)])  4.22 us
    ppermute x3, starting transfers between devices, shards(): lax.ppermute(incoming, 'order', [(g, g ^ m) for g in range(orders)])  3.94 us
    unnamed x8, local copies, waits for them, and re-layouts  2.92 us
  transfers between devices with their start and end apart: 7, of which 4 were waited for; matrix products, arithmetic and copies ran while one was open for 2% of the time, Pallas kernels for 24%

profile of v6, /device:TPU:103, one launch (start us, length us, event | category | flops | bytes accessed | tf_op | source)
XLA Modules:
  0.0 104.1 jit_solution(13048948023867286656)
XLA Ops:
  0.7 0.7 subtract_bitcast_fusion
  1.4 0.1 pad_add_fusion.1.flags
  1.5 0.0 copy-start
  1.5 1.1 %copy-done = s32[2,384,256]{2,1,0:T(8,128)S(1)} copy-done((s32[2,384,256]{2,1,0:T(8,128)S(1)}, s32[2,384,256]{2,1,0:T(8,128)}, u32[]{:S(2)}) %copy-start) | copy-done | bytes 786456
  2.6 1.1 %copy-done.1 = f32[2,384,256]{2,1,0:T(8,128)S(1)} copy-done((f32[2,384,256]{2,1,0:T(8,128)S(1)}, f32[2,384,256]{2,1,0:T(8,128)}, u32[]{:S(2)}) %copy-start.1) | copy-done | bytes 786456
  3.7 0.7 copy-done.2
  4.4 17.2 %shard_map.68 = (f32[2,384,256]{2,1,0:T(8,128)S(1)}, f32[2,384,256]{2,1,0:T(8,128)S(1)}, f32[2,384,256]{2,1,0:T(8,128)S(1)}, f32[384,256]{1,0:T(8,128)S(1)}) custom-call(s32[3]{0:T(128)S(1)} %pad_add_fusion.1.flags, s32[3,16]{1,0:T(4,128)S(1)} %pad_add_fusion.stims, f32[16]{0:T(128)S(1)} %copy-done.2, f32[6,2,384,256]{3,2,1,0:T(8,128)} %fibre.1, ...), custom_call_target="tpu_custom_call" | custom-call | flops 58982400 | bytes 7864320 | tf_op jit(solution)/shard_map/pallas_call | solution.py:129
  21.6 1.4 %collective-permute-start = (f32[384,256]{1,0:T(8,128)S(1)}, f32[384,256]{1,0:T(8,128)S(1)}, u32[]{:S(2)}, u32[]{:S(2)}) collective-permute-start(f32[384,256]{1,0:T(8,128)S(1)} %get-tuple-element.6), channel_id=1, source_target_pairs={{0,64},{32,96},{64,0},{96,32},{128,192},{160,224},{192,128},{224,1... | collective-permute-start | bytes 1179656 | tf_op jit(solution)/shard_map/ppermute | solution.py:390
  23.0 2.8 %collective-permute-start.1 = (f32[384,256]{1,0:T(8,128)S(1)}, f32[384,256]{1,0:T(8,128)S(1)}, u32[]{:S(2)}, u32[]{:S(2)}) collective-permute-start(f32[384,256]{1,0:T(8,128)S(1)} %get-tuple-element.6), channel_id=1, source_target_pairs={{0,128},{32,160},{64,192},{96,224},{128,0},{160,32},{192,64},{224,... | collective-permute-start | bytes 1179656 | tf_op jit(solution)/shard_map/ppermute | solution.py:390
  25.8 0.0 collective-permute-start.2
  25.8 0.9 slice_bitcast_fusion.2
  26.8 24.5 %shard_map.69 = f32[384,256]{1,0:T(8,128)} custom-call(f32[384,256]{1,0:T(8,128)} %get-tuple-element.26.total_add, f32[384,256]{1,0:T(8,128)} %get-tuple-element.25.total_min), custom_call_target="tpu_custom_call" | custom-call | tf_op jit(solution)/shard_map/pallas_call | solution.py:347
  51.3 0.1 collective-permute-start.3
  51.4 3.8 %collective-permute-start.4 = (f32[384,256]{1,0:T(8,128)}, f32[384,256]{1,0:T(8,128)S(1)}, u32[]{:S(2)}, u32[]{:S(2)}) collective-permute-start(f32[384,256]{1,0:T(8,128)} %shard_map.69), channel_id=1, source_target_pairs={{0,128},{32,160},{64,192},{96,224},{128,0},{160,32},{192,64},{224,... | collective-permute-start | bytes 1179656 | tf_op jit(solution)/shard_map/ppermute | solution.py:399
  55.2 0.0 collective-permute-done
  55.2 0.0 collective-permute-start.5
  55.2 0.0 collective-permute-done.1
  55.2 0.0 collective-permute-done.2
  55.2 0.1 minimum_minimum_fusion.1
  55.3 0.0 copy-start.3
  55.3 2.8 %collective-permute-done.3 = f32[384,256]{1,0:T(8,128)S(1)} collective-permute-done((f32[384,256]{1,0:T(8,128)}, f32[384,256]{1,0:T(8,128)S(1)}, u32[]{:S(2)}, u32[]{:S(2)}) %collective-permute-start.3) | collective-permute-done | bytes 393248 | tf_op jit(solution)/shard_map/ppermute | solution.py:399
  58.2 6.7 %collective-permute-done.4 = f32[384,256]{1,0:T(8,128)S(1)} collective-permute-done((f32[384,256]{1,0:T(8,128)}, f32[384,256]{1,0:T(8,128)S(1)}, u32[]{:S(2)}, u32[]{:S(2)}) %collective-permute-start.4) | collective-permute-done | bytes 393248 | tf_op jit(solution)/shard_map/ppermute | solution.py:399
  64.9 2.6 %collective-permute-done.5 = f32[384,256]{1,0:T(8,128)S(1)} collective-permute-done((f32[384,256]{1,0:T(8,128)}, f32[384,256]{1,0:T(8,128)S(1)}, u32[]{:S(2)}, u32[]{:S(2)}) %collective-permute-start.5) | collective-permute-done | bytes 393248 | tf_op jit(solution)/shard_map/ppermute | solution.py:399
  67.5 1.1 %minimum_minimum_fusion = f32[384,256]{1,0:T(8,128)S(1)} fusion(f32[384,256]{1,0:T(8,128)S(1)} %collective-permute-done.5, f32[384,256]{1,0:T(8,128)S(1)} %collective-permute-done.4, f32[384,256]{1,0:T(8,128)} %shard_map.69, f32[384,256]{1,0:T(8,128)S(1)} %collective-permute-done.3), kind=kLoop, calls=%fused_computation.19 | loop fusion | flops 294912 | bytes 1966080 | tf_op jit(solution)/shard_map/min | solution.py:399
  68.6 0.1 pad_maximum_fusion
  68.6 31.1 %collective-permute-start.6 = (f32[2,384,256]{2,1,0:T(8,128)S(1)}, f32[2,384,256]{2,1,0:T(8,128)}, u32[]{:S(2)}, u32[]{:S(2)}) collective-permute-start(f32[2,384,256]{2,1,0:T(8,128)S(1)} %pad_maximum_fusion), channel_id=1, source_target_pairs={{0,32},{32,0},{64,96},{96,64},{128,160},{160,128},{192,224},{224,1... | collective-permute-start | bytes 2359304 | tf_op jit(solution)/shard_map/ppermute | solution.py:400
  99.7 0.3 minimum_bitcast_fusion
  100.0 0.0 copy-done.3
  100.0 1.1 %fusion.2 = f32[1,2,384,256]{3,2,1,0:T(8,128)} fusion(f32[1,1,384,256]{3,2,1,0:T(8,128)S(1)} %get-tuple-element.19, f32[1,1,384,256]{3,2,1,0:T(8,128)S(1)} %bitcast.64, f32[1,1,384,256]{3,2,1,0:T(8,128)S(1)} %get-tuple-element.17, f32[1,1,384,256]{3,2,1,0:T(8,128)S(1)} %get-tuple-element.22, f32[1,1,384,256]{3,2,1,0:T(8,128)S(1)} %get-tuple-element.13, ...), kind=kLoop, calls=%fused_computation.7 | loop fusion | flops 1572864 | bytes 3932161 | tf_op jit(solution)/shard_map/min | solution.py:414
  101.1 0.6 collective-permute-done.6
  101.7 1.3 %fusion.10 = (f32[384,256]{1,0:T(8,128)S(1)}, f32[384,256]{1,0:T(8,128)S(1)}, f32[1,384,256]{2,1,0:T(8,128)S(1)}, f32[1,384,256]{2,1,0:T(8,128)S(1)}) fusion(f32[384,256]{1,0:T(8,128)S(1)} %minimum_minimum_fusion, f32[2,384,256]{2,1,0:T(8,128)} %collective-permute-done.6, pred[]{:T(512)S(6)} %eq.17, f32[2,384,256]{2,1,0:T(8,128)S(1)} %get-tuple-element.8, ...), kind=kLoop, calls=%fused_computation.26 | loop fusion | flops 786432 | bytes 3932161 | tf_op jit(solution)/shard_map/jit(_where)/select_n | solution.py:404
  103.0 1.1 %maximum_minimum_fusion = f32[2,384,256]{2,1,0:T(8,128)} fusion(f32[1,384,256]{2,1,0:T(8,128)S(1)} %get-tuple-element.23, f32[1,384,256]{2,1,0:T(8,128)S(1)} %get-tuple-element.24, f32[1,384,256]{2,1,0:T(8,128)S(1)} %get-tuple-element.18, f32[1,384,256]{2,1,0:T(8,128)S(1)} %get-tuple-element.21, f32[1,384,256]{2,1,0:T(8,128)S(1)} %get-tuple-element.20, ...), kind=kLoop, calls=%fused_computation.1 | loop fusion | flops 1376256 | bytes 3538944 | tf_op jit(solution)/shard_map/min | solution.py:420
  (3 shorter events, 0.0 us)
Async XLA Ops:
  1.5 1.1 %copy-start = (s32[2,384,256]{2,1,0:T(8,128)S(1)}, s32[2,384,256]{2,1,0:T(8,128)}, u32[]{:S(2)}) copy-start(s32[2,384,256]{2,1,0:T(8,128)} %tissue.1) | copy-start | bytes 2359300
  2.6 1.1 %copy-start.1 = (f32[2,384,256]{2,1,0:T(8,128)S(1)}, f32[2,384,256]{2,1,0:T(8,128)}, u32[]{:S(2)}) copy-start(f32[2,384,256]{2,1,0:T(8,128)} %previous.1) | copy-start | bytes 2359300
  3.7 0.7 copy-start.2
  21.6 33.6 %collective-permute-start = (f32[384,256]{1,0:T(8,128)S(1)}, f32[384,256]{1,0:T(8,128)S(1)}, u32[]{:S(2)}, u32[]{:S(2)}) collective-permute-start(f32[384,256]{1,0:T(8,128)S(1)} %get-tuple-element.6), channel_id=1, source_target_pairs={{0,64},{32,96},{64,0},{96,32},{128,192},{160,224},{192,128},{224,1... | collective-permute-start | bytes 1179656 | tf_op jit(solution)/shard_map/ppermute | solution.py:390
  23.0 32.2 %collective-permute-start.1 = (f32[384,256]{1,0:T(8,128)S(1)}, f32[384,256]{1,0:T(8,128)S(1)}, u32[]{:S(2)}, u32[]{:S(2)}) collective-permute-start(f32[384,256]{1,0:T(8,128)S(1)} %get-tuple-element.6), channel_id=1, source_target_pairs={{0,128},{32,160},{64,192},{96,224},{128,0},{160,32},{192,64},{224,... | collective-permute-start | bytes 1179656 | tf_op jit(solution)/shard_map/ppermute | solution.py:390
  25.8 29.4 %collective-permute-start.2 = (f32[384,256]{1,0:T(8,128)S(1)}, f32[384,256]{1,0:T(8,128)S(1)}, u32[]{:S(2)}, u32[]{:S(2)}) collective-permute-start(f32[384,256]{1,0:T(8,128)S(1)} %get-tuple-element.6), channel_id=1, source_target_pairs={{0,192},{32,224},{64,128},{96,160},{128,64},{160,96},{192,0},{224,... | collective-permute-start | bytes 1179656 | tf_op jit(solution)/shard_map/ppermute | solution.py:390
  51.3 6.9 %collective-permute-start.3 = (f32[384,256]{1,0:T(8,128)}, f32[384,256]{1,0:T(8,128)S(1)}, u32[]{:S(2)}, u32[]{:S(2)}) collective-permute-start(f32[384,256]{1,0:T(8,128)} %shard_map.69), channel_id=1, source_target_pairs={{0,64},{32,96},{64,0},{96,32},{128,192},{160,224},{192,128},{224,1... | collective-permute-start | bytes 1179656 | tf_op jit(solution)/shard_map/ppermute | solution.py:399
  51.4 13.5 %collective-permute-start.4 = (f32[384,256]{1,0:T(8,128)}, f32[384,256]{1,0:T(8,128)S(1)}, u32[]{:S(2)}, u32[]{:S(2)}) collective-permute-start(f32[384,256]{1,0:T(8,128)} %shard_map.69), channel_id=1, source_target_pairs={{0,128},{32,160},{64,192},{96,224},{128,0},{160,32},{192,64},{224,... | collective-permute-start | bytes 1179656 | tf_op jit(solution)/shard_map/ppermute | solution.py:399
  55.2 12.3 %collective-permute-start.5 = (f32[384,256]{1,0:T(8,128)}, f32[384,256]{1,0:T(8,128)S(1)}, u32[]{:S(2)}, u32[]{:S(2)}) collective-permute-start(f32[384,256]{1,0:T(8,128)} %shard_map.69), channel_id=1, source_target_pairs={{0,192},{32,224},{64,128},{96,160},{128,64},{160,96},{192,0},{224,... | collective-permute-start | bytes 1179656 | tf_op jit(solution)/shard_map/ppermute | solution.py:399
  55.3 44.7 %copy-start.3 = (f32[384,256]{1,0:T(8,128)S(1)}, f32[384,256]{1,0:T(8,128)}, u32[]{:S(2)}) copy-start(f32[384,256]{1,0:T(8,128)} %shard_map.69) | copy-start | bytes 1179652
  68.6 33.1 %collective-permute-start.6 = (f32[2,384,256]{2,1,0:T(8,128)S(1)}, f32[2,384,256]{2,1,0:T(8,128)}, u32[]{:S(2)}, u32[]{:S(2)}) collective-permute-start(f32[2,384,256]{2,1,0:T(8,128)S(1)} %pad_maximum_fusion), channel_id=1, source_target_pairs={{0,32},{32,0},{64,96},{96,64},{128,160},{160,128},{192,224},{224,1... | collective-permute-start | bytes 2359304 | tf_op jit(solution)/shard_map/ppermute | solution.py:400

commit v7 on v6

--- a/solution.py
+++ b/solution.py
@@ -143,8 +143,16 @@
 LINE = 8
 
 
-def relay_kernel(total_add, total_min, incoming, before, line_total, box1_in, box1_out, box2_in,
-                 box2_out, box3_in, send1, recv1, send2, recv2, send3, recv3, *, line):
+def flip_bits(value, mask, bits):
+    out = 0
+    for j in range(bits):
+        out = out + (2 ** j) * ((value // 2 ** j + (mask >> j) % 2) % 2)
+    return out
+
+
+def relay_kernel(total_add, total_min, incoming, least_in, before, line_total, box1_in, box1_out,
+                 box2_in, box2_out, box3_in, box4, send1, recv1, send2, recv2, send3, recv3, send4,
+                 recv4, *, line):
     cells_y, cells_z = incoming.shape
     chunks = cells_y // RELAY_ROWS
     slabs = lax.axis_size("slab")
@@ -165,6 +173,9 @@
     def at(c, p):
         return device(c * line + p)
 
+    orders = lax.axis_size("order")
+    masks = list(range(2, orders, 2))
+    order_bits = max(orders - 1, 1).bit_length()
     first_col = col == 0
     is_end = pos == last
     in_up = pos < half
@@ -180,6 +191,8 @@
     neighbours.append((is_end & (col > 0) & (last > 0), at(col, 0)))
     neighbours.append((is_end & (col > 0), at(col - 1, last)))
     neighbours.append((is_end & (col < lines - 1), at(col + 1, last)))
+    for m in masks:
+        neighbours.append((slab >= 0, (flip_bits(group, m, order_bits), slab)))
     count = jnp.int32(0)
     for cond, dev in neighbours:
         @pl.when(cond)
@@ -207,6 +220,15 @@
 
     def rows_of(c):
         return pl.ds(pl.multiple_of(c * RELAY_ROWS, RELAY_ROWS), RELAY_ROWS)
+
+    def copy4(c, k):
+        return pltpu.make_async_remote_copy(incoming.at[rows_of(c)], box4.at[k, c], send4.at[c, k],
+                                            recv4.at[c, k], device_id=(flip_bits(group, masks[k], order_bits), slab),
+                                            device_id_type=mesh_id)
+
+    def share(c):
+        for k in range(len(masks)):
+            copy4(c, k).start()
 
     def stage1(c, carry):
         rows = rows_of(c)
@@ -255,6 +277,7 @@
         @pl.when(is_end & first_col)
         def _():
             incoming[rows, :] = jnp.where(pos > 0, before[1, rows, :], jnp.inf)
+            share(c)
             box2_out[c] = line_total[1, rows, :]
 
         @pl.when(is_end & jnp.logical_not(first_col))
@@ -263,6 +286,7 @@
             value = box2_in[c]
             incoming[rows, :] = jnp.where(
                 pos > 0, jnp.minimum(value + before[0, rows, :], before[1, rows, :]), value)
+            share(c)
             box2_out[c] = jnp.minimum(value + line_total[0, rows, :], line_total[1, rows, :])
 
             @pl.when(pos > 0)
@@ -291,6 +315,7 @@
         @pl.when(first_col & jnp.logical_not(is_end))
         def _():
             incoming[rows, :] = jnp.where(pos > 0, before[1, rows, :], jnp.inf)
+            share(c)
 
         @pl.when(jnp.logical_not(first_col) & (in_up | in_down))
         def _():
@@ -298,6 +323,7 @@
             value = box3_in[c]
             incoming[rows, :] = jnp.where(
                 pos > 0, jnp.minimum(value + before[0, rows, :], before[1, rows, :]), value)
+            share(c)
 
             @pl.when(in_up & up_next)
             def _():
@@ -310,6 +336,17 @@
         return carry
 
     lax.fori_loop(0, chunks, stage3, 0)
+
+    def gather(c, carry):
+        rows = rows_of(c)
+        least = incoming[rows, :]
+        for k in range(len(masks)):
+            copy4(c, k).wait_recv()
+            least = jnp.minimum(least, box4[k, c])
+        least_in[rows, :] = least
+        return carry
+
+    lax.fori_loop(0, chunks, gather, 0)
 
     def drain(c, carry):
         @pl.when(pos < last)
@@ -332,23 +369,27 @@
         def _():
             copy3_relay(c, at(col, 0)).wait_send()
 
+        for k in range(len(masks)):
+            copy4(c, k).wait_send()
         return carry
 
     lax.fori_loop(0, chunks, drain, 0)
 
 
-def relay(total_add, total_min, slabs):
+def relay(total_add, total_min, slabs, orders):
     cells_y, cells_z = total_add.shape
     chunks = cells_y // RELAY_ROWS
+    sharers = len(range(2, orders, 2))
+    plane = jax.ShapeDtypeStruct(total_add.shape, jnp.float32)
     line = LINE if slabs % LINE == 0 else slabs
     vmem = pl.BlockSpec(memory_space=pltpu.VMEM)
     box = pltpu.VMEM((chunks, RELAY_ROWS, cells_z), jnp.float32)
     pair_box = pltpu.VMEM((chunks, 2, RELAY_ROWS, cells_z), jnp.float32)
     return pl.pallas_call(
         functools.partial(relay_kernel, line=line),
-        out_shape=jax.ShapeDtypeStruct(total_add.shape, jnp.float32),
+        out_shape=(plane, plane),
         in_specs=[vmem, vmem],
-        out_specs=vmem,
+        out_specs=(vmem, vmem),
         scratch_shapes=[
             pltpu.VMEM((2, cells_y, cells_z), jnp.float32),
             pltpu.VMEM((2, cells_y, cells_z), jnp.float32),
@@ -357,12 +398,15 @@
             box,
             box,
             box,
+            pltpu.VMEM((max(sharers, 1), chunks, RELAY_ROWS, cells_z), jnp.float32),
             pltpu.SemaphoreType.DMA((chunks,)),
             pltpu.SemaphoreType.DMA((chunks,)),
             pltpu.SemaphoreType.DMA((chunks,)),
             pltpu.SemaphoreType.DMA((chunks,)),
             pltpu.SemaphoreType.DMA((chunks, 2)),
             pltpu.SemaphoreType.DMA((chunks,)),
+            pltpu.SemaphoreType.DMA((chunks, max(sharers, 1))),
+            pltpu.SemaphoreType.DMA((chunks, max(sharers, 1))),
         ],
         compiler_params=pltpu.CompilerParams(collective_id=0, has_side_effects=True),
     )(total_add, total_min)
@@ -389,14 +433,11 @@
     core = group_index % 2
     gathered = [lax.ppermute(own_plane, "order", [(g, g ^ m) for g in range(orders)]) for m in partners]
 
-    incoming = relay(totals[0], totals[1], slabs)
+    incoming, least_in = relay(totals[0], totals[1], slabs, orders)
 
     least_plane = own_plane
     for got in gathered:
         least_plane = jnp.minimum(least_plane, got)
-    least_in = incoming
-    for m in partners:
-        least_in = jnp.minimum(least_in, lax.ppermute(incoming, "order", [(g, g ^ m) for g in range(orders)]))
     other = lax.ppermute(jnp.stack([least_plane, least_in]), "order", [(g, g ^ 1) for g in range(orders)])
 
     least0 = jnp.where(core == 0, least_plane, other[0])

time: 104 us -> 92.9 us (0.89)
  Pallas kernels: 41.7 us -> 55 us
  starting transfers between devices: 39.2 us -> 26.5 us
  waiting for transfers between devices: 12.7 us -> 0.01 us
    pallas_call x1, Pallas kernels: 24.5 us -> 37.9 us  [relay(): pl.pallas_call(functools.partial(relay_kernel, line=line), out_shape=(pla...]
    ppermute x3 -> x0, waiting for transfers between devices: 12.1 us -> none  [shards(): lax.ppermute(incoming, 'order', [(g, g ^ m) for g in range(orders)])]
    ppermute x1, starting transfers between devices: 31.1 us -> 22.3 us  [shards(): lax.ppermute(jnp.stack([least_plane, least_in]), 'order', [(g, g ^ 1) for...]
    ppermute x3 -> x0, starting transfers between devices: 3.94 us -> none  [shards(): lax.ppermute(incoming, 'order', [(g, g ^ m) for g in range(orders)])]
    min x1 -> x0, other arithmetic: 1.1 us -> none  [shards(): jnp.minimum(least_in, lax.ppermute(incoming, 'order', [(g, g ^ m) for g i...]
    unnamed x8 -> x10, local copies, waits for them, and re-layouts: 2.92 us -> 3.61 us
  transfers between devices with their start and end apart: 7 -> 4, of which waited for: 4 -> 0; matrix products, arithmetic and copies ran while one was open for 2% -> 2% of each run, Pallas kernels for 24% -> 41%
where the time goes in v7:
time: 92.9 us; the launch traced here: 92.5 us
  Pallas kernels  55 us (59%)
  starting transfers between devices  26.5 us (29%)
  other arithmetic  5.66 us (6%)
  local copies, waits for them, and re-layouts  4.53 us (5%)
    pallas_call x1, Pallas kernels, relay(): pl.pallas_call(functools.partial(relay_kernel, line=line), out_shape=(pla...  37.9 us
    ppermute x1, starting transfers between devices, shards(): lax.ppermute(jnp.stack([least_plane, least_in]), 'order', [(g, g ^ 1) for...  22.3 us
    pallas_call x1, Pallas kernels, local_sweeps(): pl.pallas_call(functools.partial(local_kernel, grid_step=grid_step), out_...  17.2 us
    ppermute x3, starting transfers between devices, shards(): lax.ppermute(own_plane, 'order', [(g, g ^ m) for g in range(orders)])  4.22 us
    unnamed x10, local copies, waits for them, and re-layouts  3.61 us
  transfers between devices with their start and end apart: 4, of which 0 were waited for; matrix products, arithmetic and copies ran while one was open for 2% of the time, Pallas kernels for 41%

profile of v7, /device:TPU:103, one launch (start us, length us, event | category | flops | bytes accessed | tf_op | source)
XLA Modules:
  0.0 92.5 jit_solution(8694083822091738203)
XLA Ops:
  0.7 0.7 subtract_bitcast_fusion
  1.4 0.1 pad_add_fusion.1.flags
  1.5 0.0 copy-start
  1.5 1.1 %copy-done = s32[2,384,256]{2,1,0:T(8,128)S(1)} copy-done((s32[2,384,256]{2,1,0:T(8,128)S(1)}, s32[2,384,256]{2,1,0:T(8,128)}, u32[]{:S(2)}) %copy-start) | copy-done | bytes 786456
  2.6 0.0 copy-start.1
  2.6 1.1 %copy-done.1 = f32[2,384,256]{2,1,0:T(8,128)S(1)} copy-done((f32[2,384,256]{2,1,0:T(8,128)S(1)}, f32[2,384,256]{2,1,0:T(8,128)}, u32[]{:S(2)}) %copy-start.1) | copy-done | bytes 786456
  3.7 0.0 copy-start.2
  3.7 0.7 copy-done.2
  4.4 17.2 %shard_map.68 = (f32[2,384,256]{2,1,0:T(8,128)S(1)}, f32[2,384,256]{2,1,0:T(8,128)S(1)}, f32[2,384,256]{2,1,0:T(8,128)S(1)}, f32[384,256]{1,0:T(8,128)S(1)}) custom-call(s32[3]{0:T(128)S(1)} %pad_add_fusion.1.flags, s32[3,16]{1,0:T(4,128)S(1)} %pad_add_fusion.stims, f32[16]{0:T(128)S(1)} %copy-done.2, f32[6,2,384,256]{3,2,1,0:T(8,128)} %fibre.1, ...), custom_call_target="tpu_custom_call" | custom-call | flops 58982400 | bytes 7864320 | tf_op jit(solution)/shard_map/pallas_call | solution.py:129
  21.6 1.4 %collective-permute-start = (f32[384,256]{1,0:T(8,128)S(1)}, f32[384,256]{1,0:T(8,128)S(1)}, u32[]{:S(2)}, u32[]{:S(2)}) collective-permute-start(f32[384,256]{1,0:T(8,128)S(1)} %get-tuple-element.8), channel_id=1, source_target_pairs={{0,64},{32,96},{64,0},{96,32},{128,192},{160,224},{192,128},{224,1... | collective-permute-start | bytes 1179656 | tf_op jit(solution)/shard_map/ppermute | solution.py:434
  23.0 2.8 %collective-permute-start.1 = (f32[384,256]{1,0:T(8,128)S(1)}, f32[384,256]{1,0:T(8,128)S(1)}, u32[]{:S(2)}, u32[]{:S(2)}) collective-permute-start(f32[384,256]{1,0:T(8,128)S(1)} %get-tuple-element.8), channel_id=1, source_target_pairs={{0,128},{32,160},{64,192},{96,224},{128,0},{160,32},{192,64},{224,... | collective-permute-start | bytes 1179656 | tf_op jit(solution)/shard_map/ppermute | solution.py:434
  25.8 0.0 collective-permute-start.2
  25.8 0.9 %slice_bitcast_fusion.2 = (f32[384,256]{1,0:T(8,128)}, f32[384,256]{1,0:T(8,128)}) fusion(f32[2,384,256]{2,1,0:T(8,128)S(1)} %get-tuple-element.9), kind=kLoop, calls=%fused_computation.19 | loop fusion | bytes 1572864 | tf_op jit(solution)/shard_map/squeeze | solution.py:436
  26.7 37.9 %shard_map.69 = (f32[384,256]{1,0:T(8,128)}, f32[384,256]{1,0:T(8,128)}) custom-call(f32[384,256]{1,0:T(8,128)} %get-tuple-element.30.total_add, f32[384,256]{1,0:T(8,128)} %get-tuple-element.29.total_min), custom_call_target="tpu_custom_call" | custom-call | tf_op jit(solution)/shard_map/pallas_call | solution.py:388
  64.6 0.0 collective-permute-done
  64.6 0.0 collective-permute-done.1
  64.6 0.0 collective-permute-done.2
  64.6 0.1 minimum_minimum_fusion
  64.7 1.0 %pad_maximum_fusion = f32[2,384,256]{2,1,0:T(8,128)S(1)} fusion(f32[1,384,256]{2,1,0:T(8,128)} %bitcast.66, f32[1,384,256]{2,1,0:T(8,128)S(1)} %bitcast.65), kind=kLoop, calls=%fused_computation | loop fusion | flops 196608 | bytes 1572864 | tf_op jit(solution)/shard_map/stack | solution.py:441
  65.8 0.0 copy-start.3
  65.8 22.3 %collective-permute-start.3 = (f32[2,384,256]{2,1,0:T(8,128)S(1)}, f32[2,384,256]{2,1,0:T(8,128)}, u32[]{:S(2)}, u32[]{:S(2)}) collective-permute-start(f32[2,384,256]{2,1,0:T(8,128)S(1)} %pad_maximum_fusion), channel_id=1, source_target_pairs={{0,32},{32,0},{64,96},{96,64},{128,160},{160,128},{192,224},{224,1... | collective-permute-start | bytes 2359304 | tf_op jit(solution)/shard_map/ppermute | solution.py:441
  88.1 0.0 copy-start.4
  88.1 0.3 minimum_bitcast_fusion
  88.4 0.7 copy-done.4
  89.1 1.1 %fusion.2 = f32[1,2,384,256]{3,2,1,0:T(8,128)} fusion(f32[1,1,384,256]{3,2,1,0:T(8,128)S(1)} %get-tuple-element.23, f32[1,1,384,256]{3,2,1,0:T(8,128)S(1)} %bitcast.64, f32[1,1,384,256]{3,2,1,0:T(8,128)S(1)} %get-tuple-element.21, f32[1,1,384,256]{3,2,1,0:T(8,128)S(1)} %get-tuple-element.26, f32[1,1,384,256]{3,2,1,0:T(8,128)S(1)} %get-tuple-element.17, ...), kind=kLoop, calls=%fused_computation.7 | loop fusion | flops 1572864 | bytes 3932161 | tf_op jit(solution)/shard_map/min | solution.py:455
  90.1 0.0 collective-permute-done.3
  90.2 0.0 copy-done.3
  90.2 1.3 %fusion.10 = (f32[384,256]{1,0:T(8,128)S(1)}, f32[384,256]{1,0:T(8,128)S(1)}, f32[1,384,256]{2,1,0:T(8,128)S(1)}, f32[1,384,256]{2,1,0:T(8,128)S(1)}) fusion(f32[384,256]{1,0:T(8,128)S(1)} %copy-done.3, f32[2,384,256]{2,1,0:T(8,128)} %collective-permute-done.3, pred[]{:T(512)S(6)} %eq.17, f32[2,384,256]{2,1,0:T(8,128)S(1)} %get-tuple-element.11, ...), kind=kLoop, calls=%fused_computation.25 | loop fusion | flops 786432 | bytes 3932161 | tf_op jit(solution)/shard_map/jit(_where)/select_n | solution.py:445
  91.4 1.1 %maximum_minimum_fusion = f32[2,384,256]{2,1,0:T(8,128)} fusion(f32[1,384,256]{2,1,0:T(8,128)S(1)} %get-tuple-element.27, f32[1,384,256]{2,1,0:T(8,128)S(1)} %get-tuple-element.28, f32[1,384,256]{2,1,0:T(8,128)S(1)} %get-tuple-element.22, f32[1,384,256]{2,1,0:T(8,128)S(1)} %get-tuple-element.25, f32[1,384,256]{2,1,0:T(8,128)S(1)} %get-tuple-element.24, ...), kind=kLoop, calls=%fused_computation.1 | loop fusion | flops 1376256 | bytes 3538944 | tf_op jit(solution)/shard_map/min | solution.py:461
  (1 shorter events, 0.0 us)
Async XLA Ops:
  1.5 1.1 %copy-start = (s32[2,384,256]{2,1,0:T(8,128)S(1)}, s32[2,384,256]{2,1,0:T(8,128)}, u32[]{:S(2)}) copy-start(s32[2,384,256]{2,1,0:T(8,128)} %tissue.1) | copy-start | bytes 2359300
  2.6 1.1 %copy-start.1 = (f32[2,384,256]{2,1,0:T(8,128)S(1)}, f32[2,384,256]{2,1,0:T(8,128)}, u32[]{:S(2)}) copy-start(f32[2,384,256]{2,1,0:T(8,128)} %previous.1) | copy-start | bytes 2359300
  3.7 0.7 copy-start.2
  21.6 43.0 %collective-permute-start = (f32[384,256]{1,0:T(8,128)S(1)}, f32[384,256]{1,0:T(8,128)S(1)}, u32[]{:S(2)}, u32[]{:S(2)}) collective-permute-start(f32[384,256]{1,0:T(8,128)S(1)} %get-tuple-element.8), channel_id=1, source_target_pairs={{0,64},{32,96},{64,0},{96,32},{128,192},{160,224},{192,128},{224,1... | collective-permute-start | bytes 1179656 | tf_op jit(solution)/shard_map/ppermute | solution.py:434
  23.0 41.6 %collective-permute-start.1 = (f32[384,256]{1,0:T(8,128)S(1)}, f32[384,256]{1,0:T(8,128)S(1)}, u32[]{:S(2)}, u32[]{:S(2)}) collective-permute-start(f32[384,256]{1,0:T(8,128)S(1)} %get-tuple-element.8), channel_id=1, source_target_pairs={{0,128},{32,160},{64,192},{96,224},{128,0},{160,32},{192,64},{224,... | collective-permute-start | bytes 1179656 | tf_op jit(solution)/shard_map/ppermute | solution.py:434
  25.8 38.8 %collective-permute-start.2 = (f32[384,256]{1,0:T(8,128)S(1)}, f32[384,256]{1,0:T(8,128)S(1)}, u32[]{:S(2)}, u32[]{:S(2)}) collective-permute-start(f32[384,256]{1,0:T(8,128)S(1)} %get-tuple-element.8), channel_id=1, source_target_pairs={{0,192},{32,224},{64,128},{96,160},{128,64},{160,96},{192,0},{224,... | collective-permute-start | bytes 1179656 | tf_op jit(solution)/shard_map/ppermute | solution.py:434
  65.8 24.4 %copy-start.3 = (f32[384,256]{1,0:T(8,128)S(1)}, f32[384,256]{1,0:T(8,128)}, u32[]{:S(2)}) copy-start(f32[384,256]{1,0:T(8,128)} %get-tuple-element.10) | copy-start | bytes 1179652
  65.8 24.4 %collective-permute-start.3 = (f32[2,384,256]{2,1,0:T(8,128)S(1)}, f32[2,384,256]{2,1,0:T(8,128)}, u32[]{:S(2)}, u32[]{:S(2)}) collective-permute-start(f32[2,384,256]{2,1,0:T(8,128)S(1)} %pad_maximum_fusion), channel_id=1, source_target_pairs={{0,32},{32,0},{64,96},{96,64},{128,160},{160,128},{192,224},{224,1... | collective-permute-start | bytes 2359304 | tf_op jit(solution)/shard_map/ppermute | solution.py:441
  88.1 1.0 %copy-start.4 = (f32[384,256]{1,0:T(8,128)S(1)}, f32[384,256]{1,0:T(8,128)}, u32[]{:S(2)}) copy-start(f32[384,256]{1,0:T(8,128)} %get-tuple-element.12) | copy-start | bytes 1179652

commit v8 on v7

--- a/solution.py
+++ b/solution.py
@@ -74,14 +74,15 @@
             cz = xx * yy - xy * xy
             det = xx * cx - xy * (xy * zz - yz * xz) + xz * (xy * yz - yy * xz)
             factor = jnp.where(tissue[p, rows, :] == 1, 1.0, 4.0).astype(jnp.float32) * grid_step
-            cost_x[p, rows, :] = jnp.sqrt(cx / det) * factor
-            cost_y[p, rows, :] = jnp.sqrt(cy / det) * factor
-            step_z = jnp.sqrt(cz / det) * factor
+            inverse = 1.0 / det
+            cost_x[p, rows, :] = jnp.sqrt(cx * inverse) * factor
+            cost_y[p, rows, :] = jnp.sqrt(cy * inverse) * factor
+            step_z = jnp.sqrt(cz * inverse) * factor
             _, u = block_scan(step_z, field[p, rows, :], 1, reverse, False)
             field[p, rows, :] = u
             return carry
 
-        lax.fori_loop(0, planes * chunks, body, 0)
+        lax.fori_loop(0, planes * chunks, body, 0, unroll=2)
 
     def sweep_y(reverse):
         def body(j, carry):
@@ -97,7 +98,7 @@
             return tuple(out)
 
         start = tuple(jnp.full((CHUNK, cells_z), inf, jnp.float32) for _ in range(planes))
-        lax.fori_loop(0, chunks, body, start)
+        lax.fori_loop(0, chunks, body, start, unroll=2)
 
     for flag, fn in ((flags[2], costs_and_z), (flags[1], sweep_y)):
         pl.when(flag == 1)(functools.partial(fn, True))
@@ -150,9 +151,11 @@
     return out
 
 
-def relay_kernel(total_add, total_min, incoming, least_in, before, line_total, box1_in, box1_out,
-                 box2_in, box2_out, box3_in, box4, send1, recv1, send2, recv2, send3, recv3, send4,
-                 recv4, *, line):
+def relay_kernel(totals, own, incoming, least_in, least_plane, before, line_total, box1_in,
+                 box1_out, box2_in, box2_out, box3_in, box4, box5, send1, recv1, send2, recv2, send3,
+                 recv3, send4, recv4, send5, recv5, *, line):
+    total_add = totals.at[0]
+    total_min = totals.at[1]
     cells_y, cells_z = incoming.shape
     chunks = cells_y // RELAY_ROWS
     slabs = lax.axis_size("slab")
@@ -221,6 +224,14 @@
     def rows_of(c):
         return pl.ds(pl.multiple_of(c * RELAY_ROWS, RELAY_ROWS), RELAY_ROWS)
 
+    def copy5(k):
+        return pltpu.make_async_remote_copy(own, box5.at[k], send5.at[k], recv5.at[k],
+                                            device_id=(flip_bits(group, masks[k], order_bits), slab),
+                                            device_id_type=mesh_id)
+
+    for k in range(len(masks)):
+        copy5(k).start()
+
     def copy4(c, k):
         return pltpu.make_async_remote_copy(incoming.at[rows_of(c)], box4.at[k, c], send4.at[c, k],
                                             recv4.at[c, k], device_id=(flip_bits(group, masks[k], order_bits), slab),
@@ -348,6 +359,19 @@
 
     lax.fori_loop(0, chunks, gather, 0)
 
+    for k in range(len(masks)):
+        copy5(k).wait_recv()
+
+    def gather_plane(c, carry):
+        rows = rows_of(c)
+        least = own[rows, :]
+        for k in range(len(masks)):
+            least = jnp.minimum(least, box5[k, rows, :])
+        least_plane[rows, :] = least
+        return carry
+
+    lax.fori_loop(0, chunks, gather_plane, 0)
+
     def drain(c, carry):
         @pl.when(pos < last)
         def _():
@@ -374,22 +398,24 @@
         return carry
 
     lax.fori_loop(0, chunks, drain, 0)
-
-
-def relay(total_add, total_min, slabs, orders):
-    cells_y, cells_z = total_add.shape
+    for k in range(len(masks)):
+        copy5(k).wait_send()
+
+
+def relay(totals, own, slabs, orders):
+    cells_y, cells_z = own.shape
     chunks = cells_y // RELAY_ROWS
     sharers = len(range(2, orders, 2))
-    plane = jax.ShapeDtypeStruct(total_add.shape, jnp.float32)
+    plane = jax.ShapeDtypeStruct(own.shape, jnp.float32)
     line = LINE if slabs % LINE == 0 else slabs
     vmem = pl.BlockSpec(memory_space=pltpu.VMEM)
     box = pltpu.VMEM((chunks, RELAY_ROWS, cells_z), jnp.float32)
     pair_box = pltpu.VMEM((chunks, 2, RELAY_ROWS, cells_z), jnp.float32)
     return pl.pallas_call(
         functools.partial(relay_kernel, line=line),
-        out_shape=(plane, plane),
+        out_shape=(plane, plane, plane),
         in_specs=[vmem, vmem],
-        out_specs=(vmem, vmem),
+        out_specs=(vmem, vmem, vmem),
         scratch_shapes=[
             pltpu.VMEM((2, cells_y, cells_z), jnp.float32),
             pltpu.VMEM((2, cells_y, cells_z), jnp.float32),
@@ -399,6 +425,7 @@
             box,
             box,
             pltpu.VMEM((max(sharers, 1), chunks, RELAY_ROWS, cells_z), jnp.float32),
+            pltpu.VMEM((max(sharers, 1), cells_y, cells_z), jnp.float32),
             pltpu.SemaphoreType.DMA((chunks,)),
             pltpu.SemaphoreType.DMA((chunks,)),
             pltpu.SemaphoreType.DMA((chunks,)),
@@ -407,9 +434,11 @@
             pltpu.SemaphoreType.DMA((chunks,)),
             pltpu.SemaphoreType.DMA((chunks, max(sharers, 1))),
             pltpu.SemaphoreType.DMA((chunks, max(sharers, 1))),
+            pltpu.SemaphoreType.DMA((max(sharers, 1),)),
+            pltpu.SemaphoreType.DMA((max(sharers, 1),)),
         ],
         compiler_params=pltpu.CompilerParams(collective_id=0, has_side_effects=True),
-    )(total_add, total_min)
+    )(totals, own)
 
 
 def shards(previous, fibre_tensor, tissue, stim_sites, stim_times):
@@ -429,15 +458,8 @@
     cost_x, field, totals, own_plane = local_sweeps(
         bits, stims, stim_times, fibre_tensor, tissue, previous, grid_step)
 
-    partners = [m for m in range(2, orders, 2)]
     core = group_index % 2
-    gathered = [lax.ppermute(own_plane, "order", [(g, g ^ m) for g in range(orders)]) for m in partners]
-
-    incoming, least_in = relay(totals[0], totals[1], slabs, orders)
-
-    least_plane = own_plane
-    for got in gathered:
-        least_plane = jnp.minimum(least_plane, got)
+    incoming, least_in, least_plane = relay(totals, own_plane, slabs, orders)
     other = lax.ppermute(jnp.stack([least_plane, least_in]), "order", [(g, g ^ 1) for g in range(orders)])
 
     least0 = jnp.where(core == 0, least_plane, other[0])

time: 92.9 us -> 89.6 us (0.964)
  starting transfers between devices: 26.5 us -> 21.7 us
    ppermute x3 -> x0, starting transfers between devices: 4.22 us -> none  [shards(): lax.ppermute(own_plane, 'order', [(g, g ^ m) for g in range(orders)])]
    unnamed x10 -> x16, local copies, waits for them, and re-layouts: 3.61 us -> 4.55 us
  transfers between devices with their start and end apart: 4 -> 1, of which waited for: 0 -> 1; matrix products, arithmetic and copies ran while one was open for 2% -> 2% of each run, Pallas kernels for 41% -> 0%
where the time goes in v8:
time: 89.6 us; the launch traced here: 89.3 us
  Pallas kernels  55.9 us (62%)
  starting transfers between devices  21.7 us (24%)
  other arithmetic  5.73 us (6%)
  local copies, waits for them, and re-layouts  4.55 us (5%)
    pallas_call x1, Pallas kernels, relay(): pl.pallas_call(functools.partial(relay_kernel, line=line), out_shape=(pla...  38.7 us
    ppermute x1, starting transfers between devices, shards(): lax.ppermute(jnp.stack([least_plane, least_in]), 'order', [(g, g ^ 1) for...  21.7 us
    pallas_call x1, Pallas kernels, local_sweeps(): pl.pallas_call(functools.partial(local_kernel, grid_step=grid_step), out_...  17.3 us
    unnamed x16, local copies, waits for them, and re-layouts  4.55 us
  transfers between devices with their start and end apart: 1, of which 1 were waited for; matrix products, arithmetic and copies ran while one was open for 2% of the time, Pallas kernels for 0%

profile of v8, /device:TPU:103, one launch (start us, length us, event | category | flops | bytes accessed | tf_op | source)
XLA Modules:
  0.0 89.3 jit_solution(6029958792819016961)
XLA Ops:
  0.7 0.7 subtract_bitcast_fusion
  1.4 0.1 pad_add_fusion.1.flags
  1.5 0.0 copy-start
  1.5 1.1 %copy-done = s32[2,384,256]{2,1,0:T(8,128)S(1)} copy-done((s32[2,384,256]{2,1,0:T(8,128)S(1)}, s32[2,384,256]{2,1,0:T(8,128)}, u32[]{:S(2)}) %copy-start) | copy-done | bytes 786456
  2.6 0.0 copy-start.1
  2.6 1.1 %copy-done.1 = f32[2,384,256]{2,1,0:T(8,128)S(1)} copy-done((f32[2,384,256]{2,1,0:T(8,128)S(1)}, f32[2,384,256]{2,1,0:T(8,128)}, u32[]{:S(2)}) %copy-start.1) | copy-done | bytes 786456
  3.7 0.0 copy-start.4
  3.7 0.7 copy-done.4
  4.4 17.3 %shard_map.68 = (f32[2,384,256]{2,1,0:T(8,128)S(1)}, f32[2,384,256]{2,1,0:T(8,128)S(1)}, f32[2,384,256]{2,1,0:T(8,128)S(1)}, f32[384,256]{1,0:T(8,128)S(1)}) custom-call(s32[3]{0:T(128)S(1)} %pad_add_fusion.1.flags, s32[3,16]{1,0:T(4,128)S(1)} %pad_add_fusion.stims, f32[16]{0:T(128)S(1)} %copy-done.4, f32[6,2,384,256]{3,2,1,0:T(8,128)} %fibre.1, ...), custom_call_target="tpu_custom_call" | custom-call | flops 58982400 | bytes 7864320 | tf_op jit(solution)/shard_map/pallas_call | solution.py:130
  21.7 0.0 copy-start.2
  21.7 0.9 copy-done.2
  22.6 0.0 copy-start.3
  22.6 0.7 copy-done.3
  23.3 38.7 %shard_map.69 = (f32[384,256]{1,0:T(8,128)}, f32[384,256]{1,0:T(8,128)}, f32[384,256]{1,0:T(8,128)}) custom-call(f32[2,384,256]{2,1,0:T(8,128)} %copy-done.2, f32[384,256]{1,0:T(8,128)} %copy-done.3), custom_call_target="tpu_custom_call" | custom-call | tf_op jit(solution)/shard_map/pallas_call | solution.py:414
  62.0 0.0 copy-start.7
  62.0 1.2 %pad_maximum_fusion = f32[2,384,256]{2,1,0:T(8,128)S(1)} fusion(f32[1,384,256]{2,1,0:T(8,128)} %bitcast.61, f32[1,384,256]{2,1,0:T(8,128)} %bitcast.62), kind=kLoop, calls=%fused_computation | loop fusion | flops 196608 | bytes 1572864 | tf_op jit(solution)/shard_map/stack | solution.py:463
  63.2 0.0 copy-start.5
  63.2 0.0 copy-start.6
  63.2 21.7 %collective-permute-start = (f32[2,384,256]{2,1,0:T(8,128)S(1)}, f32[2,384,256]{2,1,0:T(8,128)}, u32[]{:S(2)}, u32[]{:S(2)}) collective-permute-start(f32[2,384,256]{2,1,0:T(8,128)S(1)} %pad_maximum_fusion), channel_id=1, source_target_pairs={{0,32},{32,0},{64,96},{96,64},{128,160},{160,128},{192,224},{224,1... | collective-permute-start | bytes 2359304 | tf_op jit(solution)/shard_map/ppermute | solution.py:463
  84.9 0.3 minimum_bitcast_fusion
  85.2 0.0 copy-done.7
  85.2 1.1 %fusion.2 = f32[1,2,384,256]{3,2,1,0:T(8,128)} fusion(f32[1,1,384,256]{3,2,1,0:T(8,128)S(1)} %get-tuple-element.25, f32[1,1,384,256]{3,2,1,0:T(8,128)S(1)} %bitcast.60, f32[1,1,384,256]{3,2,1,0:T(8,128)S(1)} %get-tuple-element.23, f32[1,1,384,256]{3,2,1,0:T(8,128)S(1)} %get-tuple-element.28, f32[1,1,384,256]{3,2,1,0:T(8,128)S(1)} %get-tuple-element.19, ...), kind=kLoop, calls=%fused_computation.7 | loop fusion | flops 1572864 | bytes 3932161 | tf_op jit(solution)/shard_map/min | solution.py:477
  86.3 0.6 collective-permute-done
  86.9 0.0 copy-done.5
  86.9 0.0 copy-done.6
  86.9 1.3 %fusion.10 = (f32[384,256]{1,0:T(8,128)S(1)}, f32[384,256]{1,0:T(8,128)S(1)}, f32[1,384,256]{2,1,0:T(8,128)S(1)}, f32[1,384,256]{2,1,0:T(8,128)S(1)}) fusion(f32[384,256]{1,0:T(8,128)S(1)} %copy-done.5, f32[2,384,256]{2,1,0:T(8,128)} %collective-permute-done, pred[]{:T(512)S(6)} %eq.17, f32[2,384,256]{2,1,0:T(8,128)S(1)} %get-tuple-element.13, ...), kind=kLoop, calls=%fused_computation.22 | loop fusion | flops 786432 | bytes 3932161 | tf_op jit(solution)/shard_map/jit(_where)/select_n | solution.py:467
  88.2 1.1 %maximum_minimum_fusion = f32[2,384,256]{2,1,0:T(8,128)} fusion(f32[1,384,256]{2,1,0:T(8,128)S(1)} %get-tuple-element.29, f32[1,384,256]{2,1,0:T(8,128)S(1)} %get-tuple-element.30, f32[1,384,256]{2,1,0:T(8,128)S(1)} %get-tuple-element.24, f32[1,384,256]{2,1,0:T(8,128)S(1)} %get-tuple-element.27, f32[1,384,256]{2,1,0:T(8,128)S(1)} %get-tuple-element.26, ...), kind=kLoop, calls=%fused_computation.1 | loop fusion | flops 1376256 | bytes 3538944 | tf_op jit(solution)/shard_map/min | solution.py:483
  (1 shorter events, 0.0 us)
Async XLA Ops:
  1.5 1.1 %copy-start = (s32[2,384,256]{2,1,0:T(8,128)S(1)}, s32[2,384,256]{2,1,0:T(8,128)}, u32[]{:S(2)}) copy-start(s32[2,384,256]{2,1,0:T(8,128)} %tissue.1) | copy-start | bytes 2359300
  2.6 1.1 %copy-start.1 = (f32[2,384,256]{2,1,0:T(8,128)S(1)}, f32[2,384,256]{2,1,0:T(8,128)}, u32[]{:S(2)}) copy-start(f32[2,384,256]{2,1,0:T(8,128)} %previous.1) | copy-start | bytes 2359300
  3.7 0.7 copy-start.4
  21.7 0.9 copy-start.2
  22.6 0.7 copy-start.3
  62.0 23.2 %copy-start.7 = (f32[384,256]{1,0:T(8,128)S(1)}, f32[384,256]{1,0:T(8,128)}, u32[]{:S(2)}) copy-start(f32[384,256]{1,0:T(8,128)} %get-tuple-element.14) | copy-start | bytes 1179652
  63.2 23.7 %copy-start.5 = (f32[384,256]{1,0:T(8,128)S(1)}, f32[384,256]{1,0:T(8,128)}, u32[]{:S(2)}) copy-start(f32[384,256]{1,0:T(8,128)} %get-tuple-element.12) | copy-start | bytes 1179652
  63.2 23.7 %copy-start.6 = (f32[384,256]{1,0:T(8,128)S(1)}, f32[384,256]{1,0:T(8,128)}, u32[]{:S(2)}) copy-start(f32[384,256]{1,0:T(8,128)} %get-tuple-element.11) | copy-start | bytes 1179652
  63.2 23.7 %collective-permute-start = (f32[2,384,256]{2,1,0:T(8,128)S(1)}, f32[2,384,256]{2,1,0:T(8,128)}, u32[]{:S(2)}, u32[]{:S(2)}) collective-permute-start(f32[2,384,256]{2,1,0:T(8,128)S(1)} %pad_maximum_fusion), channel_id=1, source_target_pairs={{0,32},{32,0},{64,96},{96,64},{128,160},{160,128},{192,224},{224,1... | collective-permute-start | bytes 2359304 | tf_op jit(solution)/shard_map/ppermute | solution.py:463

commit v9 on v8

--- a/solution.py
+++ b/solution.py
@@ -140,7 +140,7 @@
     )(flags, stims, stim_times, fibre, tissue, previous)
 
 
-RELAY_ROWS = 16
+RELAY_ROWS = 8
 LINE = 8
 
 

time: 89.6 us -> 91.2 us (1.018)
  Pallas kernels: 55.9 us -> 58.8 us
  starting transfers between devices: 21.7 us -> 20.4 us
    pallas_call x1, Pallas kernels: 38.7 us -> 41.5 us  [relay(): pl.pallas_call(functools.partial(relay_kernel, line=line), out_shape=(pla...]
    ppermute x1, starting transfers between devices: 21.7 us -> 20.4 us  [shards(): lax.ppermute(jnp.stack([least_plane, least_in]), 'order', [(g, g ^ 1) for...]
where the time goes in v9:
time: 91.2 us; the launch traced here: 90.9 us
  Pallas kernels  58.8 us (64%)
  starting transfers between devices  20.4 us (22%)
  other arithmetic  5.73 us (6%)
  local copies, waits for them, and re-layouts  4.55 us (5%)
    pallas_call x1, Pallas kernels, relay(): pl.pallas_call(functools.partial(relay_kernel, line=line), out_shape=(pla...  41.5 us
    ppermute x1, starting transfers between devices, shards(): lax.ppermute(jnp.stack([least_plane, least_in]), 'order', [(g, g ^ 1) for...  20.4 us
    pallas_call x1, Pallas kernels, local_sweeps(): pl.pallas_call(functools.partial(local_kernel, grid_step=grid_step), out_...  17.3 us
    unnamed x16, local copies, waits for them, and re-layouts  4.55 us
  transfers between devices with their start and end apart: 1, of which 1 were waited for; matrix products, arithmetic and copies ran while one was open for 2% of the time, Pallas kernels for 0%

profile of v9, /device:TPU:103, one launch (start us, length us, event | category | flops | bytes accessed | tf_op | source)
XLA Modules:
  0.0 90.9 jit_solution(326569789186431018)
XLA Ops:
  0.7 0.7 subtract_bitcast_fusion
  1.4 0.1 pad_add_fusion.1.flags
  1.5 0.0 copy-start
  1.5 1.1 %copy-done = s32[2,384,256]{2,1,0:T(8,128)S(1)} copy-done((s32[2,384,256]{2,1,0:T(8,128)S(1)}, s32[2,384,256]{2,1,0:T(8,128)}, u32[]{:S(2)}) %copy-start) | copy-done | bytes 786456
  2.6 0.0 copy-start.1
  2.6 1.1 %copy-done.1 = f32[2,384,256]{2,1,0:T(8,128)S(1)} copy-done((f32[2,384,256]{2,1,0:T(8,128)S(1)}, f32[2,384,256]{2,1,0:T(8,128)}, u32[]{:S(2)}) %copy-start.1) | copy-done | bytes 786456
  3.7 0.0 copy-start.4
  3.7 0.7 copy-done.4
  4.4 17.3 %shard_map.68 = (f32[2,384,256]{2,1,0:T(8,128)S(1)}, f32[2,384,256]{2,1,0:T(8,128)S(1)}, f32[2,384,256]{2,1,0:T(8,128)S(1)}, f32[384,256]{1,0:T(8,128)S(1)}) custom-call(s32[3]{0:T(128)S(1)} %pad_add_fusion.1.flags, s32[3,16]{1,0:T(4,128)S(1)} %pad_add_fusion.stims, f32[16]{0:T(128)S(1)} %copy-done.4, f32[6,2,384,256]{3,2,1,0:T(8,128)} %fibre.1, ...), custom_call_target="tpu_custom_call" | custom-call | flops 58982400 | bytes 7864320 | tf_op jit(solution)/shard_map/pallas_call | solution.py:130
  21.7 0.0 copy-start.2
  21.7 0.9 copy-done.2
  22.6 0.0 copy-start.3
  22.6 0.7 copy-done.3
  23.3 41.5 %shard_map.69 = (f32[384,256]{1,0:T(8,128)}, f32[384,256]{1,0:T(8,128)}, f32[384,256]{1,0:T(8,128)}) custom-call(f32[2,384,256]{2,1,0:T(8,128)} %copy-done.2, f32[384,256]{1,0:T(8,128)} %copy-done.3), custom_call_target="tpu_custom_call" | custom-call | tf_op jit(solution)/shard_map/pallas_call | solution.py:414
  64.8 0.0 copy-start.7
  64.9 1.2 %pad_maximum_fusion = f32[2,384,256]{2,1,0:T(8,128)S(1)} fusion(f32[1,384,256]{2,1,0:T(8,128)} %bitcast.61, f32[1,384,256]{2,1,0:T(8,128)} %bitcast.62), kind=kLoop, calls=%fused_computation | loop fusion | flops 196608 | bytes 1572864 | tf_op jit(solution)/shard_map/stack | solution.py:463
  66.1 0.0 copy-start.5
  66.1 0.0 copy-start.6
  66.1 20.4 %collective-permute-start = (f32[2,384,256]{2,1,0:T(8,128)S(1)}, f32[2,384,256]{2,1,0:T(8,128)}, u32[]{:S(2)}, u32[]{:S(2)}) collective-permute-start(f32[2,384,256]{2,1,0:T(8,128)S(1)} %pad_maximum_fusion), channel_id=1, source_target_pairs={{0,32},{32,0},{64,96},{96,64},{128,160},{160,128},{192,224},{224,1... | collective-permute-start | bytes 2359304 | tf_op jit(solution)/shard_map/ppermute | solution.py:463
  86.5 0.3 minimum_bitcast_fusion
  86.8 0.0 copy-done.7
  86.8 1.1 %fusion.2 = f32[1,2,384,256]{3,2,1,0:T(8,128)} fusion(f32[1,1,384,256]{3,2,1,0:T(8,128)S(1)} %get-tuple-element.25, f32[1,1,384,256]{3,2,1,0:T(8,128)S(1)} %bitcast.60, f32[1,1,384,256]{3,2,1,0:T(8,128)S(1)} %get-tuple-element.23, f32[1,1,384,256]{3,2,1,0:T(8,128)S(1)} %get-tuple-element.28, f32[1,1,384,256]{3,2,1,0:T(8,128)S(1)} %get-tuple-element.19, ...), kind=kLoop, calls=%fused_computation.7 | loop fusion | flops 1572864 | bytes 3932161 | tf_op jit(solution)/shard_map/min | solution.py:477
  87.9 0.6 collective-permute-done
  88.5 0.0 copy-done.5
  88.5 0.0 copy-done.6
  88.5 1.3 %fusion.10 = (f32[384,256]{1,0:T(8,128)S(1)}, f32[384,256]{1,0:T(8,128)S(1)}, f32[1,384,256]{2,1,0:T(8,128)S(1)}, f32[1,384,256]{2,1,0:T(8,128)S(1)}) fusion(f32[384,256]{1,0:T(8,128)S(1)} %copy-done.5, f32[2,384,256]{2,1,0:T(8,128)} %collective-permute-done, pred[]{:T(512)S(6)} %eq.17, f32[2,384,256]{2,1,0:T(8,128)S(1)} %get-tuple-element.13, ...), kind=kLoop, calls=%fused_computation.22 | loop fusion | flops 786432 | bytes 3932161 | tf_op jit(solution)/shard_map/jit(_where)/select_n | solution.py:467
  89.8 1.1 %maximum_minimum_fusion = f32[2,384,256]{2,1,0:T(8,128)} fusion(f32[1,384,256]{2,1,0:T(8,128)S(1)} %get-tuple-element.29, f32[1,384,256]{2,1,0:T(8,128)S(1)} %get-tuple-element.30, f32[1,384,256]{2,1,0:T(8,128)S(1)} %get-tuple-element.24, f32[1,384,256]{2,1,0:T(8,128)S(1)} %get-tuple-element.27, f32[1,384,256]{2,1,0:T(8,128)S(1)} %get-tuple-element.26, ...), kind=kLoop, calls=%fused_computation.1 | loop fusion | flops 1376256 | bytes 3538944 | tf_op jit(solution)/shard_map/min | solution.py:483
  (1 shorter events, 0.0 us)
Async XLA Ops:
  1.5 1.1 %copy-start = (s32[2,384,256]{2,1,0:T(8,128)S(1)}, s32[2,384,256]{2,1,0:T(8,128)}, u32[]{:S(2)}) copy-start(s32[2,384,256]{2,1,0:T(8,128)} %tissue.1) | copy-start | bytes 2359300
  2.6 1.1 %copy-start.1 = (f32[2,384,256]{2,1,0:T(8,128)S(1)}, f32[2,384,256]{2,1,0:T(8,128)}, u32[]{:S(2)}) copy-start(f32[2,384,256]{2,1,0:T(8,128)} %previous.1) | copy-start | bytes 2359300
  3.7 0.7 copy-start.4
  21.7 0.9 copy-start.2
  22.6 0.7 copy-start.3
  64.8 22.0 %copy-start.7 = (f32[384,256]{1,0:T(8,128)S(1)}, f32[384,256]{1,0:T(8,128)}, u32[]{:S(2)}) copy-start(f32[384,256]{1,0:T(8,128)} %get-tuple-element.14) | copy-start | bytes 1179652
  66.1 22.5 %copy-start.5 = (f32[384,256]{1,0:T(8,128)S(1)}, f32[384,256]{1,0:T(8,128)}, u32[]{:S(2)}) copy-start(f32[384,256]{1,0:T(8,128)} %get-tuple-element.12) | copy-start | bytes 1179652
  66.1 22.4 %copy-start.6 = (f32[384,256]{1,0:T(8,128)S(1)}, f32[384,256]{1,0:T(8,128)}, u32[]{:S(2)}) copy-start(f32[384,256]{1,0:T(8,128)} %get-tuple-element.11) | copy-start | bytes 1179652
  66.1 22.4 %collective-permute-start = (f32[2,384,256]{2,1,0:T(8,128)S(1)}, f32[2,384,256]{2,1,0:T(8,128)}, u32[]{:S(2)}, u32[]{:S(2)}) collective-permute-start(f32[2,384,256]{2,1,0:T(8,128)S(1)} %pad_maximum_fusion), channel_id=1, source_target_pairs={{0,32},{32,0},{64,96},{96,64},{128,160},{160,128},{192,224},{224,1... | collective-permute-start | bytes 2359304 | tf_op jit(solution)/shard_map/ppermute | solution.py:463

commit v10 on v9

--- a/solution.py
+++ b/solution.py
@@ -140,7 +140,7 @@
     )(flags, stims, stim_times, fibre, tissue, previous)
 
 
-RELAY_ROWS = 8
+RELAY_ROWS = 32
 LINE = 8
 
 

time: 91.2 us -> 91.4 us (level)
  starting transfers between devices: 20.4 us -> 24.3 us
  Pallas kernels: 58.8 us -> 55.2 us
    ppermute x1, starting transfers between devices: 20.4 us -> 24.3 us  [shards(): lax.ppermute(jnp.stack([least_plane, least_in]), 'order', [(g, g ^ 1) for...]
    pallas_call x1, Pallas kernels: 41.5 us -> 37.9 us  [relay(): pl.pallas_call(functools.partial(relay_kernel, line=line), out_shape=(pla...]
where the time goes in v10:
time: 91.4 us; the launch traced here: 91.2 us
  Pallas kernels  55.2 us (60%)
  starting transfers between devices  24.3 us (27%)
  other arithmetic  5.73 us (6%)
  local copies, waits for them, and re-layouts  4.55 us (5%)
    pallas_call x1, Pallas kernels, relay(): pl.pallas_call(functools.partial(relay_kernel, line=line), out_shape=(pla...  37.9 us
    ppermute x1, starting transfers between devices, shards(): lax.ppermute(jnp.stack([least_plane, least_in]), 'order', [(g, g ^ 1) for...  24.3 us
    pallas_call x1, Pallas kernels, local_sweeps(): pl.pallas_call(functools.partial(local_kernel, grid_step=grid_step), out_...  17.3 us
    unnamed x16, local copies, waits for them, and re-layouts  4.55 us
  transfers between devices with their start and end apart: 1, of which 1 were waited for; matrix products, arithmetic and copies ran while one was open for 2% of the time, Pallas kernels for 0%

profile of v10, /device:TPU:103, one launch (start us, length us, event | category | flops | bytes accessed | tf_op | source)
XLA Modules:
  0.0 91.2 jit_solution(2697405067291255287)
XLA Ops:
  0.7 0.7 subtract_bitcast_fusion
  1.4 0.1 pad_add_fusion.1.flags
  1.5 0.0 copy-start
  1.5 1.1 %copy-done = s32[2,384,256]{2,1,0:T(8,128)S(1)} copy-done((s32[2,384,256]{2,1,0:T(8,128)S(1)}, s32[2,384,256]{2,1,0:T(8,128)}, u32[]{:S(2)}) %copy-start) | copy-done | bytes 786456
  2.6 0.0 copy-start.1
  2.6 1.1 %copy-done.1 = f32[2,384,256]{2,1,0:T(8,128)S(1)} copy-done((f32[2,384,256]{2,1,0:T(8,128)S(1)}, f32[2,384,256]{2,1,0:T(8,128)}, u32[]{:S(2)}) %copy-start.1) | copy-done | bytes 786456
  3.7 0.0 copy-start.4
  3.7 0.7 copy-done.4
  4.4 17.3 %shard_map.68 = (f32[2,384,256]{2,1,0:T(8,128)S(1)}, f32[2,384,256]{2,1,0:T(8,128)S(1)}, f32[2,384,256]{2,1,0:T(8,128)S(1)}, f32[384,256]{1,0:T(8,128)S(1)}) custom-call(s32[3]{0:T(128)S(1)} %pad_add_fusion.1.flags, s32[3,16]{1,0:T(4,128)S(1)} %pad_add_fusion.stims, f32[16]{0:T(128)S(1)} %copy-done.4, f32[6,2,384,256]{3,2,1,0:T(8,128)} %fibre.1, ...), custom_call_target="tpu_custom_call" | custom-call | flops 58982400 | bytes 7864320 | tf_op jit(solution)/shard_map/pallas_call | solution.py:130
  21.7 0.0 copy-start.2
  21.7 0.9 copy-done.2
  22.6 0.0 copy-start.3
  22.6 0.7 copy-done.3
  23.3 37.9 %shard_map.69 = (f32[384,256]{1,0:T(8,128)}, f32[384,256]{1,0:T(8,128)}, f32[384,256]{1,0:T(8,128)}) custom-call(f32[2,384,256]{2,1,0:T(8,128)} %copy-done.2, f32[384,256]{1,0:T(8,128)} %copy-done.3), custom_call_target="tpu_custom_call" | custom-call | tf_op jit(solution)/shard_map/pallas_call | solution.py:414
  61.2 0.0 copy-start.7
  61.2 1.2 %pad_maximum_fusion = f32[2,384,256]{2,1,0:T(8,128)S(1)} fusion(f32[1,384,256]{2,1,0:T(8,128)} %bitcast.61, f32[1,384,256]{2,1,0:T(8,128)} %bitcast.62), kind=kLoop, calls=%fused_computation | loop fusion | flops 196608 | bytes 1572864 | tf_op jit(solution)/shard_map/stack | solution.py:463
  62.5 0.0 copy-start.5
  62.5 0.0 copy-start.6
  62.5 24.3 %collective-permute-start = (f32[2,384,256]{2,1,0:T(8,128)S(1)}, f32[2,384,256]{2,1,0:T(8,128)}, u32[]{:S(2)}, u32[]{:S(2)}) collective-permute-start(f32[2,384,256]{2,1,0:T(8,128)S(1)} %pad_maximum_fusion), channel_id=1, source_target_pairs={{0,32},{32,0},{64,96},{96,64},{128,160},{160,128},{192,224},{224,1... | collective-permute-start | bytes 2359304 | tf_op jit(solution)/shard_map/ppermute | solution.py:463
  86.8 0.3 minimum_bitcast_fusion
  87.1 0.0 copy-done.7
  87.1 1.1 %fusion.2 = f32[1,2,384,256]{3,2,1,0:T(8,128)} fusion(f32[1,1,384,256]{3,2,1,0:T(8,128)S(1)} %get-tuple-element.25, f32[1,1,384,256]{3,2,1,0:T(8,128)S(1)} %bitcast.60, f32[1,1,384,256]{3,2,1,0:T(8,128)S(1)} %get-tuple-element.23, f32[1,1,384,256]{3,2,1,0:T(8,128)S(1)} %get-tuple-element.28, f32[1,1,384,256]{3,2,1,0:T(8,128)S(1)} %get-tuple-element.19, ...), kind=kLoop, calls=%fused_computation.7 | loop fusion | flops 1572864 | bytes 3932161 | tf_op jit(solution)/shard_map/min | solution.py:477
  88.2 0.6 collective-permute-done
  88.8 0.0 copy-done.5
  88.8 0.0 copy-done.6
  88.8 1.3 %fusion.10 = (f32[384,256]{1,0:T(8,128)S(1)}, f32[384,256]{1,0:T(8,128)S(1)}, f32[1,384,256]{2,1,0:T(8,128)S(1)}, f32[1,384,256]{2,1,0:T(8,128)S(1)}) fusion(f32[384,256]{1,0:T(8,128)S(1)} %copy-done.5, f32[2,384,256]{2,1,0:T(8,128)} %collective-permute-done, pred[]{:T(512)S(6)} %eq.17, f32[2,384,256]{2,1,0:T(8,128)S(1)} %get-tuple-element.13, ...), kind=kLoop, calls=%fused_computation.22 | loop fusion | flops 786432 | bytes 3932161 | tf_op jit(solution)/shard_map/jit(_where)/select_n | solution.py:467
  90.1 1.1 %maximum_minimum_fusion = f32[2,384,256]{2,1,0:T(8,128)} fusion(f32[1,384,256]{2,1,0:T(8,128)S(1)} %get-tuple-element.29, f32[1,384,256]{2,1,0:T(8,128)S(1)} %get-tuple-element.30, f32[1,384,256]{2,1,0:T(8,128)S(1)} %get-tuple-element.24, f32[1,384,256]{2,1,0:T(8,128)S(1)} %get-tuple-element.27, f32[1,384,256]{2,1,0:T(8,128)S(1)} %get-tuple-element.26, ...), kind=kLoop, calls=%fused_computation.1 | loop fusion | flops 1376256 | bytes 3538944 | tf_op jit(solution)/shard_map/min | solution.py:483
  (1 shorter events, 0.0 us)
Async XLA Ops:
  1.5 1.1 %copy-start = (s32[2,384,256]{2,1,0:T(8,128)S(1)}, s32[2,384,256]{2,1,0:T(8,128)}, u32[]{:S(2)}) copy-start(s32[2,384,256]{2,1,0:T(8,128)} %tissue.1) | copy-start | bytes 2359300
  2.6 1.1 %copy-start.1 = (f32[2,384,256]{2,1,0:T(8,128)S(1)}, f32[2,384,256]{2,1,0:T(8,128)}, u32[]{:S(2)}) copy-start(f32[2,384,256]{2,1,0:T(8,128)} %previous.1) | copy-start | bytes 2359300
  3.7 0.7 copy-start.4
  21.7 0.9 copy-start.2
  22.6 0.7 copy-start.3
  61.2 25.9 %copy-start.7 = (f32[384,256]{1,0:T(8,128)S(1)}, f32[384,256]{1,0:T(8,128)}, u32[]{:S(2)}) copy-start(f32[384,256]{1,0:T(8,128)} %get-tuple-element.14) | copy-start | bytes 1179652
  62.5 26.4 %copy-start.5 = (f32[384,256]{1,0:T(8,128)S(1)}, f32[384,256]{1,0:T(8,128)}, u32[]{:S(2)}) copy-start(f32[384,256]{1,0:T(8,128)} %get-tuple-element.12) | copy-start | bytes 1179652
  62.5 26.4 %copy-start.6 = (f32[384,256]{1,0:T(8,128)S(1)}, f32[384,256]{1,0:T(8,128)}, u32[]{:S(2)}) copy-start(f32[384,256]{1,0:T(8,128)} %get-tuple-element.11) | copy-start | bytes 1179652
  62.5 26.3 %collective-permute-start = (f32[2,384,256]{2,1,0:T(8,128)S(1)}, f32[2,384,256]{2,1,0:T(8,128)}, u32[]{:S(2)}, u32[]{:S(2)}) collective-permute-start(f32[2,384,256]{2,1,0:T(8,128)S(1)} %pad_maximum_fusion), channel_id=1, source_target_pairs={{0,32},{32,0},{64,96},{96,64},{128,160},{160,128},{192,224},{224,1... | collective-permute-start | bytes 2359304 | tf_op jit(solution)/shard_map/ppermute | solution.py:463

commit v11 on v8

--- a/solution.py
+++ b/solution.py
@@ -151,9 +151,10 @@
     return out
 
 
-def relay_kernel(totals, own, incoming, least_in, least_plane, before, line_total, box1_in,
-                 box1_out, box2_in, box2_out, box3_in, box4, box5, send1, recv1, send2, recv2, send3,
-                 recv3, send4, recv4, send5, recv5, *, line):
+def relay_kernel(totals, own, cost_x, field, sweep_field, merged, incoming, least_in, least_plane,
+                 before, line_total, box1_in, box1_out, box2_in, box2_out, box3_in, box4, box5,
+                 swap_in, send1, recv1, send2, recv2, send3, recv3, send4, recv4, send5, recv5,
+                 send6, recv6, *, line):
     total_add = totals.at[0]
     total_min = totals.at[1]
     cells_y, cells_z = incoming.shape
@@ -194,7 +195,7 @@
     neighbours.append((is_end & (col > 0) & (last > 0), at(col, 0)))
     neighbours.append((is_end & (col > 0), at(col - 1, last)))
     neighbours.append((is_end & (col < lines - 1), at(col + 1, last)))
-    for m in masks:
+    for m in masks + [1]:
         neighbours.append((slab >= 0, (flip_bits(group, m, order_bits), slab)))
     count = jnp.int32(0)
     for cond, dev in neighbours:
@@ -372,6 +373,48 @@
 
     lax.fori_loop(0, chunks, gather_plane, 0)
 
+    swaps = []
+    for k, source in enumerate((least_plane, least_in)):
+        copy = pltpu.make_async_remote_copy(source, swap_in.at[k], send6.at[k], recv6.at[k],
+                                            device_id=(flip_bits(group, 1, order_bits), slab),
+                                            device_id_type=mesh_id)
+        copy.start()
+        swaps.append(copy)
+    for copy in swaps:
+        copy.wait_recv()
+
+    down = odd == 1
+
+    def finish(c, carry):
+        rows = rows_of(c)
+        c0 = cost_x[0, rows, :]
+        c1 = cost_x[1, rows, :]
+        u0 = field[0, rows, :]
+        u1 = field[1, rows, :]
+        up_add = (c0, c0 + c1)
+        down_add = (c1 + c0, c1)
+        up_min = (u0, jnp.minimum(u0 + c1, u1))
+        down_min = (jnp.minimum(u1 + c0, u0), u1)
+        value = incoming[rows, :]
+        mine_plane = least_plane[rows, :]
+        mine_in = least_in[rows, :]
+        other_plane = swap_in[0, rows, :]
+        other_in = swap_in[1, rows, :]
+        least0 = jnp.where(down, other_plane, mine_plane)
+        least1 = jnp.where(down, mine_plane, other_plane)
+        up_in = jnp.where(down, other_in, mine_in)
+        down_in = jnp.where(down, mine_in, other_in)
+        least_local = (jnp.minimum(least0, least1 + c0), jnp.minimum(least1, least0 + c1))
+        for p in range(2):
+            line_add = jnp.where(down, down_add[p], up_add[p])
+            line_min = jnp.where(down, down_min[p], up_min[p])
+            sweep_field[0, p, rows, :] = jnp.minimum(value + line_add, line_min)
+            merged[p, rows, :] = jnp.minimum(
+                least_local[p], jnp.minimum(up_in + up_add[p], down_in + down_add[p]))
+        return carry
+
+    lax.fori_loop(0, chunks, finish, 0)
+
     def drain(c, carry):
         @pl.when(pos < last)
         def _():
@@ -400,9 +443,11 @@
     lax.fori_loop(0, chunks, drain, 0)
     for k in range(len(masks)):
         copy5(k).wait_send()
-
-
-def relay(totals, own, slabs, orders):
+    for copy in swaps:
+        copy.wait_send()
+
+
+def relay(totals, own, cost_x, field, slabs, orders):
     cells_y, cells_z = own.shape
     chunks = cells_y // RELAY_ROWS
     sharers = len(range(2, orders, 2))
@@ -413,10 +458,16 @@
     pair_box = pltpu.VMEM((chunks, 2, RELAY_ROWS, cells_z), jnp.float32)
     return pl.pallas_call(
         functools.partial(relay_kernel, line=line),
-        out_shape=(plane, plane, plane),
-        in_specs=[vmem, vmem],
-        out_specs=(vmem, vmem, vmem),
+        out_shape=(
+            jax.ShapeDtypeStruct((1,) + field.shape, jnp.float32),
+            jax.ShapeDtypeStruct(field.shape, jnp.float32),
+        ),
+        in_specs=[vmem, vmem, vmem, vmem],
+        out_specs=(vmem, vmem),
         scratch_shapes=[
+            pltpu.VMEM((cells_y, cells_z), jnp.float32),
+            pltpu.VMEM((cells_y, cells_z), jnp.float32),
+            pltpu.VMEM((cells_y, cells_z), jnp.float32),
             pltpu.VMEM((2, cells_y, cells_z), jnp.float32),
             pltpu.VMEM((2, cells_y, cells_z), jnp.float32),
             pair_box,
@@ -426,6 +477,7 @@
             box,
             pltpu.VMEM((max(sharers, 1), chunks, RELAY_ROWS, cells_z), jnp.float32),
             pltpu.VMEM((max(sharers, 1), cells_y, cells_z), jnp.float32),
+            pltpu.VMEM((2, cells_y, cells_z), jnp.float32),
             pltpu.SemaphoreType.DMA((chunks,)),
             pltpu.SemaphoreType.DMA((chunks,)),
             pltpu.SemaphoreType.DMA((chunks,)),
@@ -436,9 +488,11 @@
             pltpu.SemaphoreType.DMA((chunks, max(sharers, 1))),
             pltpu.SemaphoreType.DMA((max(sharers, 1),)),
             pltpu.SemaphoreType.DMA((max(sharers, 1),)),
+            pltpu.SemaphoreType.DMA((2,)),
+            pltpu.SemaphoreType.DMA((2,)),
         ],
         compiler_params=pltpu.CompilerParams(collective_id=0, has_side_effects=True),
-    )(totals, own)
+    )(totals, own, cost_x, field)
 
 
 def shards(previous, fibre_tensor, tissue, stim_sites, stim_times):
@@ -458,33 +512,8 @@
     cost_x, field, totals, own_plane = local_sweeps(
         bits, stims, stim_times, fibre_tensor, tissue, previous, grid_step)
 
-    core = group_index % 2
-    incoming, least_in, least_plane = relay(totals, own_plane, slabs, orders)
-    other = lax.ppermute(jnp.stack([least_plane, least_in]), "order", [(g, g ^ 1) for g in range(orders)])
-
-    least0 = jnp.where(core == 0, least_plane, other[0])
-    least1 = jnp.where(core == 0, other[0], least_plane)
-    up_in = jnp.where(core == 0, least_in, other[1])
-    down_in = jnp.where(core == 0, other[1], least_in)
-
-    up_add = jnp.stack([cost_x[0], cost_x[0] + cost_x[1]])
-    up_min = jnp.stack([field[0], jnp.minimum(field[0] + cost_x[1], field[1])])
-    down_add = jnp.stack([cost_x[1] + cost_x[0], cost_x[1]])
-    down_min = jnp.stack([jnp.minimum(field[1] + cost_x[0], field[0]), field[1]])
-    backward_x = core == 1
-    line_add = jnp.where(backward_x, down_add, up_add)
-    line_min = jnp.where(backward_x, down_min, up_min)
-    sweep_field = jnp.minimum(incoming[None] + line_add, line_min)
-
-    least_local = jnp.stack([
-        jnp.minimum(least0, least1 + cost_x[0]),
-        jnp.minimum(least1, least0 + cost_x[1]),
-    ])
-    merged = jnp.minimum(
-        least_local,
-        jnp.minimum(up_in[None] + up_add, down_in[None] + down_add),
-    )
-    return (merged, sweep_field[None])
+    sweep_field, merged = relay(totals, own_plane, cost_x, field, slabs, orders)
+    return (merged, sweep_field)
 
 
 def solution(mesh):

time: 89.6 us -> 92.8 us (1.036)
  Pallas kernels: 55.9 us -> 80.5 us
  starting transfers between devices: 21.7 us -> 0 us
  local copies, waits for them, and re-layouts: 4.55 us -> 10.4 us
  other arithmetic: 5.73 us -> 0.76 us
    pallas_call x1, Pallas kernels: 38.7 us -> 63.2 us  [relay(): pl.pallas_call(functools.partial(relay_kernel, line=line), out_shape=(jax...]
    ppermute x1 -> x0, starting transfers between devices: 21.7 us -> none  [shards(): lax.ppermute(jnp.stack([least_plane, least_in]), 'order', [(g, g ^ 1) for...]
    unnamed x16, local copies, waits for them, and re-layouts: 4.55 us -> 10.4 us
    min x2 -> x0, other arithmetic: 2.17 us -> none  [the longest x1 1.11 us: shards(): sweep_field = jnp.minimum(incoming[None] + line_add, line_min)]
    another operation x2 -> x0, other arithmetic: 1.52 us -> none  [the longest x1 1.22 us: shards(): jnp.stack([least_plane, least_in])]
    select_n x1 -> x0, other arithmetic: 1.27 us -> none  [shards(): up_in = jnp.where(core == 0, least_in, other[1])]
  transfers between devices with their start and end apart: 1 -> 0, of which waited for: 1 -> 0; matrix products, arithmetic and copies ran while one was open for 2% -> 0% of each run, Pallas kernels for 0% -> 0%
where the time goes in v11:
time: 92.8 us; the launch traced here: 92.4 us
  Pallas kernels  80.5 us (87%)
  local copies, waits for them, and re-layouts  10.4 us (11%)
    pallas_call x1, Pallas kernels, relay(): pl.pallas_call(functools.partial(relay_kernel, line=line), out_shape=(jax...  63.2 us
    pallas_call x1, Pallas kernels, local_sweeps(): pl.pallas_call(functools.partial(local_kernel, grid_step=grid_step), out_...  17.3 us
    unnamed x16, local copies, waits for them, and re-layouts  10.4 us

profile of v11, /device:TPU:103, one launch (start us, length us, event | category | flops | bytes accessed | tf_op | source)
XLA Modules:
  0.0 92.4 jit_solution(11401660509886962600)
XLA Ops:
  0.7 0.1 pad_add_fusion.1.flags
  0.8 0.7 subtract_bitcast_fusion
  1.5 0.0 copy-start
  1.5 1.1 %copy-done = s32[2,384,256]{2,1,0:T(8,128)S(1)} copy-done((s32[2,384,256]{2,1,0:T(8,128)S(1)}, s32[2,384,256]{2,1,0:T(8,128)}, u32[]{:S(2)}) %copy-start) | copy-done | bytes 786456
  2.6 0.0 copy-start.1
  2.6 1.1 %copy-done.1 = f32[2,384,256]{2,1,0:T(8,128)S(1)} copy-done((f32[2,384,256]{2,1,0:T(8,128)S(1)}, f32[2,384,256]{2,1,0:T(8,128)}, u32[]{:S(2)}) %copy-start.1) | copy-done | bytes 786456
  3.7 0.0 copy-start.6
  3.7 0.7 copy-done.6
  4.4 17.3 %shard_map.68 = (f32[2,384,256]{2,1,0:T(8,128)S(1)}, f32[2,384,256]{2,1,0:T(8,128)S(1)}, f32[2,384,256]{2,1,0:T(8,128)S(1)}, f32[384,256]{1,0:T(8,128)S(1)}) custom-call(s32[3]{0:T(128)S(1)} %pad_add_fusion.1.flags, s32[3,16]{1,0:T(4,128)S(1)} %pad_add_fusion.stims, f32[16]{0:T(128)S(1)} %copy-done.6, f32[6,2,384,256]{3,2,1,0:T(8,128)} %fibre.1, ...), custom_call_target="tpu_custom_call" | custom-call | flops 58982400 | bytes 7864320 | tf_op jit(solution)/shard_map/pallas_call | solution.py:130
  21.7 0.0 copy-start.2
  21.7 0.9 copy-done.2
  22.6 0.0 copy-start.3
  22.6 0.9 copy-done.3
  23.5 0.0 copy-start.4
  23.5 0.9 copy-done.4
  24.3 0.0 copy-start.5
  24.3 0.8 copy-done.5
  25.1 63.2 %shard_map.69 = (f32[1,2,384,256]{3,2,1,0:T(8,128)}, f32[2,384,256]{2,1,0:T(8,128)}) custom-call(f32[2,384,256]{2,1,0:T(8,128)} %copy-done.4, f32[384,256]{1,0:T(8,128)} %copy-done.5, f32[2,384,256]{2,1,0:T(8,128)} %copy-done.2, f32[2,384,256]{2,1,0:T(8,128)} %copy-done.3), custom_call_target="tpu_custom_call" | custom-call | tf_op jit(solution)/shard_map/pallas_call | solution.py:459
  88.3 2.1 %copy.9 = f32[2,384,256]{2,1,0:T(8,128)} copy(f32[2,384,256]{2,1,0:T(8,128)} %get-tuple-element.19) | data formatting | bytes 1572864
  90.4 2.1 %copy.10 = f32[1,2,384,256]{3,2,1,0:T(8,128)} copy(f32[1,2,384,256]{3,2,1,0:T(8,128)} %get-tuple-element.20) | data formatting | bytes 1572864
  (1 shorter events, 0.0 us)
Async XLA Ops:
  1.5 1.1 %copy-start = (s32[2,384,256]{2,1,0:T(8,128)S(1)}, s32[2,384,256]{2,1,0:T(8,128)}, u32[]{:S(2)}) copy-start(s32[2,384,256]{2,1,0:T(8,128)} %tissue.1) | copy-start | bytes 2359300
  2.6 1.1 %copy-start.1 = (f32[2,384,256]{2,1,0:T(8,128)S(1)}, f32[2,384,256]{2,1,0:T(8,128)}, u32[]{:S(2)}) copy-start(f32[2,384,256]{2,1,0:T(8,128)} %previous.1) | copy-start | bytes 2359300
  3.7 0.7 copy-start.6
  21.7 0.9 copy-start.2
  22.6 0.9 copy-start.3
  23.5 0.9 copy-start.4
  24.3 0.8 copy-start.5

commit v12 on v8

--- a/solution.py
+++ b/solution.py
@@ -34,7 +34,7 @@
 
 
 def local_kernel(flags, stims, stim_times, fibre, tissue, previous, cost_x, field, totals, own,
-                 cost_y, *, grid_step):
+                 cost_y, cost_z, *, grid_step):
     planes, cells_y, cells_z = previous.shape
     chunks = cells_y // CHUNK
     inf = jnp.float32(jnp.inf)
@@ -59,30 +59,39 @@
 
     lax.fori_loop(0, stims.shape[1], seed, 0)
 
+    blocks = cells_y // ROWS
+
+    def costs(i, carry):
+        p = i // blocks
+        rows = pl.ds(pl.multiple_of((i % blocks) * ROWS, ROWS), ROWS)
+        xx = fibre[0, p, rows, :]
+        yy = fibre[1, p, rows, :]
+        zz = fibre[2, p, rows, :]
+        xy = fibre[3, p, rows, :]
+        xz = fibre[4, p, rows, :]
+        yz = fibre[5, p, rows, :]
+        cx = yy * zz - yz * yz
+        cy = xx * zz - xz * xz
+        cz = xx * yy - xy * xy
+        det = xx * cx - xy * (xy * zz - yz * xz) + xz * (xy * yz - yy * xz)
+        factor = jnp.where(tissue[p, rows, :] == 1, 1.0, 4.0).astype(jnp.float32) * grid_step
+        inverse = 1.0 / det
+        cost_x[p, rows, :] = jnp.sqrt(cx * inverse) * factor
+        cost_y[p, rows, :] = jnp.sqrt(cy * inverse) * factor
+        cost_z[p, rows, :] = jnp.sqrt(cz * inverse) * factor
+        return carry
+
+    lax.fori_loop(0, planes * blocks, costs, 0, unroll=4)
+
     def costs_and_z(reverse):
         def body(i, carry):
             p = i // chunks
             rows = pl.ds(pl.multiple_of((i % chunks) * CHUNK, CHUNK), CHUNK)
-            xx = fibre[0, p, rows, :]
-            yy = fibre[1, p, rows, :]
-            zz = fibre[2, p, rows, :]
-            xy = fibre[3, p, rows, :]
-            xz = fibre[4, p, rows, :]
-            yz = fibre[5, p, rows, :]
-            cx = yy * zz - yz * yz
-            cy = xx * zz - xz * xz
-            cz = xx * yy - xy * xy
-            det = xx * cx - xy * (xy * zz - yz * xz) + xz * (xy * yz - yy * xz)
-            factor = jnp.where(tissue[p, rows, :] == 1, 1.0, 4.0).astype(jnp.float32) * grid_step
-            inverse = 1.0 / det
-            cost_x[p, rows, :] = jnp.sqrt(cx * inverse) * factor
-            cost_y[p, rows, :] = jnp.sqrt(cy * inverse) * factor
-            step_z = jnp.sqrt(cz * inverse) * factor
-            _, u = block_scan(step_z, field[p, rows, :], 1, reverse, False)
+            _, u = block_scan(cost_z[p, rows, :], field[p, rows, :], 1, reverse, False)
             field[p, rows, :] = u
             return carry
 
-        lax.fori_loop(0, planes * chunks, body, 0, unroll=2)
+        lax.fori_loop(0, planes * chunks, body, 0)
 
     def sweep_y(reverse):
         def body(j, carry):
@@ -98,7 +107,7 @@
             return tuple(out)
 
         start = tuple(jnp.full((CHUNK, cells_z), inf, jnp.float32) for _ in range(planes))
-        lax.fori_loop(0, chunks, body, start, unroll=2)
+        lax.fori_loop(0, chunks, body, start)
 
     for flag, fn in ((flags[2], costs_and_z), (flags[1], sweep_y)):
         pl.when(flag == 1)(functools.partial(fn, True))
@@ -132,7 +141,7 @@
         out_shape=(field, field, totals, own),
         in_specs=[smem, smem, smem, vmem, vmem, vmem],
         out_specs=(vmem, vmem, vmem, vmem),
-        scratch_shapes=[pltpu.VMEM(previous.shape, jnp.float32)],
+        scratch_shapes=[pltpu.VMEM(previous.shape, jnp.float32), pltpu.VMEM(previous.shape, jnp.float32)],
         compiler_params=pltpu.CompilerParams(vmem_limit_bytes=48 * 1024 * 1024),
         cost_estimate=pl.CostEstimate(
             flops=300 * elements, transcendentals=6 * elements, bytes_accessed=40 * elements

time: 89.6 us -> 91.6 us (1.022)
  Pallas kernels: 55.9 us -> 58 us
    pallas_call x1, Pallas kernels: 17.3 us -> 19.5 us  [local_sweeps(): pl.pallas_call(functools.partial(local_kernel, grid_step=grid_step), out_...]
where the time goes in v12:
time: 91.6 us; the launch traced here: 91.3 us
  Pallas kernels  58 us (63%)
  starting transfers between devices  21.7 us (24%)
  other arithmetic  5.73 us (6%)
  local copies, waits for them, and re-layouts  4.55 us (5%)
    pallas_call x1, Pallas kernels, relay(): pl.pallas_call(functools.partial(relay_kernel, line=line), out_shape=(pla...  38.5 us
    ppermute x1, starting transfers between devices, shards(): lax.ppermute(jnp.stack([least_plane, least_in]), 'order', [(g, g ^ 1) for...  21.7 us
    pallas_call x1, Pallas kernels, local_sweeps(): pl.pallas_call(functools.partial(local_kernel, grid_step=grid_step), out_...  19.5 us
    unnamed x16, local copies, waits for them, and re-layouts  4.55 us
  transfers between devices with their start and end apart: 1, of which 1 were waited for; matrix products, arithmetic and copies ran while one was open for 2% of the time, Pallas kernels for 0%

profile of v12, /device:TPU:103, one launch (start us, length us, event | category | flops | bytes accessed | tf_op | source)
XLA Modules:
  0.0 91.3 jit_solution(9827694294645198454)
XLA Ops:
  0.7 0.7 subtract_bitcast_fusion
  1.4 0.1 pad_add_fusion.1.flags
  1.5 0.0 copy-start
  1.5 1.1 %copy-done = s32[2,384,256]{2,1,0:T(8,128)S(1)} copy-done((s32[2,384,256]{2,1,0:T(8,128)S(1)}, s32[2,384,256]{2,1,0:T(8,128)}, u32[]{:S(2)}) %copy-start) | copy-done | bytes 786456
  2.6 0.0 copy-start.1
  2.6 1.1 %copy-done.1 = f32[2,384,256]{2,1,0:T(8,128)S(1)} copy-done((f32[2,384,256]{2,1,0:T(8,128)S(1)}, f32[2,384,256]{2,1,0:T(8,128)}, u32[]{:S(2)}) %copy-start.1) | copy-done | bytes 786456
  3.7 0.0 copy-start.4
  3.7 0.7 copy-done.4
  4.4 19.5 %shard_map.68 = (f32[2,384,256]{2,1,0:T(8,128)S(1)}, f32[2,384,256]{2,1,0:T(8,128)S(1)}, f32[2,384,256]{2,1,0:T(8,128)S(1)}, f32[384,256]{1,0:T(8,128)S(1)}) custom-call(s32[3]{0:T(128)S(1)} %pad_add_fusion.1.flags, s32[3,16]{1,0:T(4,128)S(1)} %pad_add_fusion.stims, f32[16]{0:T(128)S(1)} %copy-done.4, f32[6,2,384,256]{3,2,1,0:T(8,128)} %fibre.1, ...), custom_call_target="tpu_custom_call" | custom-call | flops 58982400 | bytes 7864320 | tf_op jit(solution)/shard_map/pallas_call | solution.py:139
  23.9 0.0 copy-start.2
  23.9 0.9 copy-done.2
  24.7 0.0 copy-start.3
  24.7 0.7 copy-done.3
  25.5 38.5 %shard_map.69 = (f32[384,256]{1,0:T(8,128)}, f32[384,256]{1,0:T(8,128)}, f32[384,256]{1,0:T(8,128)}) custom-call(f32[2,384,256]{2,1,0:T(8,128)} %copy-done.2, f32[384,256]{1,0:T(8,128)} %copy-done.3), custom_call_target="tpu_custom_call" | custom-call | tf_op jit(solution)/shard_map/pallas_call | solution.py:423
  64.0 0.0 copy-start.7
  64.0 1.2 %pad_maximum_fusion = f32[2,384,256]{2,1,0:T(8,128)S(1)} fusion(f32[1,384,256]{2,1,0:T(8,128)} %bitcast.61, f32[1,384,256]{2,1,0:T(8,128)} %bitcast.62), kind=kLoop, calls=%fused_computation | loop fusion | flops 196608 | bytes 1572864 | tf_op jit(solution)/shard_map/stack | solution.py:472
  65.2 0.0 copy-start.5
  65.2 0.0 copy-start.6
  65.3 21.7 %collective-permute-start = (f32[2,384,256]{2,1,0:T(8,128)S(1)}, f32[2,384,256]{2,1,0:T(8,128)}, u32[]{:S(2)}, u32[]{:S(2)}) collective-permute-start(f32[2,384,256]{2,1,0:T(8,128)S(1)} %pad_maximum_fusion), channel_id=1, source_target_pairs={{0,32},{32,0},{64,96},{96,64},{128,160},{160,128},{192,224},{224,1... | collective-permute-start | bytes 2359304 | tf_op jit(solution)/shard_map/ppermute | solution.py:472
  86.9 0.3 minimum_bitcast_fusion
  87.2 0.0 copy-done.7
  87.2 1.1 %fusion.2 = f32[1,2,384,256]{3,2,1,0:T(8,128)} fusion(f32[1,1,384,256]{3,2,1,0:T(8,128)S(1)} %get-tuple-element.25, f32[1,1,384,256]{3,2,1,0:T(8,128)S(1)} %bitcast.60, f32[1,1,384,256]{3,2,1,0:T(8,128)S(1)} %get-tuple-element.23, f32[1,1,384,256]{3,2,1,0:T(8,128)S(1)} %get-tuple-element.28, f32[1,1,384,256]{3,2,1,0:T(8,128)S(1)} %get-tuple-element.19, ...), kind=kLoop, calls=%fused_computation.7 | loop fusion | flops 1572864 | bytes 3932161 | tf_op jit(solution)/shard_map/min | solution.py:486
  88.4 0.6 collective-permute-done
  89.0 0.0 copy-done.5
  89.0 0.0 copy-done.6
  89.0 1.3 %fusion.10 = (f32[384,256]{1,0:T(8,128)S(1)}, f32[384,256]{1,0:T(8,128)S(1)}, f32[1,384,256]{2,1,0:T(8,128)S(1)}, f32[1,384,256]{2,1,0:T(8,128)S(1)}) fusion(f32[384,256]{1,0:T(8,128)S(1)} %copy-done.5, f32[2,384,256]{2,1,0:T(8,128)} %collective-permute-done, pred[]{:T(512)S(6)} %eq.17, f32[2,384,256]{2,1,0:T(8,128)S(1)} %get-tuple-element.13, ...), kind=kLoop, calls=%fused_computation.22 | loop fusion | flops 786432 | bytes 3932161 | tf_op jit(solution)/shard_map/jit(_where)/select_n | solution.py:476
  90.2 1.1 %maximum_minimum_fusion = f32[2,384,256]{2,1,0:T(8,128)} fusion(f32[1,384,256]{2,1,0:T(8,128)S(1)} %get-tuple-element.29, f32[1,384,256]{2,1,0:T(8,128)S(1)} %get-tuple-element.30, f32[1,384,256]{2,1,0:T(8,128)S(1)} %get-tuple-element.24, f32[1,384,256]{2,1,0:T(8,128)S(1)} %get-tuple-element.27, f32[1,384,256]{2,1,0:T(8,128)S(1)} %get-tuple-element.26, ...), kind=kLoop, calls=%fused_computation.1 | loop fusion | flops 1376256 | bytes 3538944 | tf_op jit(solution)/shard_map/min | solution.py:492
  (1 shorter events, 0.0 us)
Async XLA Ops:
  1.5 1.1 %copy-start = (s32[2,384,256]{2,1,0:T(8,128)S(1)}, s32[2,384,256]{2,1,0:T(8,128)}, u32[]{:S(2)}) copy-start(s32[2,384,256]{2,1,0:T(8,128)} %tissue.1) | copy-start | bytes 2359300
  2.6 1.1 %copy-start.1 = (f32[2,384,256]{2,1,0:T(8,128)S(1)}, f32[2,384,256]{2,1,0:T(8,128)}, u32[]{:S(2)}) copy-start(f32[2,384,256]{2,1,0:T(8,128)} %previous.1) | copy-start | bytes 2359300
  3.7 0.7 copy-start.4
  23.9 0.9 copy-start.2
  24.7 0.7 copy-start.3
  64.0 23.2 %copy-start.7 = (f32[384,256]{1,0:T(8,128)S(1)}, f32[384,256]{1,0:T(8,128)}, u32[]{:S(2)}) copy-start(f32[384,256]{1,0:T(8,128)} %get-tuple-element.14) | copy-start | bytes 1179652
  65.2 23.7 %copy-start.5 = (f32[384,256]{1,0:T(8,128)S(1)}, f32[384,256]{1,0:T(8,128)}, u32[]{:S(2)}) copy-start(f32[384,256]{1,0:T(8,128)} %get-tuple-element.12) | copy-start | bytes 1179652
  65.2 23.7 %copy-start.6 = (f32[384,256]{1,0:T(8,128)S(1)}, f32[384,256]{1,0:T(8,128)}, u32[]{:S(2)}) copy-start(f32[384,256]{1,0:T(8,128)} %get-tuple-element.11) | copy-start | bytes 1179652
  65.3 23.7 %collective-permute-start = (f32[2,384,256]{2,1,0:T(8,128)S(1)}, f32[2,384,256]{2,1,0:T(8,128)}, u32[]{:S(2)}, u32[]{:S(2)}) collective-permute-start(f32[2,384,256]{2,1,0:T(8,128)S(1)} %pad_maximum_fusion), channel_id=1, source_target_pairs={{0,32},{32,0},{64,96},{96,64},{128,160},{160,128},{192,224},{224,1... | collective-permute-start | bytes 2359304 | tf_op jit(solution)/shard_map/ppermute | solution.py:472

commit v13 on v8

--- a/solution.py
+++ b/solution.py
@@ -31,6 +31,27 @@
         a, m = scan_step(a, m, k, axis, reverse, last=(2 * k >= n) and not need_sum)
         k *= 2
     return a, m
+
+
+def lane_scan(step, seeded, reverse):
+    width = step.shape[1]
+    if width % 128 or width == 128:
+        return block_scan(step, seeded, 1, reverse, False)[1]
+    parts = []
+    for i in range(width // 128):
+        lanes = slice(i * 128, (i + 1) * 128)
+        parts.append(block_scan(step[:, lanes], seeded[:, lanes], 1, reverse, True))
+    order = range(len(parts) - 1, -1, -1) if reverse else range(len(parts))
+    carry = None
+    out = [None] * len(parts)
+    for i in order:
+        a, m = parts[i]
+        if carry is not None:
+            m = jnp.minimum(carry + a, m)
+        edge = m[:, 0:1] if reverse else m[:, 127:128]
+        carry = jnp.broadcast_to(edge, m.shape)
+        out[i] = m
+    return jnp.concatenate(out, axis=1)
 
 
 def local_kernel(flags, stims, stim_times, fibre, tissue, previous, cost_x, field, totals, own,
@@ -78,7 +99,7 @@
             cost_x[p, rows, :] = jnp.sqrt(cx * inverse) * factor
             cost_y[p, rows, :] = jnp.sqrt(cy * inverse) * factor
             step_z = jnp.sqrt(cz * inverse) * factor
-            _, u = block_scan(step_z, field[p, rows, :], 1, reverse, False)
+            u = lane_scan(step_z, field[p, rows, :], reverse)
             field[p, rows, :] = u
             return carry
 

time: 89.6 us -> 89.7 us (level)
  no operation moved by 1% of the time
where the time goes in v13:
time: 89.7 us; the launch traced here: 89.4 us
  Pallas kernels  56.1 us (63%)
  starting transfers between devices  21.7 us (24%)
  other arithmetic  5.73 us (6%)
  local copies, waits for them, and re-layouts  4.55 us (5%)
    pallas_call x1, Pallas kernels, relay(): pl.pallas_call(functools.partial(relay_kernel, line=line), out_shape=(pla...  38.6 us
    ppermute x1, starting transfers between devices, shards(): lax.ppermute(jnp.stack([least_plane, least_in]), 'order', [(g, g ^ 1) for...  21.7 us
    pallas_call x1, Pallas kernels, local_sweeps(): pl.pallas_call(functools.partial(local_kernel, grid_step=grid_step), out_...  17.5 us
    unnamed x16, local copies, waits for them, and re-layouts  4.55 us
  transfers between devices with their start and end apart: 1, of which 1 were waited for; matrix products, arithmetic and copies ran while one was open for 2% of the time, Pallas kernels for 0%

profile of v13, /device:TPU:103, one launch (start us, length us, event | category | flops | bytes accessed | tf_op | source)
XLA Modules:
  0.0 89.4 jit_solution(5625919316839650941)
XLA Ops:
  0.7 0.7 subtract_bitcast_fusion
  1.4 0.1 pad_add_fusion.1.flags
  1.5 0.0 copy-start
  1.5 1.1 %copy-done = s32[2,384,256]{2,1,0:T(8,128)S(1)} copy-done((s32[2,384,256]{2,1,0:T(8,128)S(1)}, s32[2,384,256]{2,1,0:T(8,128)}, u32[]{:S(2)}) %copy-start) | copy-done | bytes 786456
  2.6 0.0 copy-start.1
  2.6 1.1 %copy-done.1 = f32[2,384,256]{2,1,0:T(8,128)S(1)} copy-done((f32[2,384,256]{2,1,0:T(8,128)S(1)}, f32[2,384,256]{2,1,0:T(8,128)}, u32[]{:S(2)}) %copy-start.1) | copy-done | bytes 786456
  3.7 0.0 copy-start.4
  3.7 0.7 copy-done.4
  4.4 17.5 %shard_map.68 = (f32[2,384,256]{2,1,0:T(8,128)S(1)}, f32[2,384,256]{2,1,0:T(8,128)S(1)}, f32[2,384,256]{2,1,0:T(8,128)S(1)}, f32[384,256]{1,0:T(8,128)S(1)}) custom-call(s32[3]{0:T(128)S(1)} %pad_add_fusion.1.flags, s32[3,16]{1,0:T(4,128)S(1)} %pad_add_fusion.stims, f32[16]{0:T(128)S(1)} %copy-done.4, f32[6,2,384,256]{3,2,1,0:T(8,128)} %fibre.1, ...), custom_call_target="tpu_custom_call" | custom-call | flops 58982400 | bytes 7864320 | tf_op jit(solution)/shard_map/pallas_call | solution.py:151
  21.9 0.0 copy-start.2
  21.9 0.9 copy-done.2
  22.8 0.0 copy-start.3
  22.8 0.7 copy-done.3
  23.5 38.6 %shard_map.69 = (f32[384,256]{1,0:T(8,128)}, f32[384,256]{1,0:T(8,128)}, f32[384,256]{1,0:T(8,128)}) custom-call(f32[2,384,256]{2,1,0:T(8,128)} %copy-done.2, f32[384,256]{1,0:T(8,128)} %copy-done.3), custom_call_target="tpu_custom_call" | custom-call | tf_op jit(solution)/shard_map/pallas_call | solution.py:435
  62.1 0.0 copy-start.7
  62.1 1.2 %pad_maximum_fusion = f32[2,384,256]{2,1,0:T(8,128)S(1)} fusion(f32[1,384,256]{2,1,0:T(8,128)} %bitcast.61, f32[1,384,256]{2,1,0:T(8,128)} %bitcast.62), kind=kLoop, calls=%fused_computation | loop fusion | flops 196608 | bytes 1572864 | tf_op jit(solution)/shard_map/stack | solution.py:484
  63.3 0.0 copy-start.5
  63.3 0.0 copy-start.6
  63.4 21.7 %collective-permute-start = (f32[2,384,256]{2,1,0:T(8,128)S(1)}, f32[2,384,256]{2,1,0:T(8,128)}, u32[]{:S(2)}, u32[]{:S(2)}) collective-permute-start(f32[2,384,256]{2,1,0:T(8,128)S(1)} %pad_maximum_fusion), channel_id=1, source_target_pairs={{0,32},{32,0},{64,96},{96,64},{128,160},{160,128},{192,224},{224,1... | collective-permute-start | bytes 2359304 | tf_op jit(solution)/shard_map/ppermute | solution.py:484
  85.0 0.3 minimum_bitcast_fusion
  85.3 0.0 copy-done.7
  85.3 1.1 %fusion.2 = f32[1,2,384,256]{3,2,1,0:T(8,128)} fusion(f32[1,1,384,256]{3,2,1,0:T(8,128)S(1)} %get-tuple-element.25, f32[1,1,384,256]{3,2,1,0:T(8,128)S(1)} %bitcast.60, f32[1,1,384,256]{3,2,1,0:T(8,128)S(1)} %get-tuple-element.23, f32[1,1,384,256]{3,2,1,0:T(8,128)S(1)} %get-tuple-element.28, f32[1,1,384,256]{3,2,1,0:T(8,128)S(1)} %get-tuple-element.19, ...), kind=kLoop, calls=%fused_computation.7 | loop fusion | flops 1572864 | bytes 3932161 | tf_op jit(solution)/shard_map/min | solution.py:498
  86.4 0.6 collective-permute-done
  87.0 0.0 copy-done.5
  87.1 0.0 copy-done.6
  87.1 1.3 %fusion.10 = (f32[384,256]{1,0:T(8,128)S(1)}, f32[384,256]{1,0:T(8,128)S(1)}, f32[1,384,256]{2,1,0:T(8,128)S(1)}, f32[1,384,256]{2,1,0:T(8,128)S(1)}) fusion(f32[384,256]{1,0:T(8,128)S(1)} %copy-done.5, f32[2,384,256]{2,1,0:T(8,128)} %collective-permute-done, pred[]{:T(512)S(6)} %eq.17, f32[2,384,256]{2,1,0:T(8,128)S(1)} %get-tuple-element.13, ...), kind=kLoop, calls=%fused_computation.22 | loop fusion | flops 786432 | bytes 3932161 | tf_op jit(solution)/shard_map/jit(_where)/select_n | solution.py:488
  88.3 1.1 %maximum_minimum_fusion = f32[2,384,256]{2,1,0:T(8,128)} fusion(f32[1,384,256]{2,1,0:T(8,128)S(1)} %get-tuple-element.29, f32[1,384,256]{2,1,0:T(8,128)S(1)} %get-tuple-element.30, f32[1,384,256]{2,1,0:T(8,128)S(1)} %get-tuple-element.24, f32[1,384,256]{2,1,0:T(8,128)S(1)} %get-tuple-element.27, f32[1,384,256]{2,1,0:T(8,128)S(1)} %get-tuple-element.26, ...), kind=kLoop, calls=%fused_computation.1 | loop fusion | flops 1376256 | bytes 3538944 | tf_op jit(solution)/shard_map/min | solution.py:504
  (1 shorter events, 0.0 us)
Async XLA Ops:
  1.5 1.1 %copy-start = (s32[2,384,256]{2,1,0:T(8,128)S(1)}, s32[2,384,256]{2,1,0:T(8,128)}, u32[]{:S(2)}) copy-start(s32[2,384,256]{2,1,0:T(8,128)} %tissue.1) | copy-start | bytes 2359300
  2.6 1.1 %copy-start.1 = (f32[2,384,256]{2,1,0:T(8,128)S(1)}, f32[2,384,256]{2,1,0:T(8,128)}, u32[]{:S(2)}) copy-start(f32[2,384,256]{2,1,0:T(8,128)} %previous.1) | copy-start | bytes 2359300
  3.7 0.7 copy-start.4
  21.9 0.9 copy-start.2
  22.8 0.7 copy-start.3
  62.1 23.2 %copy-start.7 = (f32[384,256]{1,0:T(8,128)S(1)}, f32[384,256]{1,0:T(8,128)}, u32[]{:S(2)}) copy-start(f32[384,256]{1,0:T(8,128)} %get-tuple-element.14) | copy-start | bytes 1179652
  63.3 23.7 %copy-start.5 = (f32[384,256]{1,0:T(8,128)S(1)}, f32[384,256]{1,0:T(8,128)}, u32[]{:S(2)}) copy-start(f32[384,256]{1,0:T(8,128)} %get-tuple-element.12) | copy-start | bytes 1179652
  63.3 23.7 %copy-start.6 = (f32[384,256]{1,0:T(8,128)S(1)}, f32[384,256]{1,0:T(8,128)}, u32[]{:S(2)}) copy-start(f32[384,256]{1,0:T(8,128)} %get-tuple-element.11) | copy-start | bytes 1179652
  63.4 23.7 %collective-permute-start = (f32[2,384,256]{2,1,0:T(8,128)S(1)}, f32[2,384,256]{2,1,0:T(8,128)}, u32[]{:S(2)}, u32[]{:S(2)}) collective-permute-start(f32[2,384,256]{2,1,0:T(8,128)S(1)} %pad_maximum_fusion), channel_id=1, source_target_pairs={{0,32},{32,0},{64,96},{96,64},{128,160},{160,128},{192,224},{224,1... | collective-permute-start | bytes 2359304 | tf_op jit(solution)/shard_map/ppermute | solution.py:484

commit v14 on v13

--- a/solution.py
+++ b/solution.py
@@ -204,15 +204,18 @@
     is_end = pos == last
     in_up = pos < half
     in_down = (pos >= half) & (pos < last)
-    up_next = pos + 1 < half
-    down_next = pos > half
+    up_next = (pos >= 1) & (pos + 1 < half)
+    down_next = (pos <= last - 2) & (pos > half)
+    ends_to = [p for p in (0, 1) if p < half] + [p for p in (last - 1, last - 2) if half <= p < last]
 
     barrier = pltpu.get_barrier_semaphore()
     neighbours = []
     neighbours.append((pos > 0, at(col, pos - 1)))
     neighbours.append((pos < last, at(col, pos + 1)))
-    neighbours.append(((pos == 0) & (col > 0) & (last > 0), at(col, last)))
-    neighbours.append((is_end & (col > 0) & (last > 0), at(col, 0)))
+    for p in ends_to:
+        if p not in (last - 1,):
+            neighbours.append(((pos == p) & (col > 0), at(col, last)))
+            neighbours.append((is_end & (col > 0), at(col, p)))
     neighbours.append((is_end & (col > 0), at(col - 1, last)))
     neighbours.append((is_end & (col < lines - 1), at(col + 1, last)))
     for m in masks:
@@ -321,13 +324,8 @@
             share(c)
             box2_out[c] = jnp.minimum(value + line_total[0, rows, :], line_total[1, rows, :])
 
-            @pl.when(pos > 0)
-            def _():
-                copy3_from_end(c, 0, at(col, 0)).start()
-
-            @pl.when(half < last)
-            def _():
-                copy3_from_end(c, 1, at(col, last - 1)).start()
+            for k, p in enumerate(ends_to):
+                copy3_from_end(c, k, at(col, p)).start()
 
         @pl.when(is_end & (col < lines - 1))
         def _():
@@ -402,13 +400,10 @@
         def _():
             copy2(c).wait_send()
 
-        @pl.when(is_end & jnp.logical_not(first_col) & (pos > 0))
-        def _():
-            copy3_from_end(c, 0, at(col, 0)).wait_send()
-
-        @pl.when(is_end & jnp.logical_not(first_col) & (half < last))
-        def _():
-            copy3_from_end(c, 1, at(col, last - 1)).wait_send()
+        @pl.when(is_end & jnp.logical_not(first_col))
+        def _():
+            for k, p in enumerate(ends_to):
+                copy3_from_end(c, k, at(col, p)).wait_send()
 
         @pl.when(jnp.logical_not(first_col) & ((in_up & up_next) | (in_down & down_next)))
         def _():
@@ -451,7 +446,7 @@
             pltpu.SemaphoreType.DMA((chunks,)),
             pltpu.SemaphoreType.DMA((chunks,)),
             pltpu.SemaphoreType.DMA((chunks,)),
-            pltpu.SemaphoreType.DMA((chunks, 2)),
+            pltpu.SemaphoreType.DMA((chunks, 4)),
             pltpu.SemaphoreType.DMA((chunks,)),
             pltpu.SemaphoreType.DMA((chunks, max(sharers, 1))),
             pltpu.SemaphoreType.DMA((chunks, max(sharers, 1))),

time: 89.7 us -> 88.4 us (0.986)
  starting transfers between devices: 21.7 us -> 19.6 us
    ppermute x1, starting transfers between devices: 21.7 us -> 19.6 us  [shards(): lax.ppermute(jnp.stack([least_plane, least_in]), 'order', [(g, g ^ 1) for...]
where the time goes in v14:
time: 88.4 us; the launch traced here: 88.1 us
  Pallas kernels  56.8 us (64%)
  starting transfers between devices  19.6 us (22%)
  other arithmetic  5.73 us (6%)
  local copies, waits for them, and re-layouts  4.55 us (5%)
    pallas_call x1, Pallas kernels, relay(): pl.pallas_call(functools.partial(relay_kernel, line=line), out_shape=(pla...  39.3 us
    ppermute x1, starting transfers between devices, shards(): lax.ppermute(jnp.stack([least_plane, least_in]), 'order', [(g, g ^ 1) for...  19.6 us
    pallas_call x1, Pallas kernels, local_sweeps(): pl.pallas_call(functools.partial(local_kernel, grid_step=grid_step), out_...  17.5 us
    unnamed x16, local copies, waits for them, and re-layouts  4.55 us
  transfers between devices with their start and end apart: 1, of which 1 were waited for; matrix products, arithmetic and copies ran while one was open for 2% of the time, Pallas kernels for 0%

profile of v14, /device:TPU:103, one launch (start us, length us, event | category | flops | bytes accessed | tf_op | source)
XLA Modules:
  0.0 88.1 jit_solution(11405632923408615380)
XLA Ops:
  0.7 0.7 subtract_bitcast_fusion
  1.4 0.1 pad_add_fusion.1.flags
  1.5 0.0 copy-start
  1.5 1.1 %copy-done = s32[2,384,256]{2,1,0:T(8,128)S(1)} copy-done((s32[2,384,256]{2,1,0:T(8,128)S(1)}, s32[2,384,256]{2,1,0:T(8,128)}, u32[]{:S(2)}) %copy-start) | copy-done | bytes 786456
  2.6 0.0 copy-start.1
  2.6 1.1 %copy-done.1 = f32[2,384,256]{2,1,0:T(8,128)S(1)} copy-done((f32[2,384,256]{2,1,0:T(8,128)S(1)}, f32[2,384,256]{2,1,0:T(8,128)}, u32[]{:S(2)}) %copy-start.1) | copy-done | bytes 786456
  3.7 0.0 copy-start.4
  3.7 0.7 copy-done.4
  4.4 17.5 %shard_map.68 = (f32[2,384,256]{2,1,0:T(8,128)S(1)}, f32[2,384,256]{2,1,0:T(8,128)S(1)}, f32[2,384,256]{2,1,0:T(8,128)S(1)}, f32[384,256]{1,0:T(8,128)S(1)}) custom-call(s32[3]{0:T(128)S(1)} %pad_add_fusion.1.flags, s32[3,16]{1,0:T(4,128)S(1)} %pad_add_fusion.stims, f32[16]{0:T(128)S(1)} %copy-done.4, f32[6,2,384,256]{3,2,1,0:T(8,128)} %fibre.1, ...), custom_call_target="tpu_custom_call" | custom-call | flops 58982400 | bytes 7864320 | tf_op jit(solution)/shard_map/pallas_call | solution.py:151
  21.9 0.0 copy-start.2
  21.9 0.9 copy-done.2
  22.8 0.0 copy-start.3
  22.8 0.7 copy-done.3
  23.5 39.3 %shard_map.69 = (f32[384,256]{1,0:T(8,128)}, f32[384,256]{1,0:T(8,128)}, f32[384,256]{1,0:T(8,128)}) custom-call(f32[2,384,256]{2,1,0:T(8,128)} %copy-done.2, f32[384,256]{1,0:T(8,128)} %copy-done.3), custom_call_target="tpu_custom_call" | custom-call | tf_op jit(solution)/shard_map/pallas_call | solution.py:430
  62.9 0.0 copy-start.7
  62.9 1.2 %pad_maximum_fusion = f32[2,384,256]{2,1,0:T(8,128)S(1)} fusion(f32[1,384,256]{2,1,0:T(8,128)} %bitcast.61, f32[1,384,256]{2,1,0:T(8,128)} %bitcast.62), kind=kLoop, calls=%fused_computation | loop fusion | flops 196608 | bytes 1572864 | tf_op jit(solution)/shard_map/stack | solution.py:479
  64.1 0.0 copy-start.5
  64.1 0.0 copy-start.6
  64.1 19.6 %collective-permute-start = (f32[2,384,256]{2,1,0:T(8,128)S(1)}, f32[2,384,256]{2,1,0:T(8,128)}, u32[]{:S(2)}, u32[]{:S(2)}) collective-permute-start(f32[2,384,256]{2,1,0:T(8,128)S(1)} %pad_maximum_fusion), channel_id=1, source_target_pairs={{0,32},{32,0},{64,96},{96,64},{128,160},{160,128},{192,224},{224,1... | collective-permute-start | bytes 2359304 | tf_op jit(solution)/shard_map/ppermute | solution.py:479
  83.7 0.3 minimum_bitcast_fusion
  84.0 0.0 copy-done.7
  84.0 1.1 %fusion.2 = f32[1,2,384,256]{3,2,1,0:T(8,128)} fusion(f32[1,1,384,256]{3,2,1,0:T(8,128)S(1)} %get-tuple-element.25, f32[1,1,384,256]{3,2,1,0:T(8,128)S(1)} %bitcast.60, f32[1,1,384,256]{3,2,1,0:T(8,128)S(1)} %get-tuple-element.23, f32[1,1,384,256]{3,2,1,0:T(8,128)S(1)} %get-tuple-element.28, f32[1,1,384,256]{3,2,1,0:T(8,128)S(1)} %get-tuple-element.19, ...), kind=kLoop, calls=%fused_computation.7 | loop fusion | flops 1572864 | bytes 3932161 | tf_op jit(solution)/shard_map/min | solution.py:493
  85.1 0.6 collective-permute-done
  85.7 0.0 copy-done.5
  85.7 0.0 copy-done.6
  85.7 1.3 %fusion.10 = (f32[384,256]{1,0:T(8,128)S(1)}, f32[384,256]{1,0:T(8,128)S(1)}, f32[1,384,256]{2,1,0:T(8,128)S(1)}, f32[1,384,256]{2,1,0:T(8,128)S(1)}) fusion(f32[384,256]{1,0:T(8,128)S(1)} %copy-done.5, f32[2,384,256]{2,1,0:T(8,128)} %collective-permute-done, pred[]{:T(512)S(6)} %eq.17, f32[2,384,256]{2,1,0:T(8,128)S(1)} %get-tuple-element.13, ...), kind=kLoop, calls=%fused_computation.22 | loop fusion | flops 786432 | bytes 3932161 | tf_op jit(solution)/shard_map/jit(_where)/select_n | solution.py:483
  87.0 1.1 %maximum_minimum_fusion = f32[2,384,256]{2,1,0:T(8,128)} fusion(f32[1,384,256]{2,1,0:T(8,128)S(1)} %get-tuple-element.29, f32[1,384,256]{2,1,0:T(8,128)S(1)} %get-tuple-element.30, f32[1,384,256]{2,1,0:T(8,128)S(1)} %get-tuple-element.24, f32[1,384,256]{2,1,0:T(8,128)S(1)} %get-tuple-element.27, f32[1,384,256]{2,1,0:T(8,128)S(1)} %get-tuple-element.26, ...), kind=kLoop, calls=%fused_computation.1 | loop fusion | flops 1376256 | bytes 3538944 | tf_op jit(solution)/shard_map/min | solution.py:499
  (1 shorter events, 0.0 us)
Async XLA Ops:
  1.5 1.1 %copy-start = (s32[2,384,256]{2,1,0:T(8,128)S(1)}, s32[2,384,256]{2,1,0:T(8,128)}, u32[]{:S(2)}) copy-start(s32[2,384,256]{2,1,0:T(8,128)} %tissue.1) | copy-start | bytes 2359300
  2.6 1.1 %copy-start.1 = (f32[2,384,256]{2,1,0:T(8,128)S(1)}, f32[2,384,256]{2,1,0:T(8,128)}, u32[]{:S(2)}) copy-start(f32[2,384,256]{2,1,0:T(8,128)} %previous.1) | copy-start | bytes 2359300
  3.7 0.7 copy-start.4
  21.9 0.9 %copy-start.2 = (f32[2,384,256]{2,1,0:T(8,128)}, f32[2,384,256]{2,1,0:T(8,128)S(1)}, u32[]{:S(2)}) copy-start(f32[2,384,256]{2,1,0:T(8,128)S(1)} %get-tuple-element.9.totals) | copy-start | bytes 2359300
  22.8 0.7 copy-start.3
  62.9 21.1 %copy-start.7 = (f32[384,256]{1,0:T(8,128)S(1)}, f32[384,256]{1,0:T(8,128)}, u32[]{:S(2)}) copy-start(f32[384,256]{1,0:T(8,128)} %get-tuple-element.14) | copy-start | bytes 1179652
  64.1 21.6 %copy-start.5 = (f32[384,256]{1,0:T(8,128)S(1)}, f32[384,256]{1,0:T(8,128)}, u32[]{:S(2)}) copy-start(f32[384,256]{1,0:T(8,128)} %get-tuple-element.12) | copy-start | bytes 1179652
  64.1 21.6 %copy-start.6 = (f32[384,256]{1,0:T(8,128)S(1)}, f32[384,256]{1,0:T(8,128)}, u32[]{:S(2)}) copy-start(f32[384,256]{1,0:T(8,128)} %get-tuple-element.11) | copy-start | bytes 1179652
  64.1 21.6 %collective-permute-start = (f32[2,384,256]{2,1,0:T(8,128)S(1)}, f32[2,384,256]{2,1,0:T(8,128)}, u32[]{:S(2)}, u32[]{:S(2)}) collective-permute-start(f32[2,384,256]{2,1,0:T(8,128)S(1)} %pad_maximum_fusion), channel_id=1, source_target_pairs={{0,32},{32,0},{64,96},{96,64},{128,160},{160,128},{192,224},{224,1... | collective-permute-start | bytes 2359304 | tf_op jit(solution)/shard_map/ppermute | solution.py:479

commit v15 on v14

--- a/solution.py
+++ b/solution.py
@@ -163,6 +163,8 @@
 
 RELAY_ROWS = 16
 LINE = 8
+UP_DIRECT = 3
+DOWN_DIRECT = 2
 
 
 def flip_bits(value, mask, bits):
@@ -204,9 +206,10 @@
     is_end = pos == last
     in_up = pos < half
     in_down = (pos >= half) & (pos < last)
-    up_next = (pos >= 1) & (pos + 1 < half)
-    down_next = (pos <= last - 2) & (pos > half)
-    ends_to = [p for p in (0, 1) if p < half] + [p for p in (last - 1, last - 2) if half <= p < last]
+    up_next = (pos >= UP_DIRECT - 1) & (pos + 1 < half)
+    down_next = (pos <= last - DOWN_DIRECT) & (pos > half)
+    ends_to = [p for p in range(UP_DIRECT) if p < half]
+    ends_to += [last - 1 - j for j in range(DOWN_DIRECT) if half <= last - 1 - j < last]
 
     barrier = pltpu.get_barrier_semaphore()
     neighbours = []
@@ -446,7 +449,7 @@
             pltpu.SemaphoreType.DMA((chunks,)),
             pltpu.SemaphoreType.DMA((chunks,)),
             pltpu.SemaphoreType.DMA((chunks,)),
-            pltpu.SemaphoreType.DMA((chunks, 4)),
+            pltpu.SemaphoreType.DMA((chunks, UP_DIRECT + DOWN_DIRECT)),
             pltpu.SemaphoreType.DMA((chunks,)),
             pltpu.SemaphoreType.DMA((chunks, max(sharers, 1))),
             pltpu.SemaphoreType.DMA((chunks, max(sharers, 1))),

time: 88.4 us -> 90.6 us (1.025)
  starting transfers between devices: 19.6 us -> 21.5 us
    ppermute x1, starting transfers between devices: 19.6 us -> 21.5 us  [shards(): lax.ppermute(jnp.stack([least_plane, least_in]), 'order', [(g, g ^ 1) for...]
where the time goes in v15:
time: 90.6 us; the launch traced here: 90.3 us
  Pallas kernels  57.1 us (63%)
  starting transfers between devices  21.5 us (24%)
  other arithmetic  5.73 us (6%)
  local copies, waits for them, and re-layouts  4.55 us (5%)
    pallas_call x1, Pallas kernels, relay(): pl.pallas_call(functools.partial(relay_kernel, line=line), out_shape=(pla...  39.6 us
    ppermute x1, starting transfers between devices, shards(): lax.ppermute(jnp.stack([least_plane, least_in]), 'order', [(g, g ^ 1) for...  21.5 us
    pallas_call x1, Pallas kernels, local_sweeps(): pl.pallas_call(functools.partial(local_kernel, grid_step=grid_step), out_...  17.5 us
    unnamed x16, local copies, waits for them, and re-layouts  4.55 us
  transfers between devices with their start and end apart: 1, of which 1 were waited for; matrix products, arithmetic and copies ran while one was open for 2% of the time, Pallas kernels for 0%

profile of v15, /device:TPU:103, one launch (start us, length us, event | category | flops | bytes accessed | tf_op | source)
XLA Modules:
  0.0 90.3 jit_solution(4116237387968196308)
XLA Ops:
  0.7 0.7 subtract_bitcast_fusion
  1.4 0.1 pad_add_fusion.1.flags
  1.5 0.0 copy-start
  1.5 1.1 %copy-done = s32[2,384,256]{2,1,0:T(8,128)S(1)} copy-done((s32[2,384,256]{2,1,0:T(8,128)S(1)}, s32[2,384,256]{2,1,0:T(8,128)}, u32[]{:S(2)}) %copy-start) | copy-done | bytes 786456
  2.6 0.0 copy-start.1
  2.6 1.1 %copy-done.1 = f32[2,384,256]{2,1,0:T(8,128)S(1)} copy-done((f32[2,384,256]{2,1,0:T(8,128)S(1)}, f32[2,384,256]{2,1,0:T(8,128)}, u32[]{:S(2)}) %copy-start.1) | copy-done | bytes 786456
  3.7 0.0 copy-start.4
  3.7 0.7 copy-done.4
  4.4 17.5 %shard_map.68 = (f32[2,384,256]{2,1,0:T(8,128)S(1)}, f32[2,384,256]{2,1,0:T(8,128)S(1)}, f32[2,384,256]{2,1,0:T(8,128)S(1)}, f32[384,256]{1,0:T(8,128)S(1)}) custom-call(s32[3]{0:T(128)S(1)} %pad_add_fusion.1.flags, s32[3,16]{1,0:T(4,128)S(1)} %pad_add_fusion.stims, f32[16]{0:T(128)S(1)} %copy-done.4, f32[6,2,384,256]{3,2,1,0:T(8,128)} %fibre.1, ...), custom_call_target="tpu_custom_call" | custom-call | flops 58982400 | bytes 7864320 | tf_op jit(solution)/shard_map/pallas_call | solution.py:151
  21.9 0.0 copy-start.2
  21.9 0.9 copy-done.2
  22.8 0.0 copy-start.3
  22.8 0.7 copy-done.3
  23.5 39.6 %shard_map.69 = (f32[384,256]{1,0:T(8,128)}, f32[384,256]{1,0:T(8,128)}, f32[384,256]{1,0:T(8,128)}) custom-call(f32[2,384,256]{2,1,0:T(8,128)} %copy-done.2, f32[384,256]{1,0:T(8,128)} %copy-done.3), custom_call_target="tpu_custom_call" | custom-call | tf_op jit(solution)/shard_map/pallas_call | solution.py:433
  63.1 0.0 copy-start.7
  63.1 1.2 %pad_maximum_fusion = f32[2,384,256]{2,1,0:T(8,128)S(1)} fusion(f32[1,384,256]{2,1,0:T(8,128)} %bitcast.61, f32[1,384,256]{2,1,0:T(8,128)} %bitcast.62), kind=kLoop, calls=%fused_computation | loop fusion | flops 196608 | bytes 1572864 | tf_op jit(solution)/shard_map/stack | solution.py:482
  64.3 0.0 copy-start.5
  64.4 0.0 copy-start.6
  64.4 21.5 %collective-permute-start = (f32[2,384,256]{2,1,0:T(8,128)S(1)}, f32[2,384,256]{2,1,0:T(8,128)}, u32[]{:S(2)}, u32[]{:S(2)}) collective-permute-start(f32[2,384,256]{2,1,0:T(8,128)S(1)} %pad_maximum_fusion), channel_id=1, source_target_pairs={{0,32},{32,0},{64,96},{96,64},{128,160},{160,128},{192,224},{224,1... | collective-permute-start | bytes 2359304 | tf_op jit(solution)/shard_map/ppermute | solution.py:482
  85.9 0.3 minimum_bitcast_fusion
  86.2 0.0 copy-done.7
  86.2 1.1 %fusion.2 = f32[1,2,384,256]{3,2,1,0:T(8,128)} fusion(f32[1,1,384,256]{3,2,1,0:T(8,128)S(1)} %get-tuple-element.25, f32[1,1,384,256]{3,2,1,0:T(8,128)S(1)} %bitcast.60, f32[1,1,384,256]{3,2,1,0:T(8,128)S(1)} %get-tuple-element.23, f32[1,1,384,256]{3,2,1,0:T(8,128)S(1)} %get-tuple-element.28, f32[1,1,384,256]{3,2,1,0:T(8,128)S(1)} %get-tuple-element.19, ...), kind=kLoop, calls=%fused_computation.7 | loop fusion | flops 1572864 | bytes 3932161 | tf_op jit(solution)/shard_map/min | solution.py:496
  87.3 0.6 collective-permute-done
  87.9 0.0 copy-done.5
  87.9 0.0 copy-done.6
  87.9 1.3 %fusion.10 = (f32[384,256]{1,0:T(8,128)S(1)}, f32[384,256]{1,0:T(8,128)S(1)}, f32[1,384,256]{2,1,0:T(8,128)S(1)}, f32[1,384,256]{2,1,0:T(8,128)S(1)}) fusion(f32[384,256]{1,0:T(8,128)S(1)} %copy-done.5, f32[2,384,256]{2,1,0:T(8,128)} %collective-permute-done, pred[]{:T(512)S(6)} %eq.17, f32[2,384,256]{2,1,0:T(8,128)S(1)} %get-tuple-element.13, ...), kind=kLoop, calls=%fused_computation.22 | loop fusion | flops 786432 | bytes 3932161 | tf_op jit(solution)/shard_map/jit(_where)/select_n | solution.py:486
  89.2 1.1 %maximum_minimum_fusion = f32[2,384,256]{2,1,0:T(8,128)} fusion(f32[1,384,256]{2,1,0:T(8,128)S(1)} %get-tuple-element.29, f32[1,384,256]{2,1,0:T(8,128)S(1)} %get-tuple-element.30, f32[1,384,256]{2,1,0:T(8,128)S(1)} %get-tuple-element.24, f32[1,384,256]{2,1,0:T(8,128)S(1)} %get-tuple-element.27, f32[1,384,256]{2,1,0:T(8,128)S(1)} %get-tuple-element.26, ...), kind=kLoop, calls=%fused_computation.1 | loop fusion | flops 1376256 | bytes 3538944 | tf_op jit(solution)/shard_map/min | solution.py:502
  (1 shorter events, 0.0 us)
Async XLA Ops:
  1.5 1.1 %copy-start = (s32[2,384,256]{2,1,0:T(8,128)S(1)}, s32[2,384,256]{2,1,0:T(8,128)}, u32[]{:S(2)}) copy-start(s32[2,384,256]{2,1,0:T(8,128)} %tissue.1) | copy-start | bytes 2359300
  2.6 1.1 %copy-start.1 = (f32[2,384,256]{2,1,0:T(8,128)S(1)}, f32[2,384,256]{2,1,0:T(8,128)}, u32[]{:S(2)}) copy-start(f32[2,384,256]{2,1,0:T(8,128)} %previous.1) | copy-start | bytes 2359300
  3.7 0.7 copy-start.4
  21.9 0.9 copy-start.2
  22.8 0.7 copy-start.3
  63.1 23.1 %copy-start.7 = (f32[384,256]{1,0:T(8,128)S(1)}, f32[384,256]{1,0:T(8,128)}, u32[]{:S(2)}) copy-start(f32[384,256]{1,0:T(8,128)} %get-tuple-element.14) | copy-start | bytes 1179652
  64.3 23.6 %copy-start.5 = (f32[384,256]{1,0:T(8,128)S(1)}, f32[384,256]{1,0:T(8,128)}, u32[]{:S(2)}) copy-start(f32[384,256]{1,0:T(8,128)} %get-tuple-element.12) | copy-start | bytes 1179652
  64.4 23.6 %copy-start.6 = (f32[384,256]{1,0:T(8,128)S(1)}, f32[384,256]{1,0:T(8,128)}, u32[]{:S(2)}) copy-start(f32[384,256]{1,0:T(8,128)} %get-tuple-element.11) | copy-start | bytes 1179652
  64.4 23.6 %collective-permute-start = (f32[2,384,256]{2,1,0:T(8,128)S(1)}, f32[2,384,256]{2,1,0:T(8,128)}, u32[]{:S(2)}, u32[]{:S(2)}) collective-permute-start(f32[2,384,256]{2,1,0:T(8,128)S(1)} %pad_maximum_fusion), channel_id=1, source_target_pairs={{0,32},{32,0},{64,96},{96,64},{128,160},{160,128},{192,224},{224,1... | collective-permute-start | bytes 2359304 | tf_op jit(solution)/shard_map/ppermute | solution.py:482

commit v16 on v14

--- a/solution.py
+++ b/solution.py
@@ -172,11 +172,13 @@
     return out
 
 
-def relay_kernel(totals, own, incoming, least_in, least_plane, before, line_total, box1_in,
-                 box1_out, box2_in, box2_out, box3_in, box4, box5, send1, recv1, send2, recv2, send3,
-                 recv3, send4, recv4, send5, recv5, *, line):
+def relay_kernel(totals, own, incoming, least_both, before, line_total, box1_in, box1_out,
+                 box2_in, box2_out, box3_in, box4, box5, send1, recv1, send2, recv2, send3, recv3,
+                 send4, recv4, send5, recv5, *, line):
     total_add = totals.at[0]
     total_min = totals.at[1]
+    least_plane = least_both.at[0]
+    least_in = least_both.at[1]
     cells_y, cells_z = incoming.shape
     chunks = cells_y // RELAY_ROWS
     slabs = lax.axis_size("slab")
@@ -429,9 +431,9 @@
     pair_box = pltpu.VMEM((chunks, 2, RELAY_ROWS, cells_z), jnp.float32)
     return pl.pallas_call(
         functools.partial(relay_kernel, line=line),
-        out_shape=(plane, plane, plane),
+        out_shape=(plane, jax.ShapeDtypeStruct((2,) + own.shape, jnp.float32)),
         in_specs=[vmem, vmem],
-        out_specs=(vmem, vmem, vmem),
+        out_specs=(vmem, vmem),
         scratch_shapes=[
             pltpu.VMEM((2, cells_y, cells_z), jnp.float32),
             pltpu.VMEM((2, cells_y, cells_z), jnp.float32),
@@ -475,8 +477,10 @@
         bits, stims, stim_times, fibre_tensor, tissue, previous, grid_step)
 
     core = group_index % 2
-    incoming, least_in, least_plane = relay(totals, own_plane, slabs, orders)
-    other = lax.ppermute(jnp.stack([least_plane, least_in]), "order", [(g, g ^ 1) for g in range(orders)])
+    incoming, least_both = relay(totals, own_plane, slabs, orders)
+    least_plane = least_both[0]
+    least_in = least_both[1]
+    other = lax.ppermute(least_both, "order", [(g, g ^ 1) for g in range(orders)])
 
     least0 = jnp.where(core == 0, least_plane, other[0])
     least1 = jnp.where(core == 0, other[0], least_plane)

time: 88.4 us -> 88.4 us (level)
  waiting for transfers between devices: 0.61 us -> 1.95 us
  other arithmetic: 5.73 us -> 4.54 us
    add x0 -> x1, other arithmetic: none -> 1.48 us  [shards(): up_in[None] + up_add]
    another operation x2 -> x1, other arithmetic: 1.52 us -> 0.16 us  [shards(): up_add = jnp.stack([cost_x[0], cost_x[0] + cost_x[1]])]
    ppermute x1, waiting for transfers between devices: 0.61 us -> 1.95 us  [shards(): lax.ppermute(least_both, 'order', [(g, g ^ 1) for g in range(orders)])]
    select_n x1 -> x0, other arithmetic: 1.27 us -> none  [shards(): up_in = jnp.where(core == 0, least_in, other[1])]
    unnamed x16 -> x12, local copies, waits for them, and re-layouts: 4.55 us -> 4.54 us
  transfers between devices with their start and end apart: 1 -> 1, of which waited for: 1 -> 1; matrix products, arithmetic and copies ran while one was open for 2% -> 0% of each run, Pallas kernels for 0% -> 0%
where the time goes in v16:
time: 88.4 us; the launch traced here: 88.2 us
  Pallas kernels  56.8 us (64%)
  starting transfers between devices  19.6 us (22%)
  other arithmetic  4.54 us (5%)
  local copies, waits for them, and re-layouts  4.54 us (5%)
  waiting for transfers between devices  1.95 us (2%)
    pallas_call x1, Pallas kernels, relay(): pl.pallas_call(functools.partial(relay_kernel, line=line), out_shape=(pla...  39.3 us
    ppermute x1, starting transfers between devices, shards(): lax.ppermute(least_both, 'order', [(g, g ^ 1) for g in range(orders)])  19.6 us
    pallas_call x1, Pallas kernels, local_sweeps(): pl.pallas_call(functools.partial(local_kernel, grid_step=grid_step), out_...  17.5 us
    unnamed x12, local copies, waits for them, and re-layouts  4.54 us
    ppermute x1, waiting for transfers between devices, shards(): lax.ppermute(least_both, 'order', [(g, g ^ 1) for g in range(orders)])  1.95 us
  transfers between devices with their start and end apart: 1, of which 1 were waited for; matrix products, arithmetic and copies ran while one was open for 0% of the time, Pallas kernels for 0%

profile of v16, /device:TPU:103, one launch (start us, length us, event | category | flops | bytes accessed | tf_op | source)
XLA Modules:
  0.0 88.2 jit_solution(8588434851183371625)
XLA Ops:
  0.7 0.7 subtract_bitcast_fusion
  1.4 0.1 pad_add_fusion.1.flags
  1.5 0.0 copy-start
  1.5 1.1 %copy-done = s32[2,384,256]{2,1,0:T(8,128)S(1)} copy-done((s32[2,384,256]{2,1,0:T(8,128)S(1)}, s32[2,384,256]{2,1,0:T(8,128)}, u32[]{:S(2)}) %copy-start) | copy-done | bytes 786456
  2.6 0.0 copy-start.1
  2.6 1.1 %copy-done.1 = f32[2,384,256]{2,1,0:T(8,128)S(1)} copy-done((f32[2,384,256]{2,1,0:T(8,128)S(1)}, f32[2,384,256]{2,1,0:T(8,128)}, u32[]{:S(2)}) %copy-start.1) | copy-done | bytes 786456
  3.7 0.0 copy-start.4
  3.7 0.7 copy-done.4
  4.4 17.5 %shard_map.68 = (f32[2,384,256]{2,1,0:T(8,128)S(1)}, f32[2,384,256]{2,1,0:T(8,128)S(1)}, f32[2,384,256]{2,1,0:T(8,128)S(1)}, f32[384,256]{1,0:T(8,128)S(1)}) custom-call(s32[3]{0:T(128)S(1)} %pad_add_fusion.1.flags, s32[3,16]{1,0:T(4,128)S(1)} %pad_add_fusion.stims, f32[16]{0:T(128)S(1)} %copy-done.4, f32[6,2,384,256]{3,2,1,0:T(8,128)} %fibre.1, ...), custom_call_target="tpu_custom_call" | custom-call | flops 58982400 | bytes 7864320 | tf_op jit(solution)/shard_map/pallas_call | solution.py:151
  21.9 0.0 copy-start.2
  21.9 0.9 copy-done.2
  22.8 0.0 copy-start.3
  22.8 0.7 copy-done.3
  23.5 39.3 %shard_map.69 = (f32[384,256]{1,0:T(8,128)}, f32[2,384,256]{2,1,0:T(8,128)}) custom-call(f32[2,384,256]{2,1,0:T(8,128)} %copy-done.2, f32[384,256]{1,0:T(8,128)} %copy-done.3), custom_call_target="tpu_custom_call" | custom-call | tf_op jit(solution)/shard_map/pallas_call | solution.py:432
  62.8 19.6 %collective-permute-start = (f32[2,384,256]{2,1,0:T(8,128)}, f32[2,384,256]{2,1,0:T(8,128)S(1)}, u32[]{:S(2)}, u32[]{:S(2)}) collective-permute-start(f32[2,384,256]{2,1,0:T(8,128)} %get-tuple-element.10), channel_id=1, source_target_pairs={{0,32},{32,0},{64,96},{96,64},{128,160},{160,128},{192,224},{224,1... | collective-permute-start | bytes 2359304 | tf_op jit(solution)/shard_map/ppermute | solution.py:483
  82.4 0.2 slice_bitcast_fusion.3
  82.6 2.0 %collective-permute-done = f32[2,384,256]{2,1,0:T(8,128)S(1)} collective-permute-done((f32[2,384,256]{2,1,0:T(8,128)}, f32[2,384,256]{2,1,0:T(8,128)S(1)}, u32[]{:S(2)}, u32[]{:S(2)}) %collective-permute-start) | collective-permute-done | bytes 786464 | tf_op jit(solution)/shard_map/ppermute | solution.py:483
  84.5 0.0 copy-start.5
  84.5 1.5 %select_bitcast_fusion.1 = (f32[384,256]{1,0:T(8,128)S(1)}, f32[384,256]{1,0:T(8,128)S(1)}, f32[1,384,256]{2,1,0:T(8,128)S(1)}, f32[1,384,256]{2,1,0:T(8,128)S(1...) fusion(f32[2,384,256]{2,1,0:T(8,128)S(1)} %collective-permute-d, ...), kind=kLoop, calls=%fused_computation.11 | loop fusion | flops 1179648 | bytes 6291457 | tf_op jit(solution)/shard_map/add | solution.py:505
  86.0 1.1 %maximum_minimum_fusion = f32[2,384,256]{2,1,0:T(8,128)} fusion(f32[1,384,256]{2,1,0:T(8,128)S(1)} %get-tuple-element.20, f32[1,384,256]{2,1,0:T(8,128)S(1)} %get-tuple-element.21, f32[1,384,256]{2,1,0:T(8,128)S(1)} %get-tuple-element.27, f32[1,384,256]{2,1,0:T(8,128)S(1)} %get-tuple-element.30, f32[1,384,256]{2,1,0:T(8,128)S(1)} %get-tuple-element.29, ...), kind=kLoop, calls=%fused_computation | loop fusion | flops 1376256 | bytes 3538944 | tf_op jit(solution)/shard_map/min | solution.py:503
  87.1 0.0 copy-done.5
  87.1 1.1 %fusion.2 = f32[1,2,384,256]{3,2,1,0:T(8,128)} fusion(f32[1,1,384,256]{3,2,1,0:T(8,128)S(1)} %get-tuple-element.28, f32[1,1,384,256]{3,2,1,0:T(8,128)S(1)} %bitcast.26, f32[1,1,384,256]{3,2,1,0:T(8,128)S(1)} %get-tuple-element.26, f32[1,1,384,256]{3,2,1,0:T(8,128)S(1)} %get-tuple-element.25, f32[1,1,384,256]{3,2,1,0:T(8,128)S(1)} %get-tuple-element.22, ...), kind=kLoop, calls=%fused_computation.6 | loop fusion | flops 1572864 | bytes 3932161 | tf_op jit(solution)/shard_map/min | solution.py:497
  (1 shorter events, 0.0 us)
Async XLA Ops:
  1.5 1.1 %copy-start = (s32[2,384,256]{2,1,0:T(8,128)S(1)}, s32[2,384,256]{2,1,0:T(8,128)}, u32[]{:S(2)}) copy-start(s32[2,384,256]{2,1,0:T(8,128)} %tissue.1) | copy-start | bytes 2359300
  2.6 1.1 %copy-start.1 = (f32[2,384,256]{2,1,0:T(8,128)S(1)}, f32[2,384,256]{2,1,0:T(8,128)}, u32[]{:S(2)}) copy-start(f32[2,384,256]{2,1,0:T(8,128)} %previous.1) | copy-start | bytes 2359300
  3.7 0.7 copy-start.4
  21.9 0.9 %copy-start.2 = (f32[2,384,256]{2,1,0:T(8,128)}, f32[2,384,256]{2,1,0:T(8,128)S(1)}, u32[]{:S(2)}) copy-start(f32[2,384,256]{2,1,0:T(8,128)S(1)} %get-tuple-element.8.totals) | copy-start | bytes 2359300
  22.8 0.7 copy-start.3
  62.8 21.7 %collective-permute-start = (f32[2,384,256]{2,1,0:T(8,128)}, f32[2,384,256]{2,1,0:T(8,128)S(1)}, u32[]{:S(2)}, u32[]{:S(2)}) collective-permute-start(f32[2,384,256]{2,1,0:T(8,128)} %get-tuple-element.10), channel_id=1, source_target_pairs={{0,32},{32,0},{64,96},{96,64},{128,160},{160,128},{192,224},{224,1... | collective-permute-start | bytes 2359304 | tf_op jit(solution)/shard_map/ppermute | solution.py:483
  84.5 2.5 %copy-start.5 = (f32[384,256]{1,0:T(8,128)S(1)}, f32[384,256]{1,0:T(8,128)}, u32[]{:S(2)}) copy-start(f32[384,256]{1,0:T(8,128)} %get-tuple-element.12) | copy-start | bytes 1179652

commit v17 on v14

--- a/solution.py
+++ b/solution.py
@@ -55,12 +55,14 @@
 
 
 def local_kernel(flags, stims, stim_times, fibre, tissue, previous, cost_x, field, totals, own,
-                 cost_y, *, grid_step):
+                 cost_y, dma, *, grid_step):
     planes, cells_y, cells_z = previous.shape
     chunks = cells_y // CHUNK
     inf = jnp.float32(jnp.inf)
 
-    field[...] = previous[...]
+    seed_copy = pltpu.make_async_copy(previous, field, dma)
+    seed_copy.start()
+    seed_copy.wait()
 
     def seed(k, carry):
         p = stims[0, k]
@@ -153,7 +155,7 @@
         out_shape=(field, field, totals, own),
         in_specs=[smem, smem, smem, vmem, vmem, vmem],
         out_specs=(vmem, vmem, vmem, vmem),
-        scratch_shapes=[pltpu.VMEM(previous.shape, jnp.float32)],
+        scratch_shapes=[pltpu.VMEM(previous.shape, jnp.float32), pltpu.SemaphoreType.DMA(())],
         compiler_params=pltpu.CompilerParams(vmem_limit_bytes=48 * 1024 * 1024),
         cost_estimate=pl.CostEstimate(
             flops=300 * elements, transcendentals=6 * elements, bytes_accessed=40 * elements

time: 88.4 us -> 88.4 us (level)
  no operation moved by 1% of the time
where the time goes in v17:
time: 88.4 us; the launch traced here: 88.1 us
  Pallas kernels  56.9 us (64%)
  starting transfers between devices  19.6 us (22%)
  other arithmetic  5.73 us (6%)
  local copies, waits for them, and re-layouts  4.55 us (5%)
    pallas_call x1, Pallas kernels, relay(): pl.pallas_call(functools.partial(relay_kernel, line=line), out_shape=(pla...  39.3 us
    ppermute x1, starting transfers between devices, shards(): lax.ppermute(jnp.stack([least_plane, least_in]), 'order', [(g, g ^ 1) for...  19.6 us
    pallas_call x1, Pallas kernels, local_sweeps(): pl.pallas_call(functools.partial(local_kernel, grid_step=grid_step), out_...  17.5 us
    unnamed x16, local copies, waits for them, and re-layouts  4.55 us
  transfers between devices with their start and end apart: 1, of which 1 were waited for; matrix products, arithmetic and copies ran while one was open for 2% of the time, Pallas kernels for 0%

profile of v17, /device:TPU:103, one launch (start us, length us, event | category | flops | bytes accessed | tf_op | source)
XLA Modules:
  0.0 88.1 jit_solution(16220536951506093553)
XLA Ops:
  0.7 0.7 subtract_bitcast_fusion
  1.4 0.1 pad_add_fusion.1.flags
  1.5 0.0 copy-start
  1.5 1.1 %copy-done = s32[2,384,256]{2,1,0:T(8,128)S(1)} copy-done((s32[2,384,256]{2,1,0:T(8,128)S(1)}, s32[2,384,256]{2,1,0:T(8,128)}, u32[]{:S(2)}) %copy-start) | copy-done | bytes 786456
  2.6 0.0 copy-start.1
  2.6 1.1 %copy-done.1 = f32[2,384,256]{2,1,0:T(8,128)S(1)} copy-done((f32[2,384,256]{2,1,0:T(8,128)S(1)}, f32[2,384,256]{2,1,0:T(8,128)}, u32[]{:S(2)}) %copy-start.1) | copy-done | bytes 786456
  3.7 0.0 copy-start.4
  3.7 0.7 copy-done.4
  4.4 17.5 %shard_map.68 = (f32[2,384,256]{2,1,0:T(8,128)S(1)}, f32[2,384,256]{2,1,0:T(8,128)S(1)}, f32[2,384,256]{2,1,0:T(8,128)S(1)}, f32[384,256]{1,0:T(8,128)S(1)}) custom-call(s32[3]{0:T(128)S(1)} %pad_add_fusion.1.flags, s32[3,16]{1,0:T(4,128)S(1)} %pad_add_fusion.stims, f32[16]{0:T(128)S(1)} %copy-done.4, f32[6,2,384,256]{3,2,1,0:T(8,128)} %fibre.1, ...), custom_call_target="tpu_custom_call" | custom-call | flops 58982400 | bytes 7864320 | tf_op jit(solution)/shard_map/pallas_call | solution.py:153
  21.9 0.0 copy-start.2
  21.9 0.9 copy-done.2
  22.8 0.0 copy-start.3
  22.8 0.7 copy-done.3
  23.5 39.3 %shard_map.69 = (f32[384,256]{1,0:T(8,128)}, f32[384,256]{1,0:T(8,128)}, f32[384,256]{1,0:T(8,128)}) custom-call(f32[2,384,256]{2,1,0:T(8,128)} %copy-done.2, f32[384,256]{1,0:T(8,128)} %copy-done.3), custom_call_target="tpu_custom_call" | custom-call | tf_op jit(solution)/shard_map/pallas_call | solution.py:432
  62.9 0.0 copy-start.7
  62.9 1.2 %pad_maximum_fusion = f32[2,384,256]{2,1,0:T(8,128)S(1)} fusion(f32[1,384,256]{2,1,0:T(8,128)} %bitcast.61, f32[1,384,256]{2,1,0:T(8,128)} %bitcast.62), kind=kLoop, calls=%fused_computation | loop fusion | flops 196608 | bytes 1572864 | tf_op jit(solution)/shard_map/stack | solution.py:481
  64.1 0.0 copy-start.5
  64.1 0.0 copy-start.6
  64.1 19.6 %collective-permute-start = (f32[2,384,256]{2,1,0:T(8,128)S(1)}, f32[2,384,256]{2,1,0:T(8,128)}, u32[]{:S(2)}, u32[]{:S(2)}) collective-permute-start(f32[2,384,256]{2,1,0:T(8,128)S(1)} %pad_maximum_fusion), channel_id=1, source_target_pairs={{0,32},{32,0},{64,96},{96,64},{128,160},{160,128},{192,224},{224,1... | collective-permute-start | bytes 2359304 | tf_op jit(solution)/shard_map/ppermute | solution.py:481
  83.7 0.3 minimum_bitcast_fusion
  84.0 0.0 copy-done.7
  84.0 1.1 %fusion.2 = f32[1,2,384,256]{3,2,1,0:T(8,128)} fusion(f32[1,1,384,256]{3,2,1,0:T(8,128)S(1)} %get-tuple-element.25, f32[1,1,384,256]{3,2,1,0:T(8,128)S(1)} %bitcast.60, f32[1,1,384,256]{3,2,1,0:T(8,128)S(1)} %get-tuple-element.23, f32[1,1,384,256]{3,2,1,0:T(8,128)S(1)} %get-tuple-element.28, f32[1,1,384,256]{3,2,1,0:T(8,128)S(1)} %get-tuple-element.19, ...), kind=kLoop, calls=%fused_computation.7 | loop fusion | flops 1572864 | bytes 3932161 | tf_op jit(solution)/shard_map/min | solution.py:495
  85.2 0.6 collective-permute-done
  85.8 0.0 copy-done.5
  85.8 0.0 copy-done.6
  85.8 1.3 %fusion.10 = (f32[384,256]{1,0:T(8,128)S(1)}, f32[384,256]{1,0:T(8,128)S(1)}, f32[1,384,256]{2,1,0:T(8,128)S(1)}, f32[1,384,256]{2,1,0:T(8,128)S(1)}) fusion(f32[384,256]{1,0:T(8,128)S(1)} %copy-done.5, f32[2,384,256]{2,1,0:T(8,128)} %collective-permute-done, pred[]{:T(512)S(6)} %eq.17, f32[2,384,256]{2,1,0:T(8,128)S(1)} %get-tuple-element.13, ...), kind=kLoop, calls=%fused_computation.22 | loop fusion | flops 786432 | bytes 3932161 | tf_op jit(solution)/shard_map/jit(_where)/select_n | solution.py:485
  87.0 1.1 %maximum_minimum_fusion = f32[2,384,256]{2,1,0:T(8,128)} fusion(f32[1,384,256]{2,1,0:T(8,128)S(1)} %get-tuple-element.29, f32[1,384,256]{2,1,0:T(8,128)S(1)} %get-tuple-element.30, f32[1,384,256]{2,1,0:T(8,128)S(1)} %get-tuple-element.24, f32[1,384,256]{2,1,0:T(8,128)S(1)} %get-tuple-element.27, f32[1,384,256]{2,1,0:T(8,128)S(1)} %get-tuple-element.26, ...), kind=kLoop, calls=%fused_computation.1 | loop fusion | flops 1376256 | bytes 3538944 | tf_op jit(solution)/shard_map/min | solution.py:501
  (1 shorter events, 0.0 us)
Async XLA Ops:
  1.5 1.1 %copy-start = (s32[2,384,256]{2,1,0:T(8,128)S(1)}, s32[2,384,256]{2,1,0:T(8,128)}, u32[]{:S(2)}) copy-start(s32[2,384,256]{2,1,0:T(8,128)} %tissue.1) | copy-start | bytes 2359300
  2.6 1.1 %copy-start.1 = (f32[2,384,256]{2,1,0:T(8,128)S(1)}, f32[2,384,256]{2,1,0:T(8,128)}, u32[]{:S(2)}) copy-start(f32[2,384,256]{2,1,0:T(8,128)} %previous.1) | copy-start | bytes 2359300
  3.7 0.7 copy-start.4
  21.9 0.9 %copy-start.2 = (f32[2,384,256]{2,1,0:T(8,128)}, f32[2,384,256]{2,1,0:T(8,128)S(1)}, u32[]{:S(2)}) copy-start(f32[2,384,256]{2,1,0:T(8,128)S(1)} %get-tuple-element.9.totals) | copy-start | bytes 2359300
  22.8 0.7 copy-start.3
  62.9 21.1 %copy-start.7 = (f32[384,256]{1,0:T(8,128)S(1)}, f32[384,256]{1,0:T(8,128)}, u32[]{:S(2)}) copy-start(f32[384,256]{1,0:T(8,128)} %get-tuple-element.14) | copy-start | bytes 1179652
  64.1 21.6 %copy-start.5 = (f32[384,256]{1,0:T(8,128)S(1)}, f32[384,256]{1,0:T(8,128)}, u32[]{:S(2)}) copy-start(f32[384,256]{1,0:T(8,128)} %get-tuple-element.12) | copy-start | bytes 1179652
  64.1 21.6 %copy-start.6 = (f32[384,256]{1,0:T(8,128)S(1)}, f32[384,256]{1,0:T(8,128)}, u32[]{:S(2)}) copy-start(f32[384,256]{1,0:T(8,128)} %get-tuple-element.11) | copy-start | bytes 1179652
  64.1 21.6 %collective-permute-start = (f32[2,384,256]{2,1,0:T(8,128)S(1)}, f32[2,384,256]{2,1,0:T(8,128)}, u32[]{:S(2)}, u32[]{:S(2)}) collective-permute-start(f32[2,384,256]{2,1,0:T(8,128)S(1)} %pad_maximum_fusion), channel_id=1, source_target_pairs={{0,32},{32,0},{64,96},{96,64},{128,160},{160,128},{192,224},{224,1... | collective-permute-start | bytes 2359304 | tf_op jit(solution)/shard_map/ppermute | solution.py:481

commit v18 on v14

--- a/solution.py
+++ b/solution.py
@@ -161,7 +161,7 @@
     )(flags, stims, stim_times, fibre, tissue, previous)
 
 
-RELAY_ROWS = 16
+RELAY_ROWS = 24
 LINE = 8
 
 

time: 88.4 us -> 88.8 us (level)
  starting transfers between devices: 19.6 us -> 20.8 us
    ppermute x1, starting transfers between devices: 19.6 us -> 20.8 us  [shards(): lax.ppermute(jnp.stack([least_plane, least_in]), 'order', [(g, g ^ 1) for...]
where the time goes in v18:
time: 88.8 us; the launch traced here: 88.5 us
  Pallas kernels  56 us (63%)
  starting transfers between devices  20.8 us (23%)
  other arithmetic  5.73 us (6%)
  local copies, waits for them, and re-layouts  4.55 us (5%)
    pallas_call x1, Pallas kernels, relay(): pl.pallas_call(functools.partial(relay_kernel, line=line), out_shape=(pla...  38.5 us
    ppermute x1, starting transfers between devices, shards(): lax.ppermute(jnp.stack([least_plane, least_in]), 'order', [(g, g ^ 1) for...  20.8 us
    pallas_call x1, Pallas kernels, local_sweeps(): pl.pallas_call(functools.partial(local_kernel, grid_step=grid_step), out_...  17.5 us
    unnamed x16, local copies, waits for them, and re-layouts  4.55 us
  transfers between devices with their start and end apart: 1, of which 1 were waited for; matrix products, arithmetic and copies ran while one was open for 2% of the time, Pallas kernels for 0%

profile of v18, /device:TPU:103, one launch (start us, length us, event | category | flops | bytes accessed | tf_op | source)
XLA Modules:
  0.0 88.5 jit_solution(9411241089305429738)
XLA Ops:
  0.7 0.7 subtract_bitcast_fusion
  1.4 0.1 pad_add_fusion.1.flags
  1.5 0.0 copy-start
  1.5 1.1 %copy-done = s32[2,384,256]{2,1,0:T(8,128)S(1)} copy-done((s32[2,384,256]{2,1,0:T(8,128)S(1)}, s32[2,384,256]{2,1,0:T(8,128)}, u32[]{:S(2)}) %copy-start) | copy-done | bytes 786456
  2.6 0.0 copy-start.1
  2.6 1.1 %copy-done.1 = f32[2,384,256]{2,1,0:T(8,128)S(1)} copy-done((f32[2,384,256]{2,1,0:T(8,128)S(1)}, f32[2,384,256]{2,1,0:T(8,128)}, u32[]{:S(2)}) %copy-start.1) | copy-done | bytes 786456
  3.7 0.0 copy-start.4
  3.7 0.7 copy-done.4
  4.4 17.5 %shard_map.68 = (f32[2,384,256]{2,1,0:T(8,128)S(1)}, f32[2,384,256]{2,1,0:T(8,128)S(1)}, f32[2,384,256]{2,1,0:T(8,128)S(1)}, f32[384,256]{1,0:T(8,128)S(1)}) custom-call(s32[3]{0:T(128)S(1)} %pad_add_fusion.1.flags, s32[3,16]{1,0:T(4,128)S(1)} %pad_add_fusion.stims, f32[16]{0:T(128)S(1)} %copy-done.4, f32[6,2,384,256]{3,2,1,0:T(8,128)} %fibre.1, ...), custom_call_target="tpu_custom_call" | custom-call | flops 58982400 | bytes 7864320 | tf_op jit(solution)/shard_map/pallas_call | solution.py:151
  21.9 0.0 copy-start.2
  21.9 0.9 copy-done.2
  22.8 0.0 copy-start.3
  22.8 0.7 copy-done.3
  23.5 38.5 %shard_map.69 = (f32[384,256]{1,0:T(8,128)}, f32[384,256]{1,0:T(8,128)}, f32[384,256]{1,0:T(8,128)}) custom-call(f32[2,384,256]{2,1,0:T(8,128)} %copy-done.2, f32[384,256]{1,0:T(8,128)} %copy-done.3), custom_call_target="tpu_custom_call" | custom-call | tf_op jit(solution)/shard_map/pallas_call | solution.py:430
  62.0 0.0 copy-start.7
  62.0 1.2 %pad_maximum_fusion = f32[2,384,256]{2,1,0:T(8,128)S(1)} fusion(f32[1,384,256]{2,1,0:T(8,128)} %bitcast.61, f32[1,384,256]{2,1,0:T(8,128)} %bitcast.62), kind=kLoop, calls=%fused_computation | loop fusion | flops 196608 | bytes 1572864 | tf_op jit(solution)/shard_map/stack | solution.py:479
  63.2 0.0 copy-start.5
  63.3 0.0 copy-start.6
  63.3 20.8 %collective-permute-start = (f32[2,384,256]{2,1,0:T(8,128)S(1)}, f32[2,384,256]{2,1,0:T(8,128)}, u32[]{:S(2)}, u32[]{:S(2)}) collective-permute-start(f32[2,384,256]{2,1,0:T(8,128)S(1)} %pad_maximum_fusion), channel_id=1, source_target_pairs={{0,32},{32,0},{64,96},{96,64},{128,160},{160,128},{192,224},{224,1... | collective-permute-start | bytes 2359304 | tf_op jit(solution)/shard_map/ppermute | solution.py:479
  84.1 0.3 minimum_bitcast_fusion
  84.4 0.0 copy-done.7
  84.4 1.1 %fusion.2 = f32[1,2,384,256]{3,2,1,0:T(8,128)} fusion(f32[1,1,384,256]{3,2,1,0:T(8,128)S(1)} %get-tuple-element.25, f32[1,1,384,256]{3,2,1,0:T(8,128)S(1)} %bitcast.60, f32[1,1,384,256]{3,2,1,0:T(8,128)S(1)} %get-tuple-element.23, f32[1,1,384,256]{3,2,1,0:T(8,128)S(1)} %get-tuple-element.28, f32[1,1,384,256]{3,2,1,0:T(8,128)S(1)} %get-tuple-element.19, ...), kind=kLoop, calls=%fused_computation.7 | loop fusion | flops 1572864 | bytes 3932161 | tf_op jit(solution)/shard_map/min | solution.py:493
  85.5 0.6 collective-permute-done
  86.1 0.0 copy-done.5
  86.1 0.0 copy-done.6
  86.1 1.3 %fusion.10 = (f32[384,256]{1,0:T(8,128)S(1)}, f32[384,256]{1,0:T(8,128)S(1)}, f32[1,384,256]{2,1,0:T(8,128)S(1)}, f32[1,384,256]{2,1,0:T(8,128)S(1)}) fusion(f32[384,256]{1,0:T(8,128)S(1)} %copy-done.5, f32[2,384,256]{2,1,0:T(8,128)} %collective-permute-done, pred[]{:T(512)S(6)} %eq.17, f32[2,384,256]{2,1,0:T(8,128)S(1)} %get-tuple-element.13, ...), kind=kLoop, calls=%fused_computation.22 | loop fusion | flops 786432 | bytes 3932161 | tf_op jit(solution)/shard_map/jit(_where)/select_n | solution.py:483
  87.4 1.1 %maximum_minimum_fusion = f32[2,384,256]{2,1,0:T(8,128)} fusion(f32[1,384,256]{2,1,0:T(8,128)S(1)} %get-tuple-element.29, f32[1,384,256]{2,1,0:T(8,128)S(1)} %get-tuple-element.30, f32[1,384,256]{2,1,0:T(8,128)S(1)} %get-tuple-element.24, f32[1,384,256]{2,1,0:T(8,128)S(1)} %get-tuple-element.27, f32[1,384,256]{2,1,0:T(8,128)S(1)} %get-tuple-element.26, ...), kind=kLoop, calls=%fused_computation.1 | loop fusion | flops 1376256 | bytes 3538944 | tf_op jit(solution)/shard_map/min | solution.py:499
  (1 shorter events, 0.0 us)
Async XLA Ops:
  1.5 1.1 %copy-start = (s32[2,384,256]{2,1,0:T(8,128)S(1)}, s32[2,384,256]{2,1,0:T(8,128)}, u32[]{:S(2)}) copy-start(s32[2,384,256]{2,1,0:T(8,128)} %tissue.1) | copy-start | bytes 2359300
  2.6 1.1 %copy-start.1 = (f32[2,384,256]{2,1,0:T(8,128)S(1)}, f32[2,384,256]{2,1,0:T(8,128)}, u32[]{:S(2)}) copy-start(f32[2,384,256]{2,1,0:T(8,128)} %previous.1) | copy-start | bytes 2359300
  3.7 0.7 copy-start.4
  21.9 0.9 copy-start.2
  22.8 0.7 copy-start.3
  62.0 22.4 %copy-start.7 = (f32[384,256]{1,0:T(8,128)S(1)}, f32[384,256]{1,0:T(8,128)}, u32[]{:S(2)}) copy-start(f32[384,256]{1,0:T(8,128)} %get-tuple-element.14) | copy-start | bytes 1179652
  63.2 22.9 %copy-start.5 = (f32[384,256]{1,0:T(8,128)S(1)}, f32[384,256]{1,0:T(8,128)}, u32[]{:S(2)}) copy-start(f32[384,256]{1,0:T(8,128)} %get-tuple-element.12) | copy-start | bytes 1179652
  63.3 22.9 %copy-start.6 = (f32[384,256]{1,0:T(8,128)S(1)}, f32[384,256]{1,0:T(8,128)}, u32[]{:S(2)}) copy-start(f32[384,256]{1,0:T(8,128)} %get-tuple-element.11) | copy-start | bytes 1179652
  63.3 22.9 %collective-permute-start = (f32[2,384,256]{2,1,0:T(8,128)S(1)}, f32[2,384,256]{2,1,0:T(8,128)}, u32[]{:S(2)}, u32[]{:S(2)}) collective-permute-start(f32[2,384,256]{2,1,0:T(8,128)S(1)} %pad_maximum_fusion), channel_id=1, source_target_pairs={{0,32},{32,0},{64,96},{96,64},{128,160},{160,128},{192,224},{224,1... | collective-permute-start | bytes 2359304 | tf_op jit(solution)/shard_map/ppermute | solution.py:479

commit v19 on v14

--- a/solution.py
+++ b/solution.py
@@ -274,14 +274,14 @@
         def _():
             box1_out[c, 0] = own_add
             box1_out[c, 1] = own_min
+            if last > 0:
+                copy1(c).start()
 
         @pl.when(pos > 0)
         def _():
             copy1(c).wait_recv()
             got_add = box1_in[c, 0]
             got_min = box1_in[c, 1]
-            before[0, rows, :] = got_add
-            before[1, rows, :] = got_min
             new_add = got_add + own_add
             new_min = jnp.minimum(got_min + own_add, own_min)
 
@@ -289,6 +289,10 @@
             def _():
                 box1_out[c, 0] = new_add
                 box1_out[c, 1] = new_min
+                copy1(c).start()
+
+            before[0, rows, :] = got_add
+            before[1, rows, :] = got_min
 
             @pl.when(is_end)
             def _():
@@ -299,10 +303,6 @@
         def _():
             line_total[0, rows, :] = own_add
             line_total[1, rows, :] = own_min
-
-        @pl.when(pos < last)
-        def _():
-            copy1(c).start()
 
         return carry
 

time: 88.4 us -> 88.4 us (level)
  no operation moved by 1% of the time
where the time goes in v19:
time: 88.4 us; the launch traced here: 88.1 us
  Pallas kernels  56.8 us (64%)
  starting transfers between devices  19.6 us (22%)
  other arithmetic  5.73 us (6%)
  local copies, waits for them, and re-layouts  4.55 us (5%)
    pallas_call x1, Pallas kernels, relay(): pl.pallas_call(functools.partial(relay_kernel, line=line), out_shape=(pla...  39.3 us
    ppermute x1, starting transfers between devices, shards(): lax.ppermute(jnp.stack([least_plane, least_in]), 'order', [(g, g ^ 1) for...  19.6 us
    pallas_call x1, Pallas kernels, local_sweeps(): pl.pallas_call(functools.partial(local_kernel, grid_step=grid_step), out_...  17.5 us
    unnamed x16, local copies, waits for them, and re-layouts  4.55 us
  transfers between devices with their start and end apart: 1, of which 1 were waited for; matrix products, arithmetic and copies ran while one was open for 2% of the time, Pallas kernels for 0%

profile of v19, /device:TPU:103, one launch (start us, length us, event | category | flops | bytes accessed | tf_op | source)
XLA Modules:
  0.0 88.1 jit_solution(11578520773484381958)
XLA Ops:
  0.7 0.7 subtract_bitcast_fusion
  1.4 0.1 pad_add_fusion.1.flags
  1.5 0.0 copy-start
  1.5 1.1 %copy-done = s32[2,384,256]{2,1,0:T(8,128)S(1)} copy-done((s32[2,384,256]{2,1,0:T(8,128)S(1)}, s32[2,384,256]{2,1,0:T(8,128)}, u32[]{:S(2)}) %copy-start) | copy-done | bytes 786456
  2.6 0.0 copy-start.1
  2.6 1.1 %copy-done.1 = f32[2,384,256]{2,1,0:T(8,128)S(1)} copy-done((f32[2,384,256]{2,1,0:T(8,128)S(1)}, f32[2,384,256]{2,1,0:T(8,128)}, u32[]{:S(2)}) %copy-start.1) | copy-done | bytes 786456
  3.7 0.0 copy-start.4
  3.7 0.7 copy-done.4
  4.4 17.5 %shard_map.68 = (f32[2,384,256]{2,1,0:T(8,128)S(1)}, f32[2,384,256]{2,1,0:T(8,128)S(1)}, f32[2,384,256]{2,1,0:T(8,128)S(1)}, f32[384,256]{1,0:T(8,128)S(1)}) custom-call(s32[3]{0:T(128)S(1)} %pad_add_fusion.1.flags, s32[3,16]{1,0:T(4,128)S(1)} %pad_add_fusion.stims, f32[16]{0:T(128)S(1)} %copy-done.4, f32[6,2,384,256]{3,2,1,0:T(8,128)} %fibre.1, ...), custom_call_target="tpu_custom_call" | custom-call | flops 58982400 | bytes 7864320 | tf_op jit(solution)/shard_map/pallas_call | solution.py:151
  21.9 0.0 copy-start.2
  21.9 0.9 copy-done.2
  22.8 0.0 copy-start.3
  22.8 0.7 copy-done.3
  23.5 39.3 %shard_map.69 = (f32[384,256]{1,0:T(8,128)}, f32[384,256]{1,0:T(8,128)}, f32[384,256]{1,0:T(8,128)}) custom-call(f32[2,384,256]{2,1,0:T(8,128)} %copy-done.2, f32[384,256]{1,0:T(8,128)} %copy-done.3), custom_call_target="tpu_custom_call" | custom-call | tf_op jit(solution)/shard_map/pallas_call | solution.py:430
  62.9 0.0 copy-start.7
  62.9 1.2 %pad_maximum_fusion = f32[2,384,256]{2,1,0:T(8,128)S(1)} fusion(f32[1,384,256]{2,1,0:T(8,128)} %bitcast.61, f32[1,384,256]{2,1,0:T(8,128)} %bitcast.62), kind=kLoop, calls=%fused_computation | loop fusion | flops 196608 | bytes 1572864 | tf_op jit(solution)/shard_map/stack | solution.py:479
  64.1 0.0 copy-start.5
  64.1 0.0 copy-start.6
  64.1 19.6 %collective-permute-start = (f32[2,384,256]{2,1,0:T(8,128)S(1)}, f32[2,384,256]{2,1,0:T(8,128)}, u32[]{:S(2)}, u32[]{:S(2)}) collective-permute-start(f32[2,384,256]{2,1,0:T(8,128)S(1)} %pad_maximum_fusion), channel_id=1, source_target_pairs={{0,32},{32,0},{64,96},{96,64},{128,160},{160,128},{192,224},{224,1... | collective-permute-start | bytes 2359304 | tf_op jit(solution)/shard_map/ppermute | solution.py:479
  83.7 0.3 minimum_bitcast_fusion
  84.0 0.0 copy-done.7
  84.0 1.1 %fusion.2 = f32[1,2,384,256]{3,2,1,0:T(8,128)} fusion(f32[1,1,384,256]{3,2,1,0:T(8,128)S(1)} %get-tuple-element.25, f32[1,1,384,256]{3,2,1,0:T(8,128)S(1)} %bitcast.60, f32[1,1,384,256]{3,2,1,0:T(8,128)S(1)} %get-tuple-element.23, f32[1,1,384,256]{3,2,1,0:T(8,128)S(1)} %get-tuple-element.28, f32[1,1,384,256]{3,2,1,0:T(8,128)S(1)} %get-tuple-element.19, ...), kind=kLoop, calls=%fused_computation.7 | loop fusion | flops 1572864 | bytes 3932161 | tf_op jit(solution)/shard_map/min | solution.py:493
  85.1 0.6 collective-permute-done
  85.7 0.0 copy-done.5
  85.7 0.0 copy-done.6
  85.8 1.3 %fusion.10 = (f32[384,256]{1,0:T(8,128)S(1)}, f32[384,256]{1,0:T(8,128)S(1)}, f32[1,384,256]{2,1,0:T(8,128)S(1)}, f32[1,384,256]{2,1,0:T(8,128)S(1)}) fusion(f32[384,256]{1,0:T(8,128)S(1)} %copy-done.5, f32[2,384,256]{2,1,0:T(8,128)} %collective-permute-done, pred[]{:T(512)S(6)} %eq.17, f32[2,384,256]{2,1,0:T(8,128)S(1)} %get-tuple-element.13, ...), kind=kLoop, calls=%fused_computation.22 | loop fusion | flops 786432 | bytes 3932161 | tf_op jit(solution)/shard_map/jit(_where)/select_n | solution.py:483
  87.0 1.1 %maximum_minimum_fusion = f32[2,384,256]{2,1,0:T(8,128)} fusion(f32[1,384,256]{2,1,0:T(8,128)S(1)} %get-tuple-element.29, f32[1,384,256]{2,1,0:T(8,128)S(1)} %get-tuple-element.30, f32[1,384,256]{2,1,0:T(8,128)S(1)} %get-tuple-element.24, f32[1,384,256]{2,1,0:T(8,128)S(1)} %get-tuple-element.27, f32[1,384,256]{2,1,0:T(8,128)S(1)} %get-tuple-element.26, ...), kind=kLoop, calls=%fused_computation.1 | loop fusion | flops 1376256 | bytes 3538944 | tf_op jit(solution)/shard_map/min | solution.py:499
  (1 shorter events, 0.0 us)
Async XLA Ops:
  1.5 1.1 %copy-start = (s32[2,384,256]{2,1,0:T(8,128)S(1)}, s32[2,384,256]{2,1,0:T(8,128)}, u32[]{:S(2)}) copy-start(s32[2,384,256]{2,1,0:T(8,128)} %tissue.1) | copy-start | bytes 2359300
  2.6 1.1 %copy-start.1 = (f32[2,384,256]{2,1,0:T(8,128)S(1)}, f32[2,384,256]{2,1,0:T(8,128)}, u32[]{:S(2)}) copy-start(f32[2,384,256]{2,1,0:T(8,128)} %previous.1) | copy-start | bytes 2359300
  3.7 0.7 copy-start.4
  21.9 0.9 %copy-start.2 = (f32[2,384,256]{2,1,0:T(8,128)}, f32[2,384,256]{2,1,0:T(8,128)S(1)}, u32[]{:S(2)}) copy-start(f32[2,384,256]{2,1,0:T(8,128)S(1)} %get-tuple-element.9.totals) | copy-start | bytes 2359300
  22.8 0.7 copy-start.3
  62.9 21.1 %copy-start.7 = (f32[384,256]{1,0:T(8,128)S(1)}, f32[384,256]{1,0:T(8,128)}, u32[]{:S(2)}) copy-start(f32[384,256]{1,0:T(8,128)} %get-tuple-element.14) | copy-start | bytes 1179652
  64.1 21.6 %copy-start.5 = (f32[384,256]{1,0:T(8,128)S(1)}, f32[384,256]{1,0:T(8,128)}, u32[]{:S(2)}) copy-start(f32[384,256]{1,0:T(8,128)} %get-tuple-element.12) | copy-start | bytes 1179652
  64.1 21.6 %copy-start.6 = (f32[384,256]{1,0:T(8,128)S(1)}, f32[384,256]{1,0:T(8,128)}, u32[]{:S(2)}) copy-start(f32[384,256]{1,0:T(8,128)} %get-tuple-element.11) | copy-start | bytes 1179652
  64.1 21.6 %collective-permute-start = (f32[2,384,256]{2,1,0:T(8,128)S(1)}, f32[2,384,256]{2,1,0:T(8,128)}, u32[]{:S(2)}, u32[]{:S(2)}) collective-permute-start(f32[2,384,256]{2,1,0:T(8,128)S(1)} %pad_maximum_fusion), channel_id=1, source_target_pairs={{0,32},{32,0},{64,96},{96,64},{128,160},{160,128},{192,224},{224,1... | collective-permute-start | bytes 2359304 | tf_op jit(solution)/shard_map/ppermute | solution.py:479

commit v20 on v14

--- a/solution.py
+++ b/solution.py
@@ -8,7 +8,7 @@
 from jax.sharding import PartitionSpec as P
 
 ROWS = 8
-CHUNK = 32
+CHUNK = 16
 
 
 def scan_step(a, m, k, axis, reverse, last):

time: 88.4 us -> 102 us (1.15)
  Pallas kernels: 56.8 us -> 70.2 us
    pallas_call x1, Pallas kernels: 17.5 us -> 30.8 us  [local_sweeps(): pl.pallas_call(functools.partial(local_kernel, grid_step=grid_step), out_...]
  transfers between devices with their start and end apart: 1 -> 1, of which waited for: 1 -> 1; matrix products, arithmetic and copies ran while one was open for 2% -> 1% of each run, Pallas kernels for 0% -> 0%
where the time goes in v20:
time: 102 us; the launch traced here: 101 us
  Pallas kernels  70.2 us (69%)
  starting transfers between devices  19.6 us (19%)
  other arithmetic  5.73 us (6%)
  local copies, waits for them, and re-layouts  4.55 us (4%)
    pallas_call x1, Pallas kernels, relay(): pl.pallas_call(functools.partial(relay_kernel, line=line), out_shape=(pla...  39.4 us
    pallas_call x1, Pallas kernels, local_sweeps(): pl.pallas_call(functools.partial(local_kernel, grid_step=grid_step), out_...  30.8 us
    ppermute x1, starting transfers between devices, shards(): lax.ppermute(jnp.stack([least_plane, least_in]), 'order', [(g, g ^ 1) for...  19.6 us
    unnamed x16, local copies, waits for them, and re-layouts  4.55 us
  transfers between devices with their start and end apart: 1, of which 1 were waited for; matrix products, arithmetic and copies ran while one was open for 1% of the time, Pallas kernels for 0%

profile of v20, /device:TPU:103, one launch (start us, length us, event | category | flops | bytes accessed | tf_op | source)
XLA Modules:
  0.0 101.4 jit_solution(13945121913131210799)
XLA Ops:
  0.7 0.7 subtract_bitcast_fusion
  1.4 0.1 pad_add_fusion.1.flags
  1.5 0.0 copy-start
  1.5 1.1 %copy-done = s32[2,384,256]{2,1,0:T(8,128)S(1)} copy-done((s32[2,384,256]{2,1,0:T(8,128)S(1)}, s32[2,384,256]{2,1,0:T(8,128)}, u32[]{:S(2)}) %copy-start) | copy-done | bytes 786456
  2.6 0.0 copy-start.1
  2.6 1.1 %copy-done.1 = f32[2,384,256]{2,1,0:T(8,128)S(1)} copy-done((f32[2,384,256]{2,1,0:T(8,128)S(1)}, f32[2,384,256]{2,1,0:T(8,128)}, u32[]{:S(2)}) %copy-start.1) | copy-done | bytes 786456
  3.7 0.0 copy-start.4
  3.7 0.7 copy-done.4
  4.4 30.8 %shard_map.68 = (f32[2,384,256]{2,1,0:T(8,128)S(1)}, f32[2,384,256]{2,1,0:T(8,128)S(1)}, f32[2,384,256]{2,1,0:T(8,128)S(1)}, f32[384,256]{1,0:T(8,128)S(1)}) custom-call(s32[3]{0:T(128)S(1)} %pad_add_fusion.1.flags, s32[3,16]{1,0:T(4,128)S(1)} %pad_add_fusion.stims, f32[16]{0:T(128)S(1)} %copy-done.4, f32[6,2,384,256]{3,2,1,0:T(8,128)} %fibre.1, ...), custom_call_target="tpu_custom_call" | custom-call | flops 58982400 | bytes 7864320 | tf_op jit(solution)/shard_map/pallas_call | solution.py:151
  35.2 0.0 copy-start.2
  35.2 0.9 copy-done.2
  36.1 0.0 copy-start.3
  36.1 0.7 copy-done.3
  36.8 39.4 %shard_map.69 = (f32[384,256]{1,0:T(8,128)}, f32[384,256]{1,0:T(8,128)}, f32[384,256]{1,0:T(8,128)}) custom-call(f32[2,384,256]{2,1,0:T(8,128)} %copy-done.2, f32[384,256]{1,0:T(8,128)} %copy-done.3), custom_call_target="tpu_custom_call" | custom-call | tf_op jit(solution)/shard_map/pallas_call | solution.py:430
  76.2 0.0 copy-start.7
  76.2 1.2 %pad_maximum_fusion = f32[2,384,256]{2,1,0:T(8,128)S(1)} fusion(f32[1,384,256]{2,1,0:T(8,128)} %bitcast.61, f32[1,384,256]{2,1,0:T(8,128)} %bitcast.62), kind=kLoop, calls=%fused_computation | loop fusion | flops 196608 | bytes 1572864 | tf_op jit(solution)/shard_map/stack | solution.py:479
  77.4 0.0 copy-start.5
  77.5 0.0 copy-start.6
  77.5 19.6 %collective-permute-start = (f32[2,384,256]{2,1,0:T(8,128)S(1)}, f32[2,384,256]{2,1,0:T(8,128)}, u32[]{:S(2)}, u32[]{:S(2)}) collective-permute-start(f32[2,384,256]{2,1,0:T(8,128)S(1)} %pad_maximum_fusion), channel_id=1, source_target_pairs={{0,32},{32,0},{64,96},{96,64},{128,160},{160,128},{192,224},{224,1... | collective-permute-start | bytes 2359304 | tf_op jit(solution)/shard_map/ppermute | solution.py:479
  97.0 0.3 minimum_bitcast_fusion
  97.3 0.0 copy-done.7
  97.3 1.1 %fusion.2 = f32[1,2,384,256]{3,2,1,0:T(8,128)} fusion(f32[1,1,384,256]{3,2,1,0:T(8,128)S(1)} %get-tuple-element.25, f32[1,1,384,256]{3,2,1,0:T(8,128)S(1)} %bitcast.60, f32[1,1,384,256]{3,2,1,0:T(8,128)S(1)} %get-tuple-element.23, f32[1,1,384,256]{3,2,1,0:T(8,128)S(1)} %get-tuple-element.28, f32[1,1,384,256]{3,2,1,0:T(8,128)S(1)} %get-tuple-element.19, ...), kind=kLoop, calls=%fused_computation.7 | loop fusion | flops 1572864 | bytes 3932161 | tf_op jit(solution)/shard_map/min | solution.py:493
  98.5 0.6 collective-permute-done
  99.1 0.0 copy-done.5
  99.1 0.0 copy-done.6
  99.1 1.3 %fusion.10 = (f32[384,256]{1,0:T(8,128)S(1)}, f32[384,256]{1,0:T(8,128)S(1)}, f32[1,384,256]{2,1,0:T(8,128)S(1)}, f32[1,384,256]{2,1,0:T(8,128)S(1)}) fusion(f32[384,256]{1,0:T(8,128)S(1)} %copy-done.5, f32[2,384,256]{2,1,0:T(8,128)} %collective-permute-done, pred[]{:T(512)S(6)} %eq.17, f32[2,384,256]{2,1,0:T(8,128)S(1)} %get-tuple-element.13, ...), kind=kLoop, calls=%fused_computation.22 | loop fusion | flops 786432 | bytes 3932161 | tf_op jit(solution)/shard_map/jit(_where)/select_n | solution.py:483
  100.3 1.1 %maximum_minimum_fusion = f32[2,384,256]{2,1,0:T(8,128)} fusion(f32[1,384,256]{2,1,0:T(8,128)S(1)} %get-tuple-element.29, f32[1,384,256]{2,1,0:T(8,128)S(1)} %get-tuple-element.30, f32[1,384,256]{2,1,0:T(8,128)S(1)} %get-tuple-element.24, f32[1,384,256]{2,1,0:T(8,128)S(1)} %get-tuple-element.27, f32[1,384,256]{2,1,0:T(8,128)S(1)} %get-tuple-element.26, ...), kind=kLoop, calls=%fused_computation.1 | loop fusion | flops 1376256 | bytes 3538944 | tf_op jit(solution)/shard_map/min | solution.py:499
  (1 shorter events, 0.0 us)
Async XLA Ops:
  1.5 1.1 %copy-start = (s32[2,384,256]{2,1,0:T(8,128)S(1)}, s32[2,384,256]{2,1,0:T(8,128)}, u32[]{:S(2)}) copy-start(s32[2,384,256]{2,1,0:T(8,128)} %tissue.1) | copy-start | bytes 2359300
  2.6 1.1 %copy-start.1 = (f32[2,384,256]{2,1,0:T(8,128)S(1)}, f32[2,384,256]{2,1,0:T(8,128)}, u32[]{:S(2)}) copy-start(f32[2,384,256]{2,1,0:T(8,128)} %previous.1) | copy-start | bytes 2359300
  3.7 0.7 copy-start.4
  35.2 0.9 copy-start.2
  36.1 0.7 copy-start.3
  76.2 21.1 %copy-start.7 = (f32[384,256]{1,0:T(8,128)S(1)}, f32[384,256]{1,0:T(8,128)}, u32[]{:S(2)}) copy-start(f32[384,256]{1,0:T(8,128)} %get-tuple-element.14) | copy-start | bytes 1179652
  77.4 21.6 %copy-start.5 = (f32[384,256]{1,0:T(8,128)S(1)}, f32[384,256]{1,0:T(8,128)}, u32[]{:S(2)}) copy-start(f32[384,256]{1,0:T(8,128)} %get-tuple-element.12) | copy-start | bytes 1179652
  77.5 21.6 %copy-start.6 = (f32[384,256]{1,0:T(8,128)S(1)}, f32[384,256]{1,0:T(8,128)}, u32[]{:S(2)}) copy-start(f32[384,256]{1,0:T(8,128)} %get-tuple-element.11) | copy-start | bytes 1179652
  77.5 21.6 %collective-permute-start = (f32[2,384,256]{2,1,0:T(8,128)S(1)}, f32[2,384,256]{2,1,0:T(8,128)}, u32[]{:S(2)}, u32[]{:S(2)}) collective-permute-start(f32[2,384,256]{2,1,0:T(8,128)S(1)} %pad_maximum_fusion), channel_id=1, source_target_pairs={{0,32},{32,0},{64,96},{96,64},{128,160},{160,128},{192,224},{224,1... | collective-permute-start | bytes 2359304 | tf_op jit(solution)/shard_map/ppermute | solution.py:479

commit v21 on v20

--- a/solution.py
+++ b/solution.py
@@ -8,7 +8,7 @@
 from jax.sharding import PartitionSpec as P
 
 ROWS = 8
-CHUNK = 16
+CHUNK = 64
 
 
 def scan_step(a, m, k, axis, reverse, last):

time: 102 us -> 82 us (0.80)
  Pallas kernels: 70.2 us -> 50.4 us
    pallas_call x1, Pallas kernels: 30.8 us -> 11.1 us  [local_sweeps(): pl.pallas_call(functools.partial(local_kernel, grid_step=grid_step), out_...]
  transfers between devices with their start and end apart: 1 -> 1, of which waited for: 1 -> 1; matrix products, arithmetic and copies ran while one was open for 1% -> 2% of each run, Pallas kernels for 0% -> 0%
where the time goes in v21:
time: 82 us; the launch traced here: 81.7 us
  Pallas kernels  50.4 us (61%)
  starting transfers between devices  19.6 us (24%)
  other arithmetic  5.73 us (7%)
  local copies, waits for them, and re-layouts  4.55 us (6%)
    pallas_call x1, Pallas kernels, relay(): pl.pallas_call(functools.partial(relay_kernel, line=line), out_shape=(pla...  39.3 us
    ppermute x1, starting transfers between devices, shards(): lax.ppermute(jnp.stack([least_plane, least_in]), 'order', [(g, g ^ 1) for...  19.6 us
    pallas_call x1, Pallas kernels, local_sweeps(): pl.pallas_call(functools.partial(local_kernel, grid_step=grid_step), out_...  11.1 us
    unnamed x16, local copies, waits for them, and re-layouts  4.55 us
  transfers between devices with their start and end apart: 1, of which 1 were waited for; matrix products, arithmetic and copies ran while one was open for 2% of the time, Pallas kernels for 0%

profile of v21, /device:TPU:103, one launch (start us, length us, event | category | flops | bytes accessed | tf_op | source)
XLA Modules:
  0.0 81.7 jit_solution(6848265606801638039)
XLA Ops:
  0.7 0.7 subtract_bitcast_fusion
  1.4 0.1 pad_add_fusion.1.flags
  1.5 0.0 copy-start
  1.5 1.1 %copy-done = s32[2,384,256]{2,1,0:T(8,128)S(1)} copy-done((s32[2,384,256]{2,1,0:T(8,128)S(1)}, s32[2,384,256]{2,1,0:T(8,128)}, u32[]{:S(2)}) %copy-start) | copy-done | bytes 786456
  2.6 0.0 copy-start.1
  2.6 1.1 %copy-done.1 = f32[2,384,256]{2,1,0:T(8,128)S(1)} copy-done((f32[2,384,256]{2,1,0:T(8,128)S(1)}, f32[2,384,256]{2,1,0:T(8,128)}, u32[]{:S(2)}) %copy-start.1) | copy-done | bytes 786456
  3.7 0.0 copy-start.4
  3.7 0.7 copy-done.4
  4.4 11.1 %shard_map.68 = (f32[2,384,256]{2,1,0:T(8,128)S(1)}, f32[2,384,256]{2,1,0:T(8,128)S(1)}, f32[2,384,256]{2,1,0:T(8,128)S(1)}, f32[384,256]{1,0:T(8,128)S(1)}) custom-call(s32[3]{0:T(128)S(1)} %pad_add_fusion.1.flags, s32[3,16]{1,0:T(4,128)S(1)} %pad_add_fusion.stims, f32[16]{0:T(128)S(1)} %copy-done.4, f32[6,2,384,256]{3,2,1,0:T(8,128)} %fibre.1, ...), custom_call_target="tpu_custom_call" | custom-call | flops 58982400 | bytes 7864320 | tf_op jit(solution)/shard_map/pallas_call | solution.py:151
  15.5 0.0 copy-start.2
  15.5 0.9 %copy-done.2 = f32[2,384,256]{2,1,0:T(8,128)} copy-done((f32[2,384,256]{2,1,0:T(8,128)}, f32[2,384,256]{2,1,0:T(8,128)S(1)}, u32[]{:S(2)}) %copy-start.2) | copy-done | bytes 786456
  16.4 0.0 copy-start.3
  16.4 0.7 copy-done.3
  17.1 39.3 %shard_map.69 = (f32[384,256]{1,0:T(8,128)}, f32[384,256]{1,0:T(8,128)}, f32[384,256]{1,0:T(8,128)}) custom-call(f32[2,384,256]{2,1,0:T(8,128)} %copy-done.2, f32[384,256]{1,0:T(8,128)} %copy-done.3), custom_call_target="tpu_custom_call" | custom-call | tf_op jit(solution)/shard_map/pallas_call | solution.py:430
  56.5 0.0 copy-start.7
  56.5 1.2 %pad_maximum_fusion = f32[2,384,256]{2,1,0:T(8,128)S(1)} fusion(f32[1,384,256]{2,1,0:T(8,128)} %bitcast.61, f32[1,384,256]{2,1,0:T(8,128)} %bitcast.62), kind=kLoop, calls=%fused_computation | loop fusion | flops 196608 | bytes 1572864 | tf_op jit(solution)/shard_map/stack | solution.py:479
  57.7 0.0 copy-start.5
  57.7 0.0 copy-start.6
  57.7 19.6 %collective-permute-start = (f32[2,384,256]{2,1,0:T(8,128)S(1)}, f32[2,384,256]{2,1,0:T(8,128)}, u32[]{:S(2)}, u32[]{:S(2)}) collective-permute-start(f32[2,384,256]{2,1,0:T(8,128)S(1)} %pad_maximum_fusion), channel_id=1, source_target_pairs={{0,32},{32,0},{64,96},{96,64},{128,160},{160,128},{192,224},{224,1... | collective-permute-start | bytes 2359304 | tf_op jit(solution)/shard_map/ppermute | solution.py:479
  77.3 0.3 minimum_bitcast_fusion
  77.6 0.0 copy-done.7
  77.6 1.1 %fusion.2 = f32[1,2,384,256]{3,2,1,0:T(8,128)} fusion(f32[1,1,384,256]{3,2,1,0:T(8,128)S(1)} %get-tuple-element.25, f32[1,1,384,256]{3,2,1,0:T(8,128)S(1)} %bitcast.60, f32[1,1,384,256]{3,2,1,0:T(8,128)S(1)} %get-tuple-element.23, f32[1,1,384,256]{3,2,1,0:T(8,128)S(1)} %get-tuple-element.28, f32[1,1,384,256]{3,2,1,0:T(8,128)S(1)} %get-tuple-element.19, ...), kind=kLoop, calls=%fused_computation.7 | loop fusion | flops 1572864 | bytes 3932161 | tf_op jit(solution)/shard_map/min | solution.py:493
  78.7 0.6 collective-permute-done
  79.4 0.0 copy-done.5
  79.4 0.0 copy-done.6
  79.4 1.3 %fusion.10 = (f32[384,256]{1,0:T(8,128)S(1)}, f32[384,256]{1,0:T(8,128)S(1)}, f32[1,384,256]{2,1,0:T(8,128)S(1)}, f32[1,384,256]{2,1,0:T(8,128)S(1)}) fusion(f32[384,256]{1,0:T(8,128)S(1)} %copy-done.5, f32[2,384,256]{2,1,0:T(8,128)} %collective-permute-done, pred[]{:T(512)S(6)} %eq.17, f32[2,384,256]{2,1,0:T(8,128)S(1)} %get-tuple-element.13, ...), kind=kLoop, calls=%fused_computation.22 | loop fusion | flops 786432 | bytes 3932161 | tf_op jit(solution)/shard_map/jit(_where)/select_n | solution.py:483
  80.6 1.1 %maximum_minimum_fusion = f32[2,384,256]{2,1,0:T(8,128)} fusion(f32[1,384,256]{2,1,0:T(8,128)S(1)} %get-tuple-element.29, f32[1,384,256]{2,1,0:T(8,128)S(1)} %get-tuple-element.30, f32[1,384,256]{2,1,0:T(8,128)S(1)} %get-tuple-element.24, f32[1,384,256]{2,1,0:T(8,128)S(1)} %get-tuple-element.27, f32[1,384,256]{2,1,0:T(8,128)S(1)} %get-tuple-element.26, ...), kind=kLoop, calls=%fused_computation.1 | loop fusion | flops 1376256 | bytes 3538944 | tf_op jit(solution)/shard_map/min | solution.py:499
  (1 shorter events, 0.0 us)
Async XLA Ops:
  1.5 1.1 %copy-start = (s32[2,384,256]{2,1,0:T(8,128)S(1)}, s32[2,384,256]{2,1,0:T(8,128)}, u32[]{:S(2)}) copy-start(s32[2,384,256]{2,1,0:T(8,128)} %tissue.1) | copy-start | bytes 2359300
  2.6 1.1 %copy-start.1 = (f32[2,384,256]{2,1,0:T(8,128)S(1)}, f32[2,384,256]{2,1,0:T(8,128)}, u32[]{:S(2)}) copy-start(f32[2,384,256]{2,1,0:T(8,128)} %previous.1) | copy-start | bytes 2359300
  3.7 0.7 copy-start.4
  15.5 0.9 %copy-start.2 = (f32[2,384,256]{2,1,0:T(8,128)}, f32[2,384,256]{2,1,0:T(8,128)S(1)}, u32[]{:S(2)}) copy-start(f32[2,384,256]{2,1,0:T(8,128)S(1)} %get-tuple-element.9.totals) | copy-start | bytes 2359300
  16.4 0.7 copy-start.3
  56.5 21.2 %copy-start.7 = (f32[384,256]{1,0:T(8,128)S(1)}, f32[384,256]{1,0:T(8,128)}, u32[]{:S(2)}) copy-start(f32[384,256]{1,0:T(8,128)} %get-tuple-element.14) | copy-start | bytes 1179652
  57.7 21.7 %copy-start.5 = (f32[384,256]{1,0:T(8,128)S(1)}, f32[384,256]{1,0:T(8,128)}, u32[]{:S(2)}) copy-start(f32[384,256]{1,0:T(8,128)} %get-tuple-element.12) | copy-start | bytes 1179652
  57.7 21.7 %copy-start.6 = (f32[384,256]{1,0:T(8,128)S(1)}, f32[384,256]{1,0:T(8,128)}, u32[]{:S(2)}) copy-start(f32[384,256]{1,0:T(8,128)} %get-tuple-element.11) | copy-start | bytes 1179652
  57.7 21.6 %collective-permute-start = (f32[2,384,256]{2,1,0:T(8,128)S(1)}, f32[2,384,256]{2,1,0:T(8,128)}, u32[]{:S(2)}, u32[]{:S(2)}) collective-permute-start(f32[2,384,256]{2,1,0:T(8,128)S(1)} %pad_maximum_fusion), channel_id=1, source_target_pairs={{0,32},{32,0},{64,96},{96,64},{128,160},{160,128},{192,224},{224,1... | collective-permute-start | bytes 2359304 | tf_op jit(solution)/shard_map/ppermute | solution.py:479

commit v22 on v21

--- a/solution.py
+++ b/solution.py
@@ -8,7 +8,7 @@
 from jax.sharding import PartitionSpec as P
 
 ROWS = 8
-CHUNK = 64
+CHUNK = 128
 
 
 def scan_step(a, m, k, axis, reverse, last):

time: 82 us -> 80 us (0.976)
  Pallas kernels: 50.4 us -> 48.4 us
    pallas_call x1, Pallas kernels: 11.1 us -> 9.22 us  [local_sweeps(): pl.pallas_call(functools.partial(local_kernel, grid_step=grid_step), out_...]
where the time goes in v22:
time: 80 us; the launch traced here: 79.7 us
  Pallas kernels  48.4 us (60%)
  starting transfers between devices  19.6 us (25%)
  other arithmetic  5.73 us (7%)
  local copies, waits for them, and re-layouts  4.55 us (6%)
    pallas_call x1, Pallas kernels, relay(): pl.pallas_call(functools.partial(relay_kernel, line=line), out_shape=(pla...  39.2 us
    ppermute x1, starting transfers between devices, shards(): lax.ppermute(jnp.stack([least_plane, least_in]), 'order', [(g, g ^ 1) for...  19.6 us
    pallas_call x1, Pallas kernels, local_sweeps(): pl.pallas_call(functools.partial(local_kernel, grid_step=grid_step), out_...  9.22 us
    unnamed x16, local copies, waits for them, and re-layouts  4.55 us
  transfers between devices with their start and end apart: 1, of which 1 were waited for; matrix products, arithmetic and copies ran while one was open for 2% of the time, Pallas kernels for 0%

profile of v22, /device:TPU:103, one launch (start us, length us, event | category | flops | bytes accessed | tf_op | source)
XLA Modules:
  0.0 79.7 jit_solution(15838618871076980392)
XLA Ops:
  0.7 0.7 subtract_bitcast_fusion
  1.4 0.1 pad_add_fusion.1.flags
  1.5 0.0 copy-start
  1.5 1.1 %copy-done = s32[2,384,256]{2,1,0:T(8,128)S(1)} copy-done((s32[2,384,256]{2,1,0:T(8,128)S(1)}, s32[2,384,256]{2,1,0:T(8,128)}, u32[]{:S(2)}) %copy-start) | copy-done | bytes 786456
  2.6 0.0 copy-start.1
  2.6 1.1 %copy-done.1 = f32[2,384,256]{2,1,0:T(8,128)S(1)} copy-done((f32[2,384,256]{2,1,0:T(8,128)S(1)}, f32[2,384,256]{2,1,0:T(8,128)}, u32[]{:S(2)}) %copy-start.1) | copy-done | bytes 786456
  3.7 0.0 copy-start.4
  3.7 0.7 copy-done.4
  4.4 9.2 %shard_map.68 = (f32[2,384,256]{2,1,0:T(8,128)S(1)}, f32[2,384,256]{2,1,0:T(8,128)S(1)}, f32[2,384,256]{2,1,0:T(8,128)S(1)}, f32[384,256]{1,0:T(8,128)S(1)}) custom-call(s32[3]{0:T(128)S(1)} %pad_add_fusion.1.flags, s32[3,16]{1,0:T(4,128)S(1)} %pad_add_fusion.stims, f32[16]{0:T(128)S(1)} %copy-done.4, f32[6,2,384,256]{3,2,1,0:T(8,128)} %fibre.1, ...), custom_call_target="tpu_custom_call" | custom-call | flops 58982400 | bytes 7864320 | tf_op jit(solution)/shard_map/pallas_call | solution.py:151
  13.6 0.0 copy-start.2
  13.6 0.9 %copy-done.2 = f32[2,384,256]{2,1,0:T(8,128)} copy-done((f32[2,384,256]{2,1,0:T(8,128)}, f32[2,384,256]{2,1,0:T(8,128)S(1)}, u32[]{:S(2)}) %copy-start.2) | copy-done | bytes 786456
  14.5 0.0 copy-start.3
  14.5 0.7 copy-done.3
  15.2 39.2 %shard_map.69 = (f32[384,256]{1,0:T(8,128)}, f32[384,256]{1,0:T(8,128)}, f32[384,256]{1,0:T(8,128)}) custom-call(f32[2,384,256]{2,1,0:T(8,128)} %copy-done.2, f32[384,256]{1,0:T(8,128)} %copy-done.3), custom_call_target="tpu_custom_call" | custom-call | tf_op jit(solution)/shard_map/pallas_call | solution.py:430
  54.4 0.0 copy-start.7
  54.5 1.2 %pad_maximum_fusion = f32[2,384,256]{2,1,0:T(8,128)S(1)} fusion(f32[1,384,256]{2,1,0:T(8,128)} %bitcast.61, f32[1,384,256]{2,1,0:T(8,128)} %bitcast.62), kind=kLoop, calls=%fused_computation | loop fusion | flops 196608 | bytes 1572864 | tf_op jit(solution)/shard_map/stack | solution.py:479
  55.7 0.0 copy-start.5
  55.7 0.0 copy-start.6
  55.7 19.6 %collective-permute-start = (f32[2,384,256]{2,1,0:T(8,128)S(1)}, f32[2,384,256]{2,1,0:T(8,128)}, u32[]{:S(2)}, u32[]{:S(2)}) collective-permute-start(f32[2,384,256]{2,1,0:T(8,128)S(1)} %pad_maximum_fusion), channel_id=1, source_target_pairs={{0,32},{32,0},{64,96},{96,64},{128,160},{160,128},{192,224},{224,1... | collective-permute-start | bytes 2359304 | tf_op jit(solution)/shard_map/ppermute | solution.py:479
  75.3 0.3 minimum_bitcast_fusion
  75.6 0.0 copy-done.7
  75.6 1.1 %fusion.2 = f32[1,2,384,256]{3,2,1,0:T(8,128)} fusion(f32[1,1,384,256]{3,2,1,0:T(8,128)S(1)} %get-tuple-element.25, f32[1,1,384,256]{3,2,1,0:T(8,128)S(1)} %bitcast.60, f32[1,1,384,256]{3,2,1,0:T(8,128)S(1)} %get-tuple-element.23, f32[1,1,384,256]{3,2,1,0:T(8,128)S(1)} %get-tuple-element.28, f32[1,1,384,256]{3,2,1,0:T(8,128)S(1)} %get-tuple-element.19, ...), kind=kLoop, calls=%fused_computation.7 | loop fusion | flops 1572864 | bytes 3932161 | tf_op jit(solution)/shard_map/min | solution.py:493
  76.7 0.6 collective-permute-done
  77.4 0.0 copy-done.5
  77.4 0.0 copy-done.6
  77.4 1.3 %fusion.10 = (f32[384,256]{1,0:T(8,128)S(1)}, f32[384,256]{1,0:T(8,128)S(1)}, f32[1,384,256]{2,1,0:T(8,128)S(1)}, f32[1,384,256]{2,1,0:T(8,128)S(1)}) fusion(f32[384,256]{1,0:T(8,128)S(1)} %copy-done.5, f32[2,384,256]{2,1,0:T(8,128)} %collective-permute-done, pred[]{:T(512)S(6)} %eq.17, f32[2,384,256]{2,1,0:T(8,128)S(1)} %get-tuple-element.13, ...), kind=kLoop, calls=%fused_computation.22 | loop fusion | flops 786432 | bytes 3932161 | tf_op jit(solution)/shard_map/jit(_where)/select_n | solution.py:483
  78.6 1.1 %maximum_minimum_fusion = f32[2,384,256]{2,1,0:T(8,128)} fusion(f32[1,384,256]{2,1,0:T(8,128)S(1)} %get-tuple-element.29, f32[1,384,256]{2,1,0:T(8,128)S(1)} %get-tuple-element.30, f32[1,384,256]{2,1,0:T(8,128)S(1)} %get-tuple-element.24, f32[1,384,256]{2,1,0:T(8,128)S(1)} %get-tuple-element.27, f32[1,384,256]{2,1,0:T(8,128)S(1)} %get-tuple-element.26, ...), kind=kLoop, calls=%fused_computation.1 | loop fusion | flops 1376256 | bytes 3538944 | tf_op jit(solution)/shard_map/min | solution.py:499
  (1 shorter events, 0.0 us)
Async XLA Ops:
  1.5 1.1 %copy-start = (s32[2,384,256]{2,1,0:T(8,128)S(1)}, s32[2,384,256]{2,1,0:T(8,128)}, u32[]{:S(2)}) copy-start(s32[2,384,256]{2,1,0:T(8,128)} %tissue.1) | copy-start | bytes 2359300
  2.6 1.1 %copy-start.1 = (f32[2,384,256]{2,1,0:T(8,128)S(1)}, f32[2,384,256]{2,1,0:T(8,128)}, u32[]{:S(2)}) copy-start(f32[2,384,256]{2,1,0:T(8,128)} %previous.1) | copy-start | bytes 2359300
  3.7 0.7 copy-start.4
  13.6 0.9 %copy-start.2 = (f32[2,384,256]{2,1,0:T(8,128)}, f32[2,384,256]{2,1,0:T(8,128)S(1)}, u32[]{:S(2)}) copy-start(f32[2,384,256]{2,1,0:T(8,128)S(1)} %get-tuple-element.9.totals) | copy-start | bytes 2359300
  14.5 0.7 copy-start.3
  54.4 21.2 %copy-start.7 = (f32[384,256]{1,0:T(8,128)S(1)}, f32[384,256]{1,0:T(8,128)}, u32[]{:S(2)}) copy-start(f32[384,256]{1,0:T(8,128)} %get-tuple-element.14) | copy-start | bytes 1179652
  55.7 21.7 %copy-start.5 = (f32[384,256]{1,0:T(8,128)S(1)}, f32[384,256]{1,0:T(8,128)}, u32[]{:S(2)}) copy-start(f32[384,256]{1,0:T(8,128)} %get-tuple-element.12) | copy-start | bytes 1179652
  55.7 21.7 %copy-start.6 = (f32[384,256]{1,0:T(8,128)S(1)}, f32[384,256]{1,0:T(8,128)}, u32[]{:S(2)}) copy-start(f32[384,256]{1,0:T(8,128)} %get-tuple-element.11) | copy-start | bytes 1179652
  55.7 21.7 %collective-permute-start = (f32[2,384,256]{2,1,0:T(8,128)S(1)}, f32[2,384,256]{2,1,0:T(8,128)}, u32[]{:S(2)}, u32[]{:S(2)}) collective-permute-start(f32[2,384,256]{2,1,0:T(8,128)S(1)} %pad_maximum_fusion), channel_id=1, source_target_pairs={{0,32},{32,0},{64,96},{96,64},{128,160},{160,128},{192,224},{224,1... | collective-permute-start | bytes 2359304 | tf_op jit(solution)/shard_map/ppermute | solution.py:479
